TPU v7x, 256 devices: a whole 4x4x8 slice. The times are simulated.
256 devices in a mesh: stripe: 32 (over z, x_lo, core), tile: 8 (over y, x_hi).
Axes of the slice: x: 4 (x_hi: 2, x_lo: 2; x = x_hi * 2 + x_lo), y: 4, z: 8, core: 2. Of those that a mesh axis runs over, the one named last changes fastest.
Arguments:
- positions: int32 [32, 24], P('stripe', 'tile'), may hold values from -64 to -64, as said below
- row_offsets: int32 [32, 24], P('stripe', 'tile'), may hold values from -64 to 64, as said below
- amplitudes: float32 [32, 24, 256, 256], P('stripe', 'tile'), may hold values from 0 to 2
- object_field: float32 [2, 8192, 1024], P(None, 'stripe', 'tile'), may hold values from -6 to 6
- probe_field: float32 [2, 256, 256], replicated, may hold values from -6 to 6
Outputs:
- object_out: float32 [2, 8192, 1024], P(None, 'stripe', 'tile')
- probe_out: float32 [2, 256, 256], replicated
Inputs may be any that keep to these rules, and one draw needn't show every extreme that they name: `positions`: in every block of 3 patterns of one stripe and one tile, the first offset is -64 and the second is 128 - 192. `row_offsets`: in every block of 3 patterns of one stripe and one tile, the first row offset is -64 and the second is 64.
All inputs are finite; a program needn't handle non-finite values.
Results may differ from a plain program's by a relative error of at most 0.0006.
The roundings to bfloat16 on the way count: a program that leaves them out, or rounds other values in their place, can miss the bound.
Values sent between devices are 32-bit elements; how exact they have to be, the bound alone decides.
No kernel may reach another device: no remote copies, remote signals or barrier semaphores. Data moves between devices by JAX's collectives and lax.ppermute only.
A program may use at most 64 MiB of HBM per device.

v0:
```python
import functools
import math

import jax
import jax.numpy as jnp
import numpy as np
from jax import lax
from jax.experimental import pallas as pl
from jax.experimental.pallas import tpu as pltpu
from jax.sharding import PartitionSpec as P

PW = 256
HALO = 64
TILE_W = 128
PAT_DEV = 3
OUTER = 2
STRIPES = 32
TILES = 8
EXT = PW + 2 * HALO
LANES = 128
AXES = ("stripe", "tile")
F32 = jnp.float32
BF16 = jnp.bfloat16


def place(x, y, z, core):
    return (z * 4 + (x % 2) * 2 + core) * TILES + y * 2 + x // 2


def physical(flat):
    s, t = flat // TILES, flat % TILES
    return (t % 2) * 2 + (s // 2) % 2, t // 2, s // 4, s % 2


def moved(step):
    pairs = []
    for flat in range(STRIPES * TILES):
        pairs.append((flat, place(*step(*physical(flat)))))
    return pairs


def core_swap():
    return moved(lambda x, y, z, c: (x, y, z, 1 - c))


def along_x(k):
    return moved(lambda x, y, z, c: (x ^ k, y, z, c))


def along_y(k):
    return moved(lambda x, y, z, c: (x, y ^ k, z, c))


def along_z(k):
    return moved(lambda x, y, z, c: (x, y, (z + k) % 8, c))


def next_z():
    return moved(lambda x, y, z, c: (x, y, z ^ 1, c))


def far_z():
    return moved(lambda x, y, z, c: (x, y, (z + (3 if z % 2 else 5)) % 8, c))


def host(s, t):
    return place(s % 4, t // 2, s // 4, t % 2)


def to_host():
    return [(s * TILES + t, host(s, t)) for s in range(STRIPES) for t in range(TILES)]


def from_host():
    return [(there, here) for here, there in to_host()]


def neighbour(ds, dt):
    pairs = []
    for s in range(STRIPES):
        for t in range(TILES):
            pairs.append((host(s, t), host((s + ds) % STRIPES, (t + dt) % TILES)))
    return pairs


def send(value, pairs):
    return lax.ppermute(value, AXES, pairs)


def dft_tables():
    indices = np.arange(PW, dtype=np.int32)
    phase = indices[:, None] * indices[None, :] % PW
    angles = phase.astype(np.float32) * np.float32(2.0 * math.pi / PW)
    factor = np.float32(1.0 / math.sqrt(PW))
    cosine, sine = np.cos(angles) * factor, np.sin(angles) * factor
    forward = np.block([[cosine, sine], [-sine, cosine]]).astype(BF16)
    inverse = np.block([[cosine, -sine], [sine, cosine]]).astype(BF16)
    return jnp.asarray(forward), jnp.asarray(inverse)


def vmem_call(kernel, out_shapes, scratch, *args, held=True, grant=8 << 20):
    smem = pl.BlockSpec(memory_space=pltpu.SMEM)
    vmem = pl.BlockSpec(memory_space=pltpu.VMEM)
    keep = pltpu.with_memory_space_constraint
    args = [a if a.dtype == jnp.int32 else keep(a, pltpu.VMEM) for a in args]
    return pl.pallas_call(
        kernel,
        in_specs=[smem if a.dtype == jnp.int32 else vmem for a in args],
        out_specs=[vmem for _ in out_shapes],
        out_shape=[pltpu.VMEM(s, F32) if held else jax.ShapeDtypeStruct(s, F32) for s in out_shapes],
        scratch_shapes=scratch,
        compiler_params=pltpu.CompilerParams(vmem_limit_bytes=grant),
    )(*args)


def unless(end, value):
    return jnp.where(end, jnp.zeros_like(value), value)


def step_of(probe_ref):
    power = probe_ref[0] * probe_ref[0] + probe_ref[1] * probe_ref[1]
    return 1.0 / (2.0 * PAT_DEV * jnp.max(power) + 1e-06)


def updated(place_ref, probe_ref, obj_ref, parts, store):
    gl, gr, rl, rr, rt, rb = parts
    step = step_of(probe_ref)
    s, t = place_ref[1], place_ref[2]
    row_lo = jnp.where(s == 0, HALO, 0)
    row_hi = jnp.where(s == STRIPES - 1, HALO + PW, EXT)
    col_lo = jnp.where(t == 0, HALO, 0)
    col_hi = jnp.where(t == TILES - 1, HALO + TILE_W, PW)
    for side, own, other, end in ((0, gl, rl, t == 0), (1, gr, rr, t == TILES - 1)):
        cols = slice(side * LANES, (side + 1) * LANES)
        row = lax.broadcasted_iota(jnp.int32, (LANES, LANES), 0)
        col = lax.broadcasted_iota(jnp.int32, (LANES, LANES), 1) + side * LANES
        col_ok = (col >= col_lo) & (col < col_hi)
        for block in range(3):
            span = slice(block * LANES, (block + 1) * LANES)
            at = row + block * LANES
            ok = col_ok & (at >= row_lo) & (at < row_hi)
            factor = jnp.where(ok, step, 0.0)
            for ch in range(2):
                g = own[ch, span, :] + unless(end, other[ch, span, :])
                if block == 0:
                    g = g + unless(s == 0, rt[ch, :, cols])
                if block == 2:
                    g = g + unless(s == STRIPES - 1, rb[ch, :, cols])
                store(ch, block, side, obj_ref[ch, span, cols] - factor * g)


def new_probe(place_ref, probe_ref, near_ref, far_ref, total_ref, out_ref):
    c, x, y = place_ref[3], place_ref[4], place_ref[5]
    for k in range(4):
        for j in range(4):
            block = (x ^ k) * 4 + (y ^ j)
            for half, ref in ((c, near_ref), (1 - c, far_ref)):
                row = pl.multiple_of((half * 16 + block) * 8, 8)
                for ch in range(3):
                    total_ref[ch, pl.ds(row, 8), :] = ref[k * 4 + j, ch * 8 : ch * 8 + 8, :]
    scale = 0.5 / (total_ref[2] + 1.0)
    for ch in range(2):
        out_ref[ch] = probe_ref[ch] - total_ref[ch] * scale


def lifted(value, shift):
    tiles = value.reshape(PW // 8 + 1, 8, value.shape[1])
    tiles = pltpu.roll(tiles, (8 - shift) % 8, axis=1)
    row = lax.broadcasted_iota(jnp.int32, (PW // 8, 8, value.shape[1]), 1)
    return jnp.where(row < 8 - shift, tiles[:-1], tiles[1:]).reshape(PW, value.shape[1])


def lowered(value, shift):
    tiles = value.reshape(PW // 8, 8, value.shape[1])
    tiles = pltpu.roll(tiles, shift % 8, axis=1)
    none = jnp.zeros((1, 8, value.shape[1]), F32)
    row = lax.broadcasted_iota(jnp.int32, (PW // 8 + 1, 8, value.shape[1]), 1)
    below = jnp.concatenate([tiles, none], axis=0)
    above = jnp.concatenate([none, tiles], axis=0)
    return jnp.where(row >= shift, below, above).reshape(PW + 8, value.shape[1])


def patterns(place_ref, obj_ref, probe_ref, amp_ref, fwd_ref, inv_ref, gl_ref, gr_ref, pg_ref):
    fwd, inv = fwd_ref[...], inv_ref[...]
    third, shift = pl.multiple_of(place_ref[0], 8), place_ref[6]
    for p in range(PAT_DEV):
        if p < 2:
            rows = pl.ds((0, 2 * HALO)[p], PW)
            wr, wi = obj_ref[0, rows, :], obj_ref[1, rows, :]
        else:
            wr, wi = [lifted(obj_ref[ch, pl.ds(third, PW + 8), :], shift) for ch in range(2)]
        pr, pi = probe_ref[0], probe_ref[1]
        exit_wave = jnp.concatenate(
            [(pr * wr - pi * wi).astype(BF16), (pr * wi + pi * wr).astype(BF16)], axis=0
        )
        half = jnp.dot(fwd, exit_wave, preferred_element_type=F32)
        half = jnp.concatenate([half[:PW].astype(BF16), half[PW:].astype(BF16)], axis=1)
        spec = jnp.dot(half, inv, preferred_element_type=F32)
        sr, si = spec[:, :PW], spec[:, PW:]
        scaling = amp_ref[p] * lax.rsqrt(jnp.maximum(sr * sr + si * si, 0.25))
        miss = jnp.concatenate(
            [(sr - scaling * sr).astype(BF16), (si - scaling * si).astype(BF16)], axis=0
        )
        half = jnp.dot(inv, miss, preferred_element_type=F32)
        half = jnp.concatenate([half[:PW].astype(BF16), half[PW:].astype(BF16)], axis=1)
        back = jnp.dot(half, fwd, preferred_element_type=F32)
        br, bi = back[:, :PW], back[:, PW:]
        for ch, og in ((0, pr * br + pi * bi), (1, pr * bi - pi * br)):
            for ref, part in ((gl_ref, og[:, :LANES]), (gr_ref, og[:, LANES:])):
                if p == 0:
                    ref[ch, 0:PW, :] = part
                elif p == 1:
                    ref[ch, 2 * HALO : PW, :] += part[: 2 * HALO]
                    ref[ch, PW:EXT, :] = part[2 * HALO :]
                else:
                    ref[ch, pl.ds(third, PW + 8), :] += lowered(part, shift)
        if pg_ref is not None:
            sums = (wr * br + wi * bi, wr * bi - wi * br, wr * wr + wi * wi)
            for ch, value in enumerate(sums):
                if p == 0:
                    pg_ref[ch] = value
                else:
                    pg_ref[ch] += value


def split_probe_grad(place_ref, pg_ref, keep_ref, send_ref):
    c, x, y = place_ref[3], place_ref[4], place_ref[5]
    for k in range(4):
        for j in range(4):
            block = (x ^ k) * 4 + (y ^ j)
            for half, ref in ((c, keep_ref), (1 - c, send_ref)):
                row = pl.multiple_of((half * 16 + block) * 8, 8)
                for ch in range(3):
                    ref[k * 4 + j, ch * 8 : ch * 8 + 8, :] = pg_ref[ch, pl.ds(row, 8), :]


def pass_kernel(first, last_inner, fresh_probe, *refs):
    refs = list(refs)
    place_ref = refs.pop(0)
    obj_ref = refs.pop(0)
    parts = None if first else [refs.pop(0) for _ in range(6)]
    probe_ref = refs.pop(0)
    sums = [refs.pop(0) for _ in range(2)] if fresh_probe else None
    amp_ref, fwd_ref, inv_ref = [refs.pop(0) for _ in range(3)]
    gl_ref, gr_ref = [refs.pop(0) for _ in range(2)]
    if not first:
        out_ref = refs.pop(0)

        def store(ch, block, side, value):
            rows = slice(block * LANES, (block + 1) * LANES)
            out_ref[ch, rows, side * LANES : (side + 1) * LANES] = value

        updated(place_ref, probe_ref, obj_ref, parts, store)
        obj_ref = out_ref
    if fresh_probe:
        fresh_ref = refs.pop(0)
    if last_inner:
        keep_ref, send_ref = [refs.pop(0) for _ in range(2)]
    if fresh_probe:
        new_probe(place_ref, probe_ref, sums[0], sums[1], refs[-1], fresh_ref)
        probe_ref = fresh_ref
    pg_ref = refs[-1] if last_inner else None
    patterns(place_ref, obj_ref, probe_ref, amp_ref, fwd_ref, inv_ref, gl_ref, gr_ref, pg_ref)
    if last_inner:
        split_probe_grad(place_ref, pg_ref, keep_ref, send_ref)


def run_pass(where, obj, parts, probe, sums, amp, tables, last_inner):
    first, fresh = parts is None, sums is not None
    args = [where, obj] + ([] if first else list(parts)) + [probe]
    args += (list(sums) if fresh else []) + [amp, *tables]
    outs = [(2, EXT, LANES)] * 2
    outs += [] if first else [(2, EXT, PW)]
    outs += [(2, PW, PW)] if fresh else []
    outs += [(16, 24, PW)] * 2 if last_inner else []
    scratch = [pltpu.VMEM((3, PW, PW), F32)] if fresh or last_inner else []
    kernel = functools.partial(pass_kernel, first, last_inner, fresh)
    got = list(vmem_call(kernel, outs, scratch, *args, grant=24 << 20))
    gl, gr = got.pop(0), got.pop(0)
    obj = obj if first else got.pop(0)
    probe = got.pop(0) if fresh else probe
    return gl, gr, obj, probe, got


def object_kernel(place_ref, obj_ref, gl, gr, rl, rr, rt, rb, probe_ref, out_ref, middle_ref):
    def store(ch, block, side, value):
        rows = slice(block * LANES, (block + 1) * LANES)
        out_ref[ch, rows, side * LANES : (side + 1) * LANES] = value

    updated(place_ref, probe_ref, obj_ref, (gl, gr, rl, rr, rt, rb), store)
    middle_ref[...] = out_ref[:, HALO : HALO + PW, HALO : HALO + TILE_W]


def probe_kernel(place_ref, probe_ref, near_ref, far_ref, out_ref, total_ref):
    new_probe(place_ref, probe_ref, near_ref, far_ref, total_ref, out_ref)


def exchange_columns(gl, gr):
    return gl, gr, send(gr, neighbour(0, 1)), send(gl, neighbour(0, -1))


def exchange_rows(where, gl, gr, rl, rr):
    def edges(place_ref, gl, gr, rl, rr, top, bottom):
        t = place_ref[2]
        halves = (slice(0, LANES), gl, rl, t == 0), (slice(LANES, PW), gr, rr, t == TILES - 1)
        for ch in range(2):
            for cols, a, b, end in halves:
                top[ch, :, cols] = a[ch, 0:LANES, :] + unless(end, b[ch, 0:LANES, :])
                bottom[ch, :, cols] = a[ch, PW:EXT, :] + unless(end, b[ch, PW:EXT, :])

    shapes = [(2, LANES, PW)] * 2
    top, bottom = vmem_call(edges, shapes, [], where, gl, gr, rl, rr)
    rt = send(bottom, neighbour(1, 0))
    rb = send(top, neighbour(-1, 0))
    return gl, gr, rl, rr, rt, rb


def add_split(shape, parts, *arrays):
    count = len(arrays)
    rows = shape[0] // parts

    def kernel(*refs):
        ins, outs = refs[:count], refs[count:]
        for k, out in enumerate(outs):
            value = ins[0][k * rows : (k + 1) * rows]
            for ref in ins[1:]:
                value = value + ref[k * rows : (k + 1) * rows]
            out[...] = value

    return vmem_call(kernel, [(rows, *shape[1:])] * parts, [], *arrays)


def add_pairs(*arrays):
    def kernel(a, b, c, d, out):
        out[...] = (a[...] + b[...]) + (c[...] + d[...])

    return vmem_call(kernel, [arrays[0].shape], [], *arrays)[0]


def join(*arrays):
    rows = arrays[0].shape[0]

    def kernel(*refs):
        for k, ref in enumerate(refs[:-1]):
            refs[-1][k * rows : (k + 1) * rows] = ref[...]

    shape = (rows * len(arrays), *arrays[0].shape[1:])
    return vmem_call(kernel, [shape], [], *arrays)[0]


def exchange(where, gl, gr):
    return exchange_rows(where, *exchange_columns(gl, gr))


def exchange_and_total(where, obj, probe, gl, gr, keep, sent):
    columns = exchange_columns(gl, gr)
    arrived = send(sent, core_swap())
    parts = add_split((16, 24, PW), 4, keep, arrived)
    arrived = [send(parts[k], along_x(k)) for k in (1, 2, 3)]
    rows = exchange_rows(where, *columns)
    parts = add_split((4, 24, PW), 4, parts[0], *arrived)
    arrived = [send(parts[k], along_y(k)) for k in (1, 2, 3)]
    value = add_split((1, 24, PW), 1, parts[0], *arrived)[0]
    value = add_split((1, 24, PW), 1, value, send(value, next_z()))[0]
    outs = [(2, EXT, PW), (2, PW, TILE_W)]
    obj, middle = vmem_call(object_kernel, outs, [], where, obj, *rows, probe)
    object_out = send(middle, from_host())
    far = send(value, far_z())
    above, below = send(value, along_z(2)), send(value, along_z(-2))
    value = add_pairs(value, far, above, below)
    value, object_out = lax.optimization_barrier((value, object_out))
    value = join(value, *[send(value, along_y(k)) for k in (1, 2, 3)])
    value = join(value, *[send(value, along_x(k)) for k in (1, 2, 3)])
    return obj, object_out, value, send(value, core_swap())


def first_windows(current, s, t):
    def packed(half):
        return jnp.concatenate([half[:, : PW // 2], half[:, PW // 2 :]], axis=2)

    def unpacked(value):
        return jnp.concatenate([value[:, :, :HALO], value[:, :, HALO:]], axis=1)

    left = unpacked(send(packed(current[:, :, TILE_W - HALO :]), neighbour(0, 1)))
    right = unpacked(send(packed(current[:, :, :HALO]), neighbour(0, -1)))
    left, right = jnp.where(t == 0, 0.0, left), jnp.where(t == TILES - 1, 0.0, right)
    wide = jnp.concatenate([left, current, right], axis=2)
    top = send(wide[:, PW - HALO :], neighbour(1, 0))
    bottom = send(wide[:, :HALO], neighbour(-1, 0))
    top, bottom = jnp.where(s == 0, 0.0, top), jnp.where(s == STRIPES - 1, 0.0, bottom)
    return jnp.concatenate([top, wide, bottom], axis=1)


def per_device(positions, row_offsets, amplitudes, object_field, probe_field):
    tables = dft_tables()
    stripe, tile = lax.axis_index("stripe"), lax.axis_index("tile")
    core, x, y, z = stripe % 2, (tile % 2) * 2 + (stripe // 2) % 2, tile // 2, stripe // 4
    s, t = z * 4 + x, y * 2 + core
    current = send(object_field, to_host())
    amp = send(amplitudes[0], to_host())
    offset = send(row_offsets, to_host())[0, 2] + HALO
    obj = first_windows(current, s, t)
    third = jnp.minimum(offset // 8, 15) * 8
    where = jnp.stack([third, s, t, core, x, y, offset - third]).astype(jnp.int32)

    def outer(unused, state):
        obj, unused, probe, near, far = state
        sums = (near, far)
        gl, gr, obj, probe, _ = run_pass(where, obj, None, probe, sums, amp, tables, False)
        parts = exchange(where, gl, gr)
        gl, gr, obj, probe, rest = run_pass(where, obj, parts, probe, None, amp, tables, True)
        obj, object_out, near, far = exchange_and_total(where, obj, probe, gl, gr, *rest)
        return obj, object_out, probe, near, far

    none = jnp.zeros((16, 24, PW), F32)
    state = (obj, jnp.zeros_like(object_field), probe_field, none, none)
    obj, object_out, probe, near, far = lax.fori_loop(0, OUTER, outer, state)
    scratch, args = [pltpu.VMEM((3, PW, PW), F32)], (where, probe, near, far)
    probe_out = vmem_call(probe_kernel, [(2, PW, PW)], scratch, *args, held=False)[0]
    return object_out, probe_out


def solution(mesh):
    placed = (
        P("stripe", "tile"),
        P("stripe", "tile"),
        P("stripe", "tile", None, None),
        P(None, "stripe", "tile"),
        P(),
    )
    return jax.shard_map(
        per_device,
        mesh=mesh,
        in_specs=placed,
        out_specs=(P(None, "stripe", "tile"), P()),
        check_vma=False,
    )
```

profile of v0, /device:TPU:2, one launch (start us, length us, event | category | flops | bytes accessed | tf_op | source)
XLA Modules:
  0.0 252.1 jit_solution(15395892196252336361)
XLA Ops:
  1.6 3.4 %collective-permute-start.27 = (f32[2,256,128]{2,1,0:T(8,128)S(1)}, f32[2,256,128]{2,1,0:T(8,128)S(1)}, u32[]{:S(2)}, u32[]{:S(2)}) collective-permute-start(f32[2,256,128]{2,1,0:T(8,128)S(1)} %copy-done.5), channel_id=1, source_target_pairs={{0,0},{1,8},{2,2},{3,10},{4,4},{5,12},{6,6},{7,14},{8,16},{9,24},{... | collective-permute-start | bytes 786440 | tf_op jit(solution)/shard_map/ppermute | solution.py:87
  5.0 4.3 %collective-permute-done.27 = f32[2,256,128]{2,1,0:T(8,128)S(1)} collective-permute-done((f32[2,256,128]{2,1,0:T(8,128)S(1)}, f32[2,256,128]{2,1,0:T(8,128)S(1)}, u32[]{:S(2)}, u32[]{:S(2)}) %collective-permute-start.27) | collective-permute-done | bytes 262176 | tf_op jit(solution)/shard_map/ppermute | solution.py:87
  11.9 3.8 %collective-permute-start.33 = (f32[3,256,256]{2,1,0:T(8,128)}, f32[3,256,256]{2,1,0:T(8,128)S(1)}, u32[]{:S(2)}, u32[]{:S(2)}) collective-permute-start(f32[3,256,256]{2,1,0:T(8,128)} %bitcast.8), channel_id=1, source_target_pairs={{0,0},{1,8},{2,2},{3,10},{4,4},{5,12},{6,6},{7,14},{8,16},{9,24},{... | collective-permute-start | bytes 2359304 | tf_op jit(solution)/shard_map/ppermute | solution.py:87
  15.9 5.5 %collective-permute-done.28 = f32[2,128,128]{2,1,0:T(8,128)S(1)} collective-permute-done((f32[2,128,128]{2,1,0:T(8,128)S(1)}, f32[2,128,128]{2,1,0:T(8,128)S(1)}, u32[]{:S(2)}, u32[]{:S(2)}) %collective-permute-start.28) | collective-permute-done | bytes 131104 | tf_op jit(solution)/shard_map/ppermute | solution.py:87
  24.4 3.8 %collective-permute-done.32 = s32[1,3]{1,0:T(1,128)S(1)} collective-permute-done((s32[1,3]{1,0:T(1,128)S(1)}, s32[1,3]{1,0:T(1,128)S(1)}, u32[]{:S(2)}, u32[]{:S(2)}) %collective-permute-start.32) | collective-permute-done | bytes 44 | tf_op jit(solution)/shard_map/ppermute | solution.py:87
  29.5 5.4 %collective-permute-done.31 = f32[2,64,256]{2,1,0:T(8,128)S(1)} collective-permute-done((f32[2,64,256]{2,1,0:T(8,128)S(1)}, f32[2,64,256]{2,1,0:T(8,128)S(1)}, u32[]{:S(2)}, u32[]{:S(2)}) %collective-permute-start.31) | collective-permute-done | bytes 131104 | tf_op jit(solution)/shard_map/ppermute | solution.py:87
  36.5 212.8 %while.19 = (s32[]{:T(128)}, f32[2,384,256]{2,1,0:T(8,128)S(1)}, f32[2,256,128]{2,1,0:T(8,128)}, f32[2,256,256]{2,1,0:T(8,128)S(1)}, f32[16,24,256]{2,1,0:T(8,12...) while((s32[]{:T(128)}, f32[2,384,256]{2,1,0:T(8,128)S(1)}, ...), condition=%wide.region_1.2_spmd.clone, body=%wide.region_0.1_spmd.sunk.clone.sunk | while | flops 2 | bytes 20120768 | solution.py:417
  36.6 4.4 %eval_jaxpr.12 = (f32[2,384,128]{2,1,0:T(8,128)S(1)}, f32[2,384,128]{2,1,0:T(8,128)S(1)}, f32[2,256,256]{2,1,0:T(8,128)S(1)}) custom-call(s32[7]{0:T(128)S(1)} %get-tuple-element.310.refs_0_.place_ref, f32[2,384,256]{2,1,0:T(8,128)S(1)} %get-tuple-element.294.refs_1_, f32[2,256,256]{2,1,0:T(8,128)S(1)} %copy.32.refs_2_, ...), custom_call_target="tpu_custom_call" | custom-call | tf_op jit(solution)/shard_map/while/body/eval_jaxpr/pallas_call | solution.py:106
  42.4 5.3 %collective-permute-done.1.rr.refs_5_ = f32[2,384,128]{2,1,0:T(8,128)S(1)} collective-permute-done((f32[2,384,128]{2,1,0:T(8,128)S(1)}, f32[2,384,128]{2,1,0:T(8,128)S(1)}, u32[]{:S(2)}, u32[]{:S(2)}) %collective-permute-start.1) | collective-permute-done | bytes 393248 | tf_op jit(solution)/shard_map/while/body/eval_jaxpr/ppermute | solution.py:87
  47.7 3.1 %collective-permute-done.rl.refs_4_ = f32[2,384,128]{2,1,0:T(8,128)S(1)} collective-permute-done((f32[2,384,128]{2,1,0:T(8,128)S(1)}, f32[2,384,128]{2,1,0:T(8,128)S(1)}, u32[]{:S(2)}, u32[]{:S(2)}) %collective-permute-start) | collective-permute-done | bytes 393248 | tf_op jit(solution)/shard_map/while/body/eval_jaxpr/ppermute | solution.py:87
  53.9 5.2 %collective-permute-done.2.refs_6_ = f32[2,128,256]{2,1,0:T(8,128)S(1)} collective-permute-done((f32[2,128,256]{2,1,0:T(8,128)S(1)}, f32[2,128,256]{2,1,0:T(8,128)S(1)}, u32[]{:S(2)}, u32[]{:S(2)}) %collective-permute-start.2) | collective-permute-done | bytes 262176 | tf_op jit(solution)/shard_map/while/body/eval_jaxpr/ppermute | solution.py:87
  61.1 4.6 %eval_jaxpr.14 = (f32[2,384,128]{2,1,0:T(8,128)S(1)}, f32[2,384,128]{2,1,0:T(8,128)S(1)}, f32[2,384,256]{2,1,0:T(8,128)S(1)}, f32[16,24,256]{2,1,0:T(8,128)S(1)}, f32[16,24,256]{2,1,0:T(8,128)S(1)}) custom-call(s32[7]{0:T(128)S(1)} %get-tuple-element.310.refs_0_.place_ref, f32[2,384,256]{2,1,0:T(8,128)S(1)} %get-tuple-element.294.refs_1_, ...), custom_call_target="tpu_custom_call" | custom-call | tf_op jit(solution)/shard_map/while/body/eval_jaxpr/pallas_call | solution.py:106
  66.9 5.3 %collective-permute-done.5.rr = f32[2,384,128]{2,1,0:T(8,128)S(1)} collective-permute-done((f32[2,384,128]{2,1,0:T(8,128)S(1)}, f32[2,384,128]{2,1,0:T(8,128)S(1)}, u32[]{:S(2)}, u32[]{:S(2)}) %collective-permute-start.5) | collective-permute-done | bytes 393248 | tf_op jit(solution)/shard_map/while/body/eval_jaxpr/ppermute | solution.py:87
  72.2 3.1 %collective-permute-done.4.rl = f32[2,384,128]{2,1,0:T(8,128)S(1)} collective-permute-done((f32[2,384,128]{2,1,0:T(8,128)S(1)}, f32[2,384,128]{2,1,0:T(8,128)S(1)}, u32[]{:S(2)}, u32[]{:S(2)}) %collective-permute-start.4) | collective-permute-done | bytes 393248 | tf_op jit(solution)/shard_map/while/body/eval_jaxpr/ppermute | solution.py:87
  78.8 5.3 %collective-permute-done.6.rt = f32[2,128,256]{2,1,0:T(8,128)S(1)} collective-permute-done((f32[2,128,256]{2,1,0:T(8,128)S(1)}, f32[2,128,256]{2,1,0:T(8,128)S(1)}, u32[]{:S(2)}, u32[]{:S(2)}) %collective-permute-start.6) | collective-permute-done | bytes 262176 | tf_op jit(solution)/shard_map/while/body/eval_jaxpr/ppermute | solution.py:87
  86.8 3.1 %collective-permute-start.19 = (f32[2,256,128]{2,1,0:T(8,128)S(1)}, f32[2,256,128]{2,1,0:T(8,128)S(1)}, u32[]{:S(2)}, u32[]{:S(2)}) collective-permute-start(f32[2,256,128]{2,1,0:T(8,128)S(1)} %get-tuple-element.279), channel_id=1, source_target_pairs={{0,0},{8,1},{2,2},{10,3},{4,4},{12,5},{6,6},{14,7},{16,8},{24,9},{... | collective-permute-start | bytes 786440 | tf_op jit(solution)/shard_map/while/body/eval_jaxpr/ppermute | solution.py:87
  96.4 4.6 %collective-permute-done.10.refs_2_ = f32[4,24,256]{2,1,0:T(8,128)S(1)} collective-permute-done((f32[4,24,256]{2,1,0:T(8,128)S(1)}, f32[4,24,256]{2,1,0:T(8,128)S(1)}, u32[]{:S(2)}, u32[]{:S(2)}) %collective-permute-start.10) | collective-permute-done | bytes 98336 | tf_op jit(solution)/shard_map/while/body/eval_jaxpr/ppermute | solution.py:87
  113.9 5.7 %collective-permute-start.18 = (f32[1,24,256]{2,1,0:T(8,128)S(1)}, f32[1,24,256]{2,1,0:T(8,128)S(1)}, u32[]{:S(2)}, u32[]{:S(2)}) collective-permute-start(f32[1,24,256]{2,1,0:T(8,128)S(1)} %eval_jaxpr.20.a), channel_id=1, source_target_pairs={{0,192},{1,193},{2,194},{3,195},{4,196},{5,197},{6,198},{7,199},{8... | collective-permute-start | bytes 73736 | tf_op jit(solution)/shard_map/while/body/eval_jaxpr/ppermute | solution.py:87
  120.5 4.0 %collective-permute-start.16 = (f32[1,24,256]{2,1,0:T(8,128)S(1)}, f32[1,24,256]{2,1,0:T(8,128)S(1)}, u32[]{:S(2)}, u32[]{:S(2)}) collective-permute-start(f32[1,24,256]{2,1,0:T(8,128)S(1)} %eval_jaxpr.20.a), channel_id=1, source_target_pairs={{0,160},{1,161},{2,162},{3,163},{4,164},{5,165},{6,166},{7,167},{8... | collective-permute-start | bytes 73736 | tf_op jit(solution)/shard_map/while/body/eval_jaxpr/ppermute | solution.py:87
  145.3 4.4 %eval_jaxpr.12 = (f32[2,384,128]{2,1,0:T(8,128)S(1)}, f32[2,384,128]{2,1,0:T(8,128)S(1)}, f32[2,256,256]{2,1,0:T(8,128)S(1)}) custom-call(s32[7]{0:T(128)S(1)} %get-tuple-element.310.refs_0_.place_ref, f32[2,384,256]{2,1,0:T(8,128)S(1)} %get-tuple-element.294.refs_1_, f32[2,256,256]{2,1,0:T(8,128)S(1)} %copy.32.refs_2_, ...), custom_call_target="tpu_custom_call" | custom-call | tf_op jit(solution)/shard_map/while/body/eval_jaxpr/pallas_call | solution.py:106
  150.8 5.3 %collective-permute-done.1.rr.refs_5_ = f32[2,384,128]{2,1,0:T(8,128)S(1)} collective-permute-done((f32[2,384,128]{2,1,0:T(8,128)S(1)}, f32[2,384,128]{2,1,0:T(8,128)S(1)}, u32[]{:S(2)}, u32[]{:S(2)}) %collective-permute-start.1) | collective-permute-done | bytes 393248 | tf_op jit(solution)/shard_map/while/body/eval_jaxpr/ppermute | solution.py:87
  156.1 3.1 %collective-permute-done.rl.refs_4_ = f32[2,384,128]{2,1,0:T(8,128)S(1)} collective-permute-done((f32[2,384,128]{2,1,0:T(8,128)S(1)}, f32[2,384,128]{2,1,0:T(8,128)S(1)}, u32[]{:S(2)}, u32[]{:S(2)}) %collective-permute-start) | collective-permute-done | bytes 393248 | tf_op jit(solution)/shard_map/while/body/eval_jaxpr/ppermute | solution.py:87
  162.0 4.3 %collective-permute-done.2.refs_6_ = f32[2,128,256]{2,1,0:T(8,128)S(1)} collective-permute-done((f32[2,128,256]{2,1,0:T(8,128)S(1)}, f32[2,128,256]{2,1,0:T(8,128)S(1)}, u32[]{:S(2)}, u32[]{:S(2)}) %collective-permute-start.2) | collective-permute-done | bytes 262176 | tf_op jit(solution)/shard_map/while/body/eval_jaxpr/ppermute | solution.py:87
  166.7 4.6 %eval_jaxpr.14 = (f32[2,384,128]{2,1,0:T(8,128)S(1)}, f32[2,384,128]{2,1,0:T(8,128)S(1)}, f32[2,384,256]{2,1,0:T(8,128)S(1)}, f32[16,24,256]{2,1,0:T(8,128)S(1)}, f32[16,24,256]{2,1,0:T(8,128)S(1)}) custom-call(s32[7]{0:T(128)S(1)} %get-tuple-element.310.refs_0_.place_ref, f32[2,384,256]{2,1,0:T(8,128)S(1)} %get-tuple-element.294.refs_1_, ...), custom_call_target="tpu_custom_call" | custom-call | tf_op jit(solution)/shard_map/while/body/eval_jaxpr/pallas_call | solution.py:106
  172.3 5.3 %collective-permute-done.5.rr = f32[2,384,128]{2,1,0:T(8,128)S(1)} collective-permute-done((f32[2,384,128]{2,1,0:T(8,128)S(1)}, f32[2,384,128]{2,1,0:T(8,128)S(1)}, u32[]{:S(2)}, u32[]{:S(2)}) %collective-permute-start.5) | collective-permute-done | bytes 393248 | tf_op jit(solution)/shard_map/while/body/eval_jaxpr/ppermute | solution.py:87
  177.6 3.1 %collective-permute-done.4.rl = f32[2,384,128]{2,1,0:T(8,128)S(1)} collective-permute-done((f32[2,384,128]{2,1,0:T(8,128)S(1)}, f32[2,384,128]{2,1,0:T(8,128)S(1)}, u32[]{:S(2)}, u32[]{:S(2)}) %collective-permute-start.4) | collective-permute-done | bytes 393248 | tf_op jit(solution)/shard_map/while/body/eval_jaxpr/ppermute | solution.py:87
  181.4 3.1 %collective-permute-start.6 = (f32[2,128,256]{2,1,0:T(8,128)S(1)}, f32[2,128,256]{2,1,0:T(8,128)S(1)}, u32[]{:S(2)}, u32[]{:S(2)}) collective-permute-start(f32[2,128,256]{2,1,0:T(8,128)S(1)} %get-tuple-element.266), channel_id=1, source_target_pairs={{0,16},{8,24},{2,18},{10,26},{4,20},{12,28},{6,22},{14,30},{16,1},... | collective-permute-start | bytes 786440 | tf_op jit(solution)/shard_map/while/body/eval_jaxpr/ppermute | solution.py:87
  185.8 4.3 %collective-permute-done.6.rt = f32[2,128,256]{2,1,0:T(8,128)S(1)} collective-permute-done((f32[2,128,256]{2,1,0:T(8,128)S(1)}, f32[2,128,256]{2,1,0:T(8,128)S(1)}, u32[]{:S(2)}, u32[]{:S(2)}) %collective-permute-start.6) | collective-permute-done | bytes 262176 | tf_op jit(solution)/shard_map/while/body/eval_jaxpr/ppermute | solution.py:87
  200.7 7.5 %collective-permute-done.10.refs_2_ = f32[4,24,256]{2,1,0:T(8,128)S(1)} collective-permute-done((f32[4,24,256]{2,1,0:T(8,128)S(1)}, f32[4,24,256]{2,1,0:T(8,128)S(1)}, u32[]{:S(2)}, u32[]{:S(2)}) %collective-permute-start.10) | collective-permute-done | bytes 98336 | tf_op jit(solution)/shard_map/while/body/eval_jaxpr/ppermute | solution.py:87
  209.1 3.4 %collective-permute-start.13 = (f32[1,24,256]{2,1,0:T(8,128)S(1)}, f32[1,24,256]{2,1,0:T(8,128)S(1)}, u32[]{:S(2)}, u32[]{:S(2)}) collective-permute-start(f32[1,24,256]{2,1,0:T(8,128)S(1)} %get-tuple-element.277), channel_id=1, source_target_pairs={{0,4},{1,5},{2,6},{3,7},{4,0},{5,1},{6,2},{7,3},{8,12},{9,13},{10,... | collective-permute-start | bytes 73736 | tf_op jit(solution)/shard_map/while/body/eval_jaxpr/ppermute | solution.py:87
  225.5 3.1 %collective-permute-start.16 = (f32[1,24,256]{2,1,0:T(8,128)S(1)}, f32[1,24,256]{2,1,0:T(8,128)S(1)}, u32[]{:S(2)}, u32[]{:S(2)}) collective-permute-start(f32[1,24,256]{2,1,0:T(8,128)S(1)} %eval_jaxpr.20.a), channel_id=1, source_target_pairs={{0,160},{1,161},{2,162},{3,163},{4,164},{5,165},{6,166},{7,167},{8... | collective-permute-start | bytes 73736 | tf_op jit(solution)/shard_map/while/body/eval_jaxpr/ppermute | solution.py:87
  233.5 3.1 %collective-permute-start.20 = (f32[1,24,256]{2,1,0:T(8,128)S(1)}, f32[1,24,256]{2,1,0:T(8,128)S(1)}, u32[]{:S(2)}, u32[]{:S(2)}) collective-permute-start(f32[1,24,256]{2,1,0:T(8,128)S(1)} %eval_jaxpr.21.refs_0_), channel_id=1, source_target_pairs={{0,2},{1,3},{2,0},{3,1},{4,6},{5,7},{6,4},{7,5},{8,10},{9,11},{10,... | collective-permute-start | bytes 73736 | tf_op jit(solution)/shard_map/while/body/eval_jaxpr/ppermute | solution.py:87
  (150 shorter events, 115.7 us)
Async XLA Ops:
  1.6 7.7 %collective-permute-start.27 = (f32[2,256,128]{2,1,0:T(8,128)S(1)}, f32[2,256,128]{2,1,0:T(8,128)S(1)}, u32[]{:S(2)}, u32[]{:S(2)}) collective-permute-start(f32[2,256,128]{2,1,0:T(8,128)S(1)} %copy-done.5), channel_id=1, source_target_pairs={{0,0},{1,8},{2,2},{3,10},{4,4},{5,12},{6,6},{7,14},{8,16},{9,24},{... | collective-permute-start | bytes 786440 | tf_op jit(solution)/shard_map/ppermute | solution.py:87
  9.5 6.3 %collective-permute-start.29 = (f32[2,128,128]{2,1,0:T(8,128)S(1)}, f32[2,128,128]{2,1,0:T(8,128)S(1)}, u32[]{:S(2)}, u32[]{:S(2)}) collective-permute-start(f32[2,128,128]{2,1,0:T(8,128)S(1)} %pad_maximum_fusion.5), channel_id=1, source_target_pairs={{0,14},{8,0},{2,8},{10,2},{4,10},{12,4},{6,12},{14,6},{16,30},{24,... | collective-permute-start | bytes 393224 | tf_op jit(solution)/shard_map/ppermute | solution.py:87
  11.9 23.4 %collective-permute-start.33 = (f32[3,256,256]{2,1,0:T(8,128)}, f32[3,256,256]{2,1,0:T(8,128)S(1)}, u32[]{:S(2)}, u32[]{:S(2)}) collective-permute-start(f32[3,256,256]{2,1,0:T(8,128)} %bitcast.8), channel_id=1, source_target_pairs={{0,0},{1,8},{2,2},{3,10},{4,4},{5,12},{6,6},{7,14},{8,16},{9,24},{... | collective-permute-start | bytes 2359304 | tf_op jit(solution)/shard_map/ppermute | solution.py:87
  21.8 7.7 %collective-permute-start.30 = (f32[2,64,256]{2,1,0:T(8,128)S(1)}, f32[2,64,256]{2,1,0:T(8,128)S(1)}, u32[]{:S(2)}, u32[]{:S(2)}) collective-permute-start(f32[2,64,256]{2,1,0:T(8,128)S(1)} %get-tuple-element.175), channel_id=1, source_target_pairs={{0,16},{8,24},{2,18},{10,26},{4,20},{12,28},{6,22},{14,30},{16,1},... | collective-permute-start | bytes 393224 | tf_op jit(solution)/shard_map/ppermute | solution.py:87
  41.0 6.7 %collective-permute-start.1 = (f32[2,384,128]{2,1,0:T(8,128)S(1)}, f32[2,384,128]{2,1,0:T(8,128)S(1)}, u32[]{:S(2)}, u32[]{:S(2)}) collective-permute-start(f32[2,384,128]{2,1,0:T(8,128)S(1)} %get-tuple-element.258.gl.refs_2_), channel_id=1, source_target_pairs={{0,14},{8,0},{2,8},{10,2},{4,10},{12,4},{6,12},{14,6},{16,30},{24,... | collective-permute-start | bytes 1179656 | tf_op jit(solution)/shard_map/while/body/eval_jaxpr/ppermute | solution.py:87
  42.4 8.4 %collective-permute-start = (f32[2,384,128]{2,1,0:T(8,128)S(1)}, f32[2,384,128]{2,1,0:T(8,128)S(1)}, u32[]{:S(2)}, u32[]{:S(2)}) collective-permute-start(f32[2,384,128]{2,1,0:T(8,128)S(1)} %get-tuple-element.259.gr.refs_3_), channel_id=1, source_target_pairs={{0,8},{8,2},{2,10},{10,4},{4,12},{12,6},{6,14},{14,0},{16,24},{24,... | collective-permute-start | bytes 1179656 | tf_op jit(solution)/shard_map/while/body/eval_jaxpr/ppermute | solution.py:87
  51.4 7.8 %collective-permute-start.2 = (f32[2,128,256]{2,1,0:T(8,128)S(1)}, f32[2,128,256]{2,1,0:T(8,128)S(1)}, u32[]{:S(2)}, u32[]{:S(2)}) collective-permute-start(f32[2,128,256]{2,1,0:T(8,128)S(1)} %get-tuple-element.260), channel_id=1, source_target_pairs={{0,16},{8,24},{2,18},{10,26},{4,20},{12,28},{6,22},{14,30},{16,1},... | collective-permute-start | bytes 786440 | tf_op jit(solution)/shard_map/while/body/eval_jaxpr/ppermute | solution.py:87
  52.2 8.9 %collective-permute-start.3 = (f32[2,128,256]{2,1,0:T(8,128)S(1)}, f32[2,128,256]{2,1,0:T(8,128)S(1)}, u32[]{:S(2)}, u32[]{:S(2)}) collective-permute-start(f32[2,128,256]{2,1,0:T(8,128)S(1)} %get-tuple-element.261), channel_id=1, source_target_pairs={{0,241},{8,249},{2,243},{10,251},{4,245},{12,253},{6,247},{14,255}... | collective-permute-start | bytes 786440 | tf_op jit(solution)/shard_map/while/body/eval_jaxpr/ppermute | solution.py:87
  65.7 6.5 %collective-permute-start.5 = (f32[2,384,128]{2,1,0:T(8,128)S(1)}, f32[2,384,128]{2,1,0:T(8,128)S(1)}, u32[]{:S(2)}, u32[]{:S(2)}) collective-permute-start(f32[2,384,128]{2,1,0:T(8,128)S(1)} %get-tuple-element.264.gl), channel_id=1, source_target_pairs={{0,14},{8,0},{2,8},{10,2},{4,10},{12,4},{6,12},{14,6},{16,30},{24,... | collective-permute-start | bytes 1179656 | tf_op jit(solution)/shard_map/while/body/eval_jaxpr/ppermute | solution.py:87
  66.9 8.4 %collective-permute-start.4 = (f32[2,384,128]{2,1,0:T(8,128)S(1)}, f32[2,384,128]{2,1,0:T(8,128)S(1)}, u32[]{:S(2)}, u32[]{:S(2)}) collective-permute-start(f32[2,384,128]{2,1,0:T(8,128)S(1)} %get-tuple-element.265.gr), channel_id=1, source_target_pairs={{0,8},{8,2},{2,10},{10,4},{4,12},{12,6},{6,14},{14,0},{16,24},{24,... | collective-permute-start | bytes 1179656 | tf_op jit(solution)/shard_map/while/body/eval_jaxpr/ppermute | solution.py:87
  66.9 23.0 %collective-permute-start.8 = (f32[16,24,256]{2,1,0:T(8,128)S(1)}, f32[16,24,256]{2,1,0:T(8,128)S(1)}, u32[]{:S(2)}, u32[]{:S(2)}) collective-permute-start(f32[16,24,256]{2,1,0:T(8,128)S(1)} %get-tuple-element.270), channel_id=1, source_target_pairs={{0,8},{1,9},{2,10},{3,11},{4,12},{5,13},{6,14},{7,15},{8,0},{9,1},... | collective-permute-start | bytes 1179656 | tf_op jit(solution)/shard_map/while/body/eval_jaxpr/ppermute | solution.py:87
  75.9 8.2 %collective-permute-start.6 = (f32[2,128,256]{2,1,0:T(8,128)S(1)}, f32[2,128,256]{2,1,0:T(8,128)S(1)}, u32[]{:S(2)}, u32[]{:S(2)}) collective-permute-start(f32[2,128,256]{2,1,0:T(8,128)S(1)} %get-tuple-element.266), channel_id=1, source_target_pairs={{0,16},{8,24},{2,18},{10,26},{4,20},{12,28},{6,22},{14,30},{16,1},... | collective-permute-start | bytes 786440 | tf_op jit(solution)/shard_map/while/body/eval_jaxpr/ppermute | solution.py:87
  78.1 7.6 %collective-permute-start.7 = (f32[2,128,256]{2,1,0:T(8,128)S(1)}, f32[2,128,256]{2,1,0:T(8,128)S(1)}, u32[]{:S(2)}, u32[]{:S(2)}) collective-permute-start(f32[2,128,256]{2,1,0:T(8,128)S(1)} %get-tuple-element.267), channel_id=1, source_target_pairs={{0,241},{8,249},{2,243},{10,251},{4,245},{12,253},{6,247},{14,255}... | collective-permute-start | bytes 786440 | tf_op jit(solution)/shard_map/while/body/eval_jaxpr/ppermute | solution.py:87
  86.8 40.6 %collective-permute-start.19 = (f32[2,256,128]{2,1,0:T(8,128)S(1)}, f32[2,256,128]{2,1,0:T(8,128)S(1)}, u32[]{:S(2)}, u32[]{:S(2)}) collective-permute-start(f32[2,256,128]{2,1,0:T(8,128)S(1)} %get-tuple-element.279), channel_id=1, source_target_pairs={{0,0},{8,1},{2,2},{10,3},{4,4},{12,5},{6,6},{14,7},{16,8},{24,9},{... | collective-permute-start | bytes 786440 | tf_op jit(solution)/shard_map/while/body/eval_jaxpr/ppermute | solution.py:87
  89.9 6.5 %collective-permute-start.9 = (f32[4,24,256]{2,1,0:T(8,128)S(1)}, f32[4,24,256]{2,1,0:T(8,128)S(1)}, u32[]{:S(2)}, u32[]{:S(2)}) collective-permute-start(f32[4,24,256]{2,1,0:T(8,128)S(1)} %get-tuple-element.272), channel_id=1, source_target_pairs={{0,16},{1,17},{2,18},{3,19},{4,20},{5,21},{6,22},{7,23},{8,24},{9,... | collective-permute-start | bytes 294920 | tf_op jit(solution)/shard_map/while/body/eval_jaxpr/ppermute | solution.py:87
  91.1 10.0 %collective-permute-start.10 = (f32[4,24,256]{2,1,0:T(8,128)S(1)}, f32[4,24,256]{2,1,0:T(8,128)S(1)}, u32[]{:S(2)}, u32[]{:S(2)}) collective-permute-start(f32[4,24,256]{2,1,0:T(8,128)S(1)} %get-tuple-element.273), channel_id=1, source_target_pairs={{0,1},{1,0},{2,3},{3,2},{4,5},{5,4},{6,7},{7,6},{8,9},{9,8},{10,11... | collective-permute-start | bytes 294920 | tf_op jit(solution)/shard_map/while/body/eval_jaxpr/ppermute | solution.py:87
  92.6 9.5 %collective-permute-start.11 = (f32[4,24,256]{2,1,0:T(8,128)S(1)}, f32[4,24,256]{2,1,0:T(8,128)S(1)}, u32[]{:S(2)}, u32[]{:S(2)}) collective-permute-start(f32[4,24,256]{2,1,0:T(8,128)S(1)} %get-tuple-element.274), channel_id=1, source_target_pairs={{0,17},{1,16},{2,19},{3,18},{4,21},{5,20},{6,23},{7,22},{8,25},{9,... | collective-permute-start | bytes 294920 | tf_op jit(solution)/shard_map/while/body/eval_jaxpr/ppermute | solution.py:87
  113.9 10.7 %collective-permute-start.18 = (f32[1,24,256]{2,1,0:T(8,128)S(1)}, f32[1,24,256]{2,1,0:T(8,128)S(1)}, u32[]{:S(2)}, u32[]{:S(2)}) collective-permute-start(f32[1,24,256]{2,1,0:T(8,128)S(1)} %eval_jaxpr.20.a), channel_id=1, source_target_pairs={{0,192},{1,193},{2,194},{3,195},{4,196},{5,197},{6,198},{7,199},{8... | collective-permute-start | bytes 73736 | tf_op jit(solution)/shard_map/while/body/eval_jaxpr/ppermute | solution.py:87
  120.5 6.8 %collective-permute-start.16 = (f32[1,24,256]{2,1,0:T(8,128)S(1)}, f32[1,24,256]{2,1,0:T(8,128)S(1)}, u32[]{:S(2)}, u32[]{:S(2)}) collective-permute-start(f32[1,24,256]{2,1,0:T(8,128)S(1)} %eval_jaxpr.20.a), channel_id=1, source_target_pairs={{0,160},{1,161},{2,162},{3,163},{4,164},{5,165},{6,166},{7,167},{8... | collective-permute-start | bytes 73736 | tf_op jit(solution)/shard_map/while/body/eval_jaxpr/ppermute | solution.py:87
  149.8 6.4 %collective-permute-start.1 = (f32[2,384,128]{2,1,0:T(8,128)S(1)}, f32[2,384,128]{2,1,0:T(8,128)S(1)}, u32[]{:S(2)}, u32[]{:S(2)}) collective-permute-start(f32[2,384,128]{2,1,0:T(8,128)S(1)} %get-tuple-element.258.gl.refs_2_), channel_id=1, source_target_pairs={{0,14},{8,0},{2,8},{10,2},{4,10},{12,4},{6,12},{14,6},{16,30},{24,... | collective-permute-start | bytes 1179656 | tf_op jit(solution)/shard_map/while/body/eval_jaxpr/ppermute | solution.py:87
  150.8 8.4 %collective-permute-start = (f32[2,384,128]{2,1,0:T(8,128)S(1)}, f32[2,384,128]{2,1,0:T(8,128)S(1)}, u32[]{:S(2)}, u32[]{:S(2)}) collective-permute-start(f32[2,384,128]{2,1,0:T(8,128)S(1)} %get-tuple-element.259.gr.refs_3_), channel_id=1, source_target_pairs={{0,8},{8,2},{2,10},{10,4},{4,12},{12,6},{6,14},{14,0},{16,24},{24,... | collective-permute-start | bytes 1179656 | tf_op jit(solution)/shard_map/while/body/eval_jaxpr/ppermute | solution.py:87
  159.9 6.4 %collective-permute-start.2 = (f32[2,128,256]{2,1,0:T(8,128)S(1)}, f32[2,128,256]{2,1,0:T(8,128)S(1)}, u32[]{:S(2)}, u32[]{:S(2)}) collective-permute-start(f32[2,128,256]{2,1,0:T(8,128)S(1)} %get-tuple-element.260), channel_id=1, source_target_pairs={{0,16},{8,24},{2,18},{10,26},{4,20},{12,28},{6,22},{14,30},{16,1},... | collective-permute-start | bytes 786440 | tf_op jit(solution)/shard_map/while/body/eval_jaxpr/ppermute | solution.py:87
  160.4 6.4 %collective-permute-start.3 = (f32[2,128,256]{2,1,0:T(8,128)S(1)}, f32[2,128,256]{2,1,0:T(8,128)S(1)}, u32[]{:S(2)}, u32[]{:S(2)}) collective-permute-start(f32[2,128,256]{2,1,0:T(8,128)S(1)} %get-tuple-element.261), channel_id=1, source_target_pairs={{0,241},{8,249},{2,243},{10,251},{4,245},{12,253},{6,247},{14,255}... | collective-permute-start | bytes 786440 | tf_op jit(solution)/shard_map/while/body/eval_jaxpr/ppermute | solution.py:87
  172.3 8.4 %collective-permute-start.4 = (f32[2,384,128]{2,1,0:T(8,128)S(1)}, f32[2,384,128]{2,1,0:T(8,128)S(1)}, u32[]{:S(2)}, u32[]{:S(2)}) collective-permute-start(f32[2,384,128]{2,1,0:T(8,128)S(1)} %get-tuple-element.265.gr), channel_id=1, source_target_pairs={{0,8},{8,2},{2,10},{10,4},{4,12},{12,6},{6,14},{14,0},{16,24},{24,... | collective-permute-start | bytes 1179656 | tf_op jit(solution)/shard_map/while/body/eval_jaxpr/ppermute | solution.py:87
  172.3 23.0 %collective-permute-start.8 = (f32[16,24,256]{2,1,0:T(8,128)S(1)}, f32[16,24,256]{2,1,0:T(8,128)S(1)}, u32[]{:S(2)}, u32[]{:S(2)}) collective-permute-start(f32[16,24,256]{2,1,0:T(8,128)S(1)} %get-tuple-element.270), channel_id=1, source_target_pairs={{0,8},{1,9},{2,10},{3,11},{4,12},{5,13},{6,14},{7,15},{8,0},{9,1},... | collective-permute-start | bytes 1179656 | tf_op jit(solution)/shard_map/while/body/eval_jaxpr/ppermute | solution.py:87
  181.4 8.7 %collective-permute-start.6 = (f32[2,128,256]{2,1,0:T(8,128)S(1)}, f32[2,128,256]{2,1,0:T(8,128)S(1)}, u32[]{:S(2)}, u32[]{:S(2)}) collective-permute-start(f32[2,128,256]{2,1,0:T(8,128)S(1)} %get-tuple-element.266), channel_id=1, source_target_pairs={{0,16},{8,24},{2,18},{10,26},{4,20},{12,28},{6,22},{14,30},{16,1},... | collective-permute-start | bytes 786440 | tf_op jit(solution)/shard_map/while/body/eval_jaxpr/ppermute | solution.py:87
  184.5 7.9 %collective-permute-start.7 = (f32[2,128,256]{2,1,0:T(8,128)S(1)}, f32[2,128,256]{2,1,0:T(8,128)S(1)}, u32[]{:S(2)}, u32[]{:S(2)}) collective-permute-start(f32[2,128,256]{2,1,0:T(8,128)S(1)} %get-tuple-element.267), channel_id=1, source_target_pairs={{0,241},{8,249},{2,243},{10,251},{4,245},{12,253},{6,247},{14,255}... | collective-permute-start | bytes 786440 | tf_op jit(solution)/shard_map/while/body/eval_jaxpr/ppermute | solution.py:87
  193.4 39.0 %collective-permute-start.19 = (f32[2,256,128]{2,1,0:T(8,128)S(1)}, f32[2,256,128]{2,1,0:T(8,128)S(1)}, u32[]{:S(2)}, u32[]{:S(2)}) collective-permute-start(f32[2,256,128]{2,1,0:T(8,128)S(1)} %get-tuple-element.279), channel_id=1, source_target_pairs={{0,0},{8,1},{2,2},{10,3},{4,4},{12,5},{6,6},{14,7},{16,8},{24,9},{... | collective-permute-start | bytes 786440 | tf_op jit(solution)/shard_map/while/body/eval_jaxpr/ppermute | solution.py:87
  197.2 10.9 %collective-permute-start.10 = (f32[4,24,256]{2,1,0:T(8,128)S(1)}, f32[4,24,256]{2,1,0:T(8,128)S(1)}, u32[]{:S(2)}, u32[]{:S(2)}) collective-permute-start(f32[4,24,256]{2,1,0:T(8,128)S(1)} %get-tuple-element.273), channel_id=1, source_target_pairs={{0,1},{1,0},{2,3},{3,2},{4,5},{5,4},{6,7},{7,6},{8,9},{9,8},{10,11... | collective-permute-start | bytes 294920 | tf_op jit(solution)/shard_map/while/body/eval_jaxpr/ppermute | solution.py:87
  199.7 8.8 %collective-permute-start.11 = (f32[4,24,256]{2,1,0:T(8,128)S(1)}, f32[4,24,256]{2,1,0:T(8,128)S(1)}, u32[]{:S(2)}, u32[]{:S(2)}) collective-permute-start(f32[4,24,256]{2,1,0:T(8,128)S(1)} %get-tuple-element.274), channel_id=1, source_target_pairs={{0,17},{1,16},{2,19},{3,18},{4,21},{5,20},{6,23},{7,22},{8,25},{9,... | collective-permute-start | bytes 294920 | tf_op jit(solution)/shard_map/while/body/eval_jaxpr/ppermute | solution.py:87
  222.0 6.6 %collective-permute-start.18 = (f32[1,24,256]{2,1,0:T(8,128)S(1)}, f32[1,24,256]{2,1,0:T(8,128)S(1)}, u32[]{:S(2)}, u32[]{:S(2)}) collective-permute-start(f32[1,24,256]{2,1,0:T(8,128)S(1)} %eval_jaxpr.20.a), channel_id=1, source_target_pairs={{0,192},{1,193},{2,194},{3,195},{4,196},{5,197},{6,198},{7,199},{8... | collective-permute-start | bytes 73736 | tf_op jit(solution)/shard_map/while/body/eval_jaxpr/ppermute | solution.py:87
  225.5 6.8 %collective-permute-start.16 = (f32[1,24,256]{2,1,0:T(8,128)S(1)}, f32[1,24,256]{2,1,0:T(8,128)S(1)}, u32[]{:S(2)}, u32[]{:S(2)}) collective-permute-start(f32[1,24,256]{2,1,0:T(8,128)S(1)} %eval_jaxpr.20.a), channel_id=1, source_target_pairs={{0,160},{1,161},{2,162},{3,163},{4,164},{5,165},{6,166},{7,167},{8... | collective-permute-start | bytes 73736 | tf_op jit(solution)/shard_map/while/body/eval_jaxpr/ppermute | solution.py:87
  (37 other events, 184.8 us)
where the time goes:
time: 254 us; the launch traced here: 252 us
  waiting for transfers between devices  129 us (51%)
  starting transfers between devices  89.9 us (35%)
  Pallas kernels  26.2 us (10%)
  local copies, waits for them, and re-layouts  4.49 us (2%)
    ppermute x61, waiting for transfers between devices, send(): return lax.ppermute(value, AXES, pairs)  129 us
    ppermute x61, starting transfers between devices, send(): return lax.ppermute(value, AXES, pairs)  89.9 us
    pallas_call x25, Pallas kernels, vmem_call(): pl.pallas_call(kernel, in_specs=[smem if a.dtype == jnp.int32 else vmem f...  26.2 us
  transfers between devices with their start and end apart: 61, of which 48 were waited for; matrix products, arithmetic and copies ran while one was open for 1% of the time, Pallas kernels for 1%

commit v1 on v0

--- a/solution.py
+++ b/solution.py
@@ -125,7 +125,7 @@
 def updated(place_ref, probe_ref, obj_ref, parts, store):
     gl, gr, rl, rr, rt, rb = parts
     step = step_of(probe_ref)
-    s, t = place_ref[1], place_ref[2]
+    s, t = place_ref[0], place_ref[1]
     row_lo = jnp.where(s == 0, HALO, 0)
     row_hi = jnp.where(s == STRIPES - 1, HALO + PW, EXT)
     col_lo = jnp.where(t == 0, HALO, 0)
@@ -149,15 +149,15 @@
                 store(ch, block, side, obj_ref[ch, span, cols] - factor * g)
 
 
-def new_probe(place_ref, probe_ref, near_ref, far_ref, total_ref, out_ref):
-    c, x, y = place_ref[3], place_ref[4], place_ref[5]
+def new_probe(place_ref, probe_ref, sums, total_ref, out_ref):
+    c, x, y = place_ref[2], place_ref[3], place_ref[4]
     for k in range(4):
         for j in range(4):
             block = (x ^ k) * 4 + (y ^ j)
-            for half, ref in ((c, near_ref), (1 - c, far_ref)):
+            for half, ref in ((c, sums[k]), (1 - c, sums[4 + k])):
                 row = pl.multiple_of((half * 16 + block) * 8, 8)
                 for ch in range(3):
-                    total_ref[ch, pl.ds(row, 8), :] = ref[k * 4 + j, ch * 8 : ch * 8 + 8, :]
+                    total_ref[ch, pl.ds(row, 8), :] = ref[j, ch * 8 : ch * 8 + 8, :]
     scale = 0.5 / (total_ref[2] + 1.0)
     for ch in range(2):
         out_ref[ch] = probe_ref[ch] - total_ref[ch] * scale
@@ -180,9 +180,11 @@
     return jnp.where(row >= shift, below, above).reshape(PW + 8, value.shape[1])
 
 
-def patterns(place_ref, obj_ref, probe_ref, amp_ref, fwd_ref, inv_ref, gl_ref, gr_ref, pg_ref):
+def patterns(offset_ref, obj_ref, probe_ref, amp_ref, fwd_ref, inv_ref, gl_ref, gr_ref, pg_ref):
     fwd, inv = fwd_ref[...], inv_ref[...]
-    third, shift = pl.multiple_of(place_ref[0], 8), place_ref[6]
+    offset = offset_ref[0, 2] + HALO
+    third = pl.multiple_of(jnp.minimum(lax.shift_right_logical(offset, 3), 15) * 8, 8)
+    shift = offset - third
     for p in range(PAT_DEV):
         if p < 2:
             rows = pl.ds((0, 2 * HALO)[p], PW)
@@ -224,7 +226,7 @@
 
 
 def split_probe_grad(place_ref, pg_ref, keep_ref, send_ref):
-    c, x, y = place_ref[3], place_ref[4], place_ref[5]
+    c, x, y = place_ref[2], place_ref[3], place_ref[4]
     for k in range(4):
         for j in range(4):
             block = (x ^ k) * 4 + (y ^ j)
@@ -236,11 +238,10 @@
 
 def pass_kernel(first, last_inner, fresh_probe, *refs):
     refs = list(refs)
-    place_ref = refs.pop(0)
-    obj_ref = refs.pop(0)
+    place_ref, offset_ref, obj_ref = [refs.pop(0) for _ in range(3)]
     parts = None if first else [refs.pop(0) for _ in range(6)]
     probe_ref = refs.pop(0)
-    sums = [refs.pop(0) for _ in range(2)] if fresh_probe else None
+    sums = [refs.pop(0) for _ in range(8)] if fresh_probe else None
     amp_ref, fwd_ref, inv_ref = [refs.pop(0) for _ in range(3)]
     gl_ref, gr_ref = [refs.pop(0) for _ in range(2)]
     if not first:
@@ -257,17 +258,17 @@
     if last_inner:
         keep_ref, send_ref = [refs.pop(0) for _ in range(2)]
     if fresh_probe:
-        new_probe(place_ref, probe_ref, sums[0], sums[1], refs[-1], fresh_ref)
+        new_probe(place_ref, probe_ref, sums, refs[-1], fresh_ref)
         probe_ref = fresh_ref
     pg_ref = refs[-1] if last_inner else None
-    patterns(place_ref, obj_ref, probe_ref, amp_ref, fwd_ref, inv_ref, gl_ref, gr_ref, pg_ref)
+    patterns(offset_ref, obj_ref, probe_ref, amp_ref, fwd_ref, inv_ref, gl_ref, gr_ref, pg_ref)
     if last_inner:
         split_probe_grad(place_ref, pg_ref, keep_ref, send_ref)
 
 
-def run_pass(where, obj, parts, probe, sums, amp, tables, last_inner):
+def run_pass(where, offsets, obj, parts, probe, sums, amp, tables, last_inner):
     first, fresh = parts is None, sums is not None
-    args = [where, obj] + ([] if first else list(parts)) + [probe]
+    args = [where, offsets, obj] + ([] if first else list(parts)) + [probe]
     args += (list(sums) if fresh else []) + [amp, *tables]
     outs = [(2, EXT, LANES)] * 2
     outs += [] if first else [(2, EXT, PW)]
@@ -291,8 +292,9 @@
     middle_ref[...] = out_ref[:, HALO : HALO + PW, HALO : HALO + TILE_W]
 
 
-def probe_kernel(place_ref, probe_ref, near_ref, far_ref, out_ref, total_ref):
-    new_probe(place_ref, probe_ref, near_ref, far_ref, total_ref, out_ref)
+def last_kernel(place_ref, probe_ref, object_ref, *refs):
+    new_probe(place_ref, probe_ref, refs[:8], refs[10], refs[8])
+    refs[9][...] = object_ref[...]
 
 
 def exchange_columns(gl, gr):
@@ -301,7 +303,7 @@
 
 def exchange_rows(where, gl, gr, rl, rr):
     def edges(place_ref, gl, gr, rl, rr, top, bottom):
-        t = place_ref[2]
+        t = place_ref[1]
         halves = (slice(0, LANES), gl, rl, t == 0), (slice(LANES, PW), gr, rr, t == TILES - 1)
         for ch in range(2):
             for cols, a, b, end in halves:
@@ -368,10 +370,10 @@
     far = send(value, far_z())
     above, below = send(value, along_z(2)), send(value, along_z(-2))
     value = add_pairs(value, far, above, below)
-    value, object_out = lax.optimization_barrier((value, object_out))
     value = join(value, *[send(value, along_y(k)) for k in (1, 2, 3)])
-    value = join(value, *[send(value, along_x(k)) for k in (1, 2, 3)])
-    return obj, object_out, value, send(value, core_swap())
+    near = [value] + [send(value, along_x(k)) for k in (1, 2, 3)]
+    near[3], object_out = lax.optimization_barrier((near[3], object_out))
+    return obj, object_out, near + [send(part, core_swap()) for part in near]
 
 
 def first_windows(current, s, t):
@@ -398,25 +400,26 @@
     s, t = z * 4 + x, y * 2 + core
     current = send(object_field, to_host())
     amp = send(amplitudes[0], to_host())
-    offset = send(row_offsets, to_host())[0, 2] + HALO
+    offsets = send(row_offsets, to_host())
     obj = first_windows(current, s, t)
-    third = jnp.minimum(offset // 8, 15) * 8
-    where = jnp.stack([third, s, t, core, x, y, offset - third]).astype(jnp.int32)
+    where = jnp.stack([s, t, core, x, y]).astype(jnp.int32)
 
     def outer(unused, state):
-        obj, unused, probe, near, far = state
-        sums = (near, far)
-        gl, gr, obj, probe, _ = run_pass(where, obj, None, probe, sums, amp, tables, False)
+        obj, unused, probe, sums = state
+        first = run_pass(where, offsets, obj, None, probe, sums, amp, tables, False)
+        gl, gr, obj, probe, _ = first
         parts = exchange(where, gl, gr)
-        gl, gr, obj, probe, rest = run_pass(where, obj, parts, probe, None, amp, tables, True)
-        obj, object_out, near, far = exchange_and_total(where, obj, probe, gl, gr, *rest)
-        return obj, object_out, probe, near, far
-
-    none = jnp.zeros((16, 24, PW), F32)
-    state = (obj, jnp.zeros_like(object_field), probe_field, none, none)
-    obj, object_out, probe, near, far = lax.fori_loop(0, OUTER, outer, state)
-    scratch, args = [pltpu.VMEM((3, PW, PW), F32)], (where, probe, near, far)
-    probe_out = vmem_call(probe_kernel, [(2, PW, PW)], scratch, *args, held=False)[0]
+        second = run_pass(where, offsets, obj, parts, probe, None, amp, tables, True)
+        gl, gr, obj, probe, rest = second
+        obj, object_out, sums = exchange_and_total(where, obj, probe, gl, gr, *rest)
+        return obj, object_out, probe, sums
+
+    none = [jnp.zeros((4, 24, PW), F32) for _ in range(8)]
+    state = (obj, jnp.zeros_like(object_field), probe_field, none)
+    obj, object_out, probe, sums = lax.fori_loop(0, OUTER, outer, state)
+    scratch, args = [pltpu.VMEM((3, PW, PW), F32)], (where, probe, object_out, *sums)
+    outs = [(2, PW, PW), (2, PW, TILE_W)]
+    probe_out, object_out = vmem_call(last_kernel, outs, scratch, *args, held=False)
     return object_out, probe_out
 
 

time: 254 us -> 233 us (0.917)
  waiting for transfers between devices: 129 us -> 97.1 us
  starting transfers between devices: 89.9 us -> 99.3 us
    ppermute x61 -> x67, waiting for transfers between devices: 129 us -> 97.1 us  [send(): return lax.ppermute(value, AXES, pairs)]
    ppermute x61 -> x67, starting transfers between devices: 89.9 us -> 99.3 us  [send(): return lax.ppermute(value, AXES, pairs)]
    another operation x1 -> x9, local copies, waits for them, and re-layouts: 0.09 us -> 2.68 us  [per_device(): jnp.stack([third, s, t, core, x, y, offset - third]).astype(jnp.int32)]
    pallas_call x25 -> x23, Pallas kernels: 26.2 us -> 26.2 us  [vmem_call(): pl.pallas_call(kernel, in_specs=[smem if a.dtype == jnp.int32 else vmem f...]
  transfers between devices with their start and end apart: 61 -> 67, of which waited for: 48 -> 43; matrix products, arithmetic and copies ran while one was open for 1% -> 0% of each run, Pallas kernels for 1% -> 2%
where the time goes in v1:
time: 233 us; the launch traced here: 229 us
  starting transfers between devices  99.3 us (43%)
  waiting for transfers between devices  97.1 us (42%)
  Pallas kernels  26.2 us (11%)
  local copies, waits for them, and re-layouts  4.58 us (2%)
    ppermute x67, starting transfers between devices, send(): return lax.ppermute(value, AXES, pairs)  99.3 us
    ppermute x67, waiting for transfers between devices, send(): return lax.ppermute(value, AXES, pairs)  97.1 us
    pallas_call x23, Pallas kernels, vmem_call(): pl.pallas_call(kernel, in_specs=[smem if a.dtype == jnp.int32 else vmem f...  26.2 us
  transfers between devices with their start and end apart: 67, of which 43 were waited for; matrix products, arithmetic and copies ran while one was open for 0% of the time, Pallas kernels for 2%

profile of v1, /device:TPU:2, one launch (start us, length us, event | category | flops | bytes accessed | tf_op | source)
XLA Modules:
  0.0 229.1 jit_solution(10614247481989243679)
XLA Ops:
  1.6 3.4 %collective-permute-start.30 = (f32[2,256,128]{2,1,0:T(8,128)S(1)}, f32[2,256,128]{2,1,0:T(8,128)S(1)}, u32[]{:S(2)}, u32[]{:S(2)}) collective-permute-start(f32[2,256,128]{2,1,0:T(8,128)S(1)} %copy-done.3), channel_id=1, source_target_pairs={{0,0},{1,8},{2,2},{3,10},{4,4},{5,12},{6,6},{7,14},{8,16},{9,24},{... | collective-permute-start | bytes 786440 | tf_op jit(solution)/shard_map/ppermute | solution.py:87
  5.0 4.3 %collective-permute-done.30 = f32[2,256,128]{2,1,0:T(8,128)S(1)} collective-permute-done((f32[2,256,128]{2,1,0:T(8,128)S(1)}, f32[2,256,128]{2,1,0:T(8,128)S(1)}, u32[]{:S(2)}, u32[]{:S(2)}) %collective-permute-start.30) | collective-permute-done | bytes 262176 | tf_op jit(solution)/shard_map/ppermute | solution.py:87
  11.9 3.8 %collective-permute-start.36 = (f32[3,256,256]{2,1,0:T(8,128)}, f32[3,256,256]{2,1,0:T(8,128)S(1)}, u32[]{:S(2)}, u32[]{:S(2)}) collective-permute-start(f32[3,256,256]{2,1,0:T(8,128)} %bitcast.5), channel_id=1, source_target_pairs={{0,0},{1,8},{2,2},{3,10},{4,4},{5,12},{6,6},{7,14},{8,16},{9,24},{... | collective-permute-start | bytes 2359304 | tf_op jit(solution)/shard_map/ppermute | solution.py:87
  15.9 5.5 %collective-permute-done.31 = f32[2,128,128]{2,1,0:T(8,128)S(1)} collective-permute-done((f32[2,128,128]{2,1,0:T(8,128)S(1)}, f32[2,128,128]{2,1,0:T(8,128)S(1)}, u32[]{:S(2)}, u32[]{:S(2)}) %collective-permute-start.31) | collective-permute-done | bytes 131104 | tf_op jit(solution)/shard_map/ppermute | solution.py:87
  24.7 3.5 %collective-permute-done.33 = f32[2,64,256]{2,1,0:T(8,128)S(1)} collective-permute-done((f32[2,64,256]{2,1,0:T(8,128)S(1)}, f32[2,64,256]{2,1,0:T(8,128)S(1)}, u32[]{:S(2)}, u32[]{:S(2)}) %collective-permute-start.33) | collective-permute-done | bytes 131104 | tf_op jit(solution)/shard_map/ppermute | solution.py:87
  32.5 194.5 %while.31 = (s32[]{:T(128)}, f32[2,384,256]{2,1,0:T(8,128)S(1)}, f32[2,256,128]{2,1,0:T(8,128)}, f32[2,256,256]{2,1,0:T(8,128)S(1)}, f32[4,24,256]{2,1,0:T(8,128...) while((s32[]{:T(128)}, f32[2,384,256]{2,1,0:T(8,128)S(1)}, ...), condition=%wide.region_1.2_spmd.clone, body=%wide.region_0.1_spmd.sunk.clone.sunk | while | flops 2 | bytes 19072340 | solution.py:419
  32.7 4.5 %eval_jaxpr.11 = (f32[2,384,128]{2,1,0:T(8,128)S(1)}, f32[2,384,128]{2,1,0:T(8,128)S(1)}, f32[2,256,256]{2,1,0:T(8,128)S(1)}) custom-call(s32[5]{0:T(128)S(1)} %get-tuple-element.458.refs_0_.place_ref, s32[1,3]{1,0:T(1,128)S(1)} %get-tuple-element.459.refs_1_, f32[2,384,256]{2,1,0:T(8,128)S(1)} %get-tuple-element.429.refs_2_, ...), custom_call_target="tpu_custom_call" | custom-call | tf_op jit(solution)/shard_map/while/body/eval_jaxpr/pallas_call | solution.py:106
  39.2 5.3 %collective-permute-done.1.rr.refs_6_ = f32[2,384,128]{2,1,0:T(8,128)S(1)} collective-permute-done((f32[2,384,128]{2,1,0:T(8,128)S(1)}, f32[2,384,128]{2,1,0:T(8,128)S(1)}, u32[]{:S(2)}, u32[]{:S(2)}) %collective-permute-start.1) | collective-permute-done | bytes 393248 | tf_op jit(solution)/shard_map/while/body/eval_jaxpr/ppermute | solution.py:87
  44.5 3.1 %collective-permute-done.rl.refs_5_ = f32[2,384,128]{2,1,0:T(8,128)S(1)} collective-permute-done((f32[2,384,128]{2,1,0:T(8,128)S(1)}, f32[2,384,128]{2,1,0:T(8,128)S(1)}, u32[]{:S(2)}, u32[]{:S(2)}) %collective-permute-start) | collective-permute-done | bytes 393248 | tf_op jit(solution)/shard_map/while/body/eval_jaxpr/ppermute | solution.py:87
  50.4 5.2 %collective-permute-done.2.refs_7_ = f32[2,128,256]{2,1,0:T(8,128)S(1)} collective-permute-done((f32[2,128,256]{2,1,0:T(8,128)S(1)}, f32[2,128,256]{2,1,0:T(8,128)S(1)}, u32[]{:S(2)}, u32[]{:S(2)}) %collective-permute-start.2) | collective-permute-done | bytes 262176 | tf_op jit(solution)/shard_map/while/body/eval_jaxpr/ppermute | solution.py:87
  56.3 4.6 %eval_jaxpr.13 = (f32[2,384,128]{2,1,0:T(8,128)S(1)}, f32[2,384,128]{2,1,0:T(8,128)S(1)}, f32[2,384,256]{2,1,0:T(8,128)S(1)}, f32[16,24,256]{2,1,0:T(8,128)S(1)}, f32[16,24,256]{2,1,0:T(8,128)S(1)}) custom-call(s32[5]{0:T(128)S(1)} %get-tuple-element.458.refs_0_.place_ref, s32[1,3]{1,0:T(1,128)S(1)} %get-tuple-element.459.refs_1_, ...), custom_call_target="tpu_custom_call" | custom-call | tf_op jit(solution)/shard_map/while/body/eval_jaxpr/pallas_call | solution.py:106
  61.5 5.3 %collective-permute-done.5.rr = f32[2,384,128]{2,1,0:T(8,128)S(1)} collective-permute-done((f32[2,384,128]{2,1,0:T(8,128)S(1)}, f32[2,384,128]{2,1,0:T(8,128)S(1)}, u32[]{:S(2)}, u32[]{:S(2)}) %collective-permute-start.5) | collective-permute-done | bytes 393248 | tf_op jit(solution)/shard_map/while/body/eval_jaxpr/ppermute | solution.py:87
  66.8 3.1 %collective-permute-done.4.rl = f32[2,384,128]{2,1,0:T(8,128)S(1)} collective-permute-done((f32[2,384,128]{2,1,0:T(8,128)S(1)}, f32[2,384,128]{2,1,0:T(8,128)S(1)}, u32[]{:S(2)}, u32[]{:S(2)}) %collective-permute-start.4) | collective-permute-done | bytes 393248 | tf_op jit(solution)/shard_map/while/body/eval_jaxpr/ppermute | solution.py:87
  70.5 3.0 %collective-permute-start.6 = (f32[2,128,256]{2,1,0:T(8,128)S(1)}, f32[2,128,256]{2,1,0:T(8,128)S(1)}, u32[]{:S(2)}, u32[]{:S(2)}) collective-permute-start(f32[2,128,256]{2,1,0:T(8,128)S(1)} %get-tuple-element.394), channel_id=1, source_target_pairs={{0,16},{8,24},{2,18},{10,26},{4,20},{12,28},{6,22},{14,30},{16,1},... | collective-permute-start | bytes 786440 | tf_op jit(solution)/shard_map/while/body/eval_jaxpr/ppermute | solution.py:87
  74.7 5.3 %collective-permute-start.9 = (f32[4,24,256]{2,1,0:T(8,128)S(1)}, f32[4,24,256]{2,1,0:T(8,128)S(1)}, u32[]{:S(2)}, u32[]{:S(2)}) collective-permute-start(f32[4,24,256]{2,1,0:T(8,128)S(1)} %get-tuple-element.400), channel_id=1, source_target_pairs={{0,16},{1,17},{2,18},{3,19},{4,20},{5,21},{6,22},{7,23},{8,24},{9,... | collective-permute-start | bytes 294920 | tf_op jit(solution)/shard_map/while/body/eval_jaxpr/ppermute | solution.py:87
  99.5 5.5 %collective-permute-start.18 = (f32[1,24,256]{2,1,0:T(8,128)S(1)}, f32[1,24,256]{2,1,0:T(8,128)S(1)}, u32[]{:S(2)}, u32[]{:S(2)}) collective-permute-start(f32[1,24,256]{2,1,0:T(8,128)S(1)} %eval_jaxpr.19.a), channel_id=1, source_target_pairs={{0,192},{1,193},{2,194},{3,195},{4,196},{5,197},{6,198},{7,199},{8... | collective-permute-start | bytes 73736 | tf_op jit(solution)/shard_map/while/body/eval_jaxpr/ppermute | solution.py:87
  106.1 4.5 %collective-permute-start.16 = (f32[1,24,256]{2,1,0:T(8,128)S(1)}, f32[1,24,256]{2,1,0:T(8,128)S(1)}, u32[]{:S(2)}, u32[]{:S(2)}) collective-permute-start(f32[1,24,256]{2,1,0:T(8,128)S(1)} %eval_jaxpr.19.a), channel_id=1, source_target_pairs={{0,160},{1,161},{2,162},{3,163},{4,164},{5,165},{6,166},{7,167},{8... | collective-permute-start | bytes 73736 | tf_op jit(solution)/shard_map/while/body/eval_jaxpr/ppermute | solution.py:87
  113.5 3.7 %collective-permute-start.19 = (f32[1,24,256]{2,1,0:T(8,128)S(1)}, f32[1,24,256]{2,1,0:T(8,128)S(1)}, u32[]{:S(2)}, u32[]{:S(2)}) collective-permute-start(f32[1,24,256]{2,1,0:T(8,128)S(1)} %eval_jaxpr.20.refs_0_), channel_id=1, source_target_pairs={{0,2},{1,3},{2,0},{3,1},{4,6},{5,7},{6,4},{7,5},{8,10},{9,11},{10,... | collective-permute-start | bytes 73736 | tf_op jit(solution)/shard_map/while/body/eval_jaxpr/ppermute | solution.py:87
  119.9 4.3 %collective-permute-start.25 = (f32[4,24,256]{2,1,0:T(8,128)}, f32[4,24,256]{2,1,0:T(8,128)}, u32[]{:S(2)}, u32[]{:S(2)}) collective-permute-start(f32[4,24,256]{2,1,0:T(8,128)} %eval_jaxpr.21), channel_id=1, source_target_pairs={{0,1},{1,0},{2,3},{3,2},{4,5},{5,4},{6,7},{7,6},{8,9},{9,8},{10,11... | collective-permute-start | bytes 294920 | tf_op jit(solution)/shard_map/while/body/eval_jaxpr/ppermute | solution.py:87
  130.8 4.5 %eval_jaxpr.11 = (f32[2,384,128]{2,1,0:T(8,128)S(1)}, f32[2,384,128]{2,1,0:T(8,128)S(1)}, f32[2,256,256]{2,1,0:T(8,128)S(1)}) custom-call(s32[5]{0:T(128)S(1)} %get-tuple-element.458.refs_0_.place_ref, s32[1,3]{1,0:T(1,128)S(1)} %get-tuple-element.459.refs_1_, f32[2,384,256]{2,1,0:T(8,128)S(1)} %get-tuple-element.429.refs_2_, ...), custom_call_target="tpu_custom_call" | custom-call | tf_op jit(solution)/shard_map/while/body/eval_jaxpr/pallas_call | solution.py:106
  137.7 5.3 %collective-permute-done.1.rr.refs_6_ = f32[2,384,128]{2,1,0:T(8,128)S(1)} collective-permute-done((f32[2,384,128]{2,1,0:T(8,128)S(1)}, f32[2,384,128]{2,1,0:T(8,128)S(1)}, u32[]{:S(2)}, u32[]{:S(2)}) %collective-permute-start.1) | collective-permute-done | bytes 393248 | tf_op jit(solution)/shard_map/while/body/eval_jaxpr/ppermute | solution.py:87
  143.0 3.1 %collective-permute-done.rl.refs_5_ = f32[2,384,128]{2,1,0:T(8,128)S(1)} collective-permute-done((f32[2,384,128]{2,1,0:T(8,128)S(1)}, f32[2,384,128]{2,1,0:T(8,128)S(1)}, u32[]{:S(2)}, u32[]{:S(2)}) %collective-permute-start) | collective-permute-done | bytes 393248 | tf_op jit(solution)/shard_map/while/body/eval_jaxpr/ppermute | solution.py:87
  147.0 2.8 %collective-permute-start.3 = (f32[2,128,256]{2,1,0:T(8,128)S(1)}, f32[2,128,256]{2,1,0:T(8,128)S(1)}, u32[]{:S(2)}, u32[]{:S(2)}) collective-permute-start(f32[2,128,256]{2,1,0:T(8,128)S(1)} %get-tuple-element.389), channel_id=1, source_target_pairs={{0,241},{8,249},{2,243},{10,251},{4,245},{12,253},{6,247},{14,255}... | collective-permute-start | bytes 786440 | tf_op jit(solution)/shard_map/while/body/eval_jaxpr/ppermute | solution.py:87
  149.8 4.3 %collective-permute-done.2.refs_7_ = f32[2,128,256]{2,1,0:T(8,128)S(1)} collective-permute-done((f32[2,128,256]{2,1,0:T(8,128)S(1)}, f32[2,128,256]{2,1,0:T(8,128)S(1)}, u32[]{:S(2)}, u32[]{:S(2)}) %collective-permute-start.2) | collective-permute-done | bytes 262176 | tf_op jit(solution)/shard_map/while/body/eval_jaxpr/ppermute | solution.py:87
  154.0 4.6 %eval_jaxpr.13 = (f32[2,384,128]{2,1,0:T(8,128)S(1)}, f32[2,384,128]{2,1,0:T(8,128)S(1)}, f32[2,384,256]{2,1,0:T(8,128)S(1)}, f32[16,24,256]{2,1,0:T(8,128)S(1)}, f32[16,24,256]{2,1,0:T(8,128)S(1)}) custom-call(s32[5]{0:T(128)S(1)} %get-tuple-element.458.refs_0_.place_ref, s32[1,3]{1,0:T(1,128)S(1)} %get-tuple-element.459.refs_1_, ...), custom_call_target="tpu_custom_call" | custom-call | tf_op jit(solution)/shard_map/while/body/eval_jaxpr/pallas_call | solution.py:106
  160.0 5.3 %collective-permute-done.5.rr = f32[2,384,128]{2,1,0:T(8,128)S(1)} collective-permute-done((f32[2,384,128]{2,1,0:T(8,128)S(1)}, f32[2,384,128]{2,1,0:T(8,128)S(1)}, u32[]{:S(2)}, u32[]{:S(2)}) %collective-permute-start.5) | collective-permute-done | bytes 393248 | tf_op jit(solution)/shard_map/while/body/eval_jaxpr/ppermute | solution.py:87
  165.2 3.1 %collective-permute-done.4.rl = f32[2,384,128]{2,1,0:T(8,128)S(1)} collective-permute-done((f32[2,384,128]{2,1,0:T(8,128)S(1)}, f32[2,384,128]{2,1,0:T(8,128)S(1)}, u32[]{:S(2)}, u32[]{:S(2)}) %collective-permute-start.4) | collective-permute-done | bytes 393248 | tf_op jit(solution)/shard_map/while/body/eval_jaxpr/ppermute | solution.py:87
  169.0 3.9 %collective-permute-start.6 = (f32[2,128,256]{2,1,0:T(8,128)S(1)}, f32[2,128,256]{2,1,0:T(8,128)S(1)}, u32[]{:S(2)}, u32[]{:S(2)}) collective-permute-start(f32[2,128,256]{2,1,0:T(8,128)S(1)} %get-tuple-element.394), channel_id=1, source_target_pairs={{0,16},{8,24},{2,18},{10,26},{4,20},{12,28},{6,22},{14,30},{16,1},... | collective-permute-start | bytes 786440 | tf_op jit(solution)/shard_map/while/body/eval_jaxpr/ppermute | solution.py:87
  174.5 5.6 %collective-permute-start.9 = (f32[4,24,256]{2,1,0:T(8,128)S(1)}, f32[4,24,256]{2,1,0:T(8,128)S(1)}, u32[]{:S(2)}, u32[]{:S(2)}) collective-permute-start(f32[4,24,256]{2,1,0:T(8,128)S(1)} %get-tuple-element.400), channel_id=1, source_target_pairs={{0,16},{1,17},{2,18},{3,19},{4,20},{5,21},{6,22},{7,23},{8,24},{9,... | collective-permute-start | bytes 294920 | tf_op jit(solution)/shard_map/while/body/eval_jaxpr/ppermute | solution.py:87
  186.4 5.4 %collective-permute-start.13 = (f32[1,24,256]{2,1,0:T(8,128)S(1)}, f32[1,24,256]{2,1,0:T(8,128)S(1)}, u32[]{:S(2)}, u32[]{:S(2)}) collective-permute-start(f32[1,24,256]{2,1,0:T(8,128)S(1)} %get-tuple-element.405), channel_id=1, source_target_pairs={{0,4},{1,5},{2,6},{3,7},{4,0},{5,1},{6,2},{7,3},{8,12},{9,13},{10,... | collective-permute-start | bytes 73736 | tf_op jit(solution)/shard_map/while/body/eval_jaxpr/ppermute | solution.py:87
  193.8 3.0 %collective-permute-done.14.refs_3_ = f32[1,24,256]{2,1,0:T(8,128)S(1)} collective-permute-done((f32[1,24,256]{2,1,0:T(8,128)S(1)}, f32[1,24,256]{2,1,0:T(8,128)S(1)}, u32[]{:S(2)}, u32[]{:S(2)}) %collective-permute-start.14) | collective-permute-done | bytes 24608 | tf_op jit(solution)/shard_map/while/body/eval_jaxpr/ppermute | solution.py:87
  211.3 3.6 %collective-permute-start.19 = (f32[1,24,256]{2,1,0:T(8,128)S(1)}, f32[1,24,256]{2,1,0:T(8,128)S(1)}, u32[]{:S(2)}, u32[]{:S(2)}) collective-permute-start(f32[1,24,256]{2,1,0:T(8,128)S(1)} %eval_jaxpr.20.refs_0_), channel_id=1, source_target_pairs={{0,2},{1,3},{2,0},{3,1},{4,6},{5,7},{6,4},{7,5},{8,10},{9,11},{10,... | collective-permute-start | bytes 73736 | tf_op jit(solution)/shard_map/while/body/eval_jaxpr/ppermute | solution.py:87
  (158 shorter events, 95.6 us)
Async XLA Ops:
  1.6 7.7 %collective-permute-start.30 = (f32[2,256,128]{2,1,0:T(8,128)S(1)}, f32[2,256,128]{2,1,0:T(8,128)S(1)}, u32[]{:S(2)}, u32[]{:S(2)}) collective-permute-start(f32[2,256,128]{2,1,0:T(8,128)S(1)} %copy-done.3), channel_id=1, source_target_pairs={{0,0},{1,8},{2,2},{3,10},{4,4},{5,12},{6,6},{7,14},{8,16},{9,24},{... | collective-permute-start | bytes 786440 | tf_op jit(solution)/shard_map/ppermute | solution.py:87
  11.9 17.9 %collective-permute-start.36 = (f32[3,256,256]{2,1,0:T(8,128)}, f32[3,256,256]{2,1,0:T(8,128)S(1)}, u32[]{:S(2)}, u32[]{:S(2)}) collective-permute-start(f32[3,256,256]{2,1,0:T(8,128)} %bitcast.5), channel_id=1, source_target_pairs={{0,0},{1,8},{2,2},{3,10},{4,4},{5,12},{6,6},{7,14},{8,16},{9,24},{... | collective-permute-start | bytes 2359304 | tf_op jit(solution)/shard_map/ppermute | solution.py:87
  22.4 7.4 %collective-permute-start.35 = (s32[1,3]{1,0:T(1,128)S(1)}, s32[1,3]{1,0:T(1,128)S(1)}, u32[]{:S(2)}, u32[]{:S(2)}) collective-permute-start(s32[1,3]{1,0:T(1,128)S(1)} %copy-done.4), channel_id=1, source_target_pairs={{0,0},{1,8},{2,2},{3,10},{4,4},{5,12},{6,6},{7,14},{8,16},{9,24},{... | collective-permute-start | bytes 44 | tf_op jit(solution)/shard_map/ppermute | solution.py:87
  37.2 7.4 %collective-permute-start.1 = (f32[2,384,128]{2,1,0:T(8,128)S(1)}, f32[2,384,128]{2,1,0:T(8,128)S(1)}, u32[]{:S(2)}, u32[]{:S(2)}) collective-permute-start(f32[2,384,128]{2,1,0:T(8,128)S(1)} %get-tuple-element.386.gl.refs_3_), channel_id=1, source_target_pairs={{0,14},{8,0},{2,8},{10,2},{4,10},{12,4},{6,12},{14,6},{16,30},{24,... | collective-permute-start | bytes 1179656 | tf_op jit(solution)/shard_map/while/body/eval_jaxpr/ppermute | solution.py:87
  39.2 8.4 %collective-permute-start = (f32[2,384,128]{2,1,0:T(8,128)S(1)}, f32[2,384,128]{2,1,0:T(8,128)S(1)}, u32[]{:S(2)}, u32[]{:S(2)}) collective-permute-start(f32[2,384,128]{2,1,0:T(8,128)S(1)} %get-tuple-element.387.gr.refs_4_), channel_id=1, source_target_pairs={{0,8},{8,2},{2,10},{10,4},{4,12},{12,6},{6,14},{14,0},{16,24},{24,... | collective-permute-start | bytes 1179656 | tf_op jit(solution)/shard_map/while/body/eval_jaxpr/ppermute | solution.py:87
  48.3 7.3 %collective-permute-start.2 = (f32[2,128,256]{2,1,0:T(8,128)S(1)}, f32[2,128,256]{2,1,0:T(8,128)S(1)}, u32[]{:S(2)}, u32[]{:S(2)}) collective-permute-start(f32[2,128,256]{2,1,0:T(8,128)S(1)} %get-tuple-element.388), channel_id=1, source_target_pairs={{0,16},{8,24},{2,18},{10,26},{4,20},{12,28},{6,22},{14,30},{16,1},... | collective-permute-start | bytes 786440 | tf_op jit(solution)/shard_map/while/body/eval_jaxpr/ppermute | solution.py:87
  48.3 8.0 %collective-permute-start.3 = (f32[2,128,256]{2,1,0:T(8,128)S(1)}, f32[2,128,256]{2,1,0:T(8,128)S(1)}, u32[]{:S(2)}, u32[]{:S(2)}) collective-permute-start(f32[2,128,256]{2,1,0:T(8,128)S(1)} %get-tuple-element.389), channel_id=1, source_target_pairs={{0,241},{8,249},{2,243},{10,251},{4,245},{12,253},{6,247},{14,255}... | collective-permute-start | bytes 786440 | tf_op jit(solution)/shard_map/while/body/eval_jaxpr/ppermute | solution.py:87
  61.5 8.4 %collective-permute-start.4 = (f32[2,384,128]{2,1,0:T(8,128)S(1)}, f32[2,384,128]{2,1,0:T(8,128)S(1)}, u32[]{:S(2)}, u32[]{:S(2)}) collective-permute-start(f32[2,384,128]{2,1,0:T(8,128)S(1)} %get-tuple-element.393.gr), channel_id=1, source_target_pairs={{0,8},{8,2},{2,10},{10,4},{4,12},{12,6},{6,14},{14,0},{16,24},{24,... | collective-permute-start | bytes 1179656 | tf_op jit(solution)/shard_map/while/body/eval_jaxpr/ppermute | solution.py:87
  61.5 13.1 %collective-permute-start.8 = (f32[16,24,256]{2,1,0:T(8,128)S(1)}, f32[16,24,256]{2,1,0:T(8,128)S(1)}, u32[]{:S(2)}, u32[]{:S(2)}) collective-permute-start(f32[16,24,256]{2,1,0:T(8,128)S(1)} %get-tuple-element.398), channel_id=1, source_target_pairs={{0,8},{1,9},{2,10},{3,11},{4,12},{5,13},{6,14},{7,15},{8,0},{9,1},... | collective-permute-start | bytes 1179656 | tf_op jit(solution)/shard_map/while/body/eval_jaxpr/ppermute | solution.py:87
  70.5 11.0 %collective-permute-start.6 = (f32[2,128,256]{2,1,0:T(8,128)S(1)}, f32[2,128,256]{2,1,0:T(8,128)S(1)}, u32[]{:S(2)}, u32[]{:S(2)}) collective-permute-start(f32[2,128,256]{2,1,0:T(8,128)S(1)} %get-tuple-element.394), channel_id=1, source_target_pairs={{0,16},{8,24},{2,18},{10,26},{4,20},{12,28},{6,22},{14,30},{16,1},... | collective-permute-start | bytes 786440 | tf_op jit(solution)/shard_map/while/body/eval_jaxpr/ppermute | solution.py:87
  73.6 10.6 %collective-permute-start.7 = (f32[2,128,256]{2,1,0:T(8,128)S(1)}, f32[2,128,256]{2,1,0:T(8,128)S(1)}, u32[]{:S(2)}, u32[]{:S(2)}) collective-permute-start(f32[2,128,256]{2,1,0:T(8,128)S(1)} %get-tuple-element.395), channel_id=1, source_target_pairs={{0,241},{8,249},{2,243},{10,251},{4,245},{12,253},{6,247},{14,255}... | collective-permute-start | bytes 786440 | tf_op jit(solution)/shard_map/while/body/eval_jaxpr/ppermute | solution.py:87
  74.7 12.4 %collective-permute-start.9 = (f32[4,24,256]{2,1,0:T(8,128)S(1)}, f32[4,24,256]{2,1,0:T(8,128)S(1)}, u32[]{:S(2)}, u32[]{:S(2)}) collective-permute-start(f32[4,24,256]{2,1,0:T(8,128)S(1)} %get-tuple-element.400), channel_id=1, source_target_pairs={{0,16},{1,17},{2,18},{3,19},{4,20},{5,21},{6,22},{7,23},{8,24},{9,... | collective-permute-start | bytes 294920 | tf_op jit(solution)/shard_map/while/body/eval_jaxpr/ppermute | solution.py:87
  80.0 7.1 %collective-permute-start.10 = (f32[4,24,256]{2,1,0:T(8,128)S(1)}, f32[4,24,256]{2,1,0:T(8,128)S(1)}, u32[]{:S(2)}, u32[]{:S(2)}) collective-permute-start(f32[4,24,256]{2,1,0:T(8,128)S(1)} %get-tuple-element.401), channel_id=1, source_target_pairs={{0,1},{1,0},{2,3},{3,2},{4,5},{5,4},{6,7},{7,6},{8,9},{9,8},{10,11... | collective-permute-start | bytes 294920 | tf_op jit(solution)/shard_map/while/body/eval_jaxpr/ppermute | solution.py:87
  80.0 7.1 %collective-permute-start.11 = (f32[4,24,256]{2,1,0:T(8,128)S(1)}, f32[4,24,256]{2,1,0:T(8,128)S(1)}, u32[]{:S(2)}, u32[]{:S(2)}) collective-permute-start(f32[4,24,256]{2,1,0:T(8,128)S(1)} %get-tuple-element.402), channel_id=1, source_target_pairs={{0,17},{1,16},{2,19},{3,18},{4,21},{5,20},{6,23},{7,22},{8,25},{9,... | collective-permute-start | bytes 294920 | tf_op jit(solution)/shard_map/while/body/eval_jaxpr/ppermute | solution.py:87
  85.1 44.0 %collective-permute-start.23 = (f32[2,256,128]{2,1,0:T(8,128)S(1)}, f32[2,256,128]{2,1,0:T(8,128)}, u32[]{:S(2)}, u32[]{:S(2)}) collective-permute-start(f32[2,256,128]{2,1,0:T(8,128)S(1)} %get-tuple-element.407), channel_id=1, source_target_pairs={{0,0},{8,1},{2,2},{10,3},{4,4},{12,5},{6,6},{14,7},{16,8},{24,9},{... | collective-permute-start | bytes 786440 | tf_op jit(solution)/shard_map/while/body/eval_jaxpr/ppermute | solution.py:87
  99.5 11.2 %collective-permute-start.18 = (f32[1,24,256]{2,1,0:T(8,128)S(1)}, f32[1,24,256]{2,1,0:T(8,128)S(1)}, u32[]{:S(2)}, u32[]{:S(2)}) collective-permute-start(f32[1,24,256]{2,1,0:T(8,128)S(1)} %eval_jaxpr.19.a), channel_id=1, source_target_pairs={{0,192},{1,193},{2,194},{3,195},{4,196},{5,197},{6,198},{7,199},{8... | collective-permute-start | bytes 73736 | tf_op jit(solution)/shard_map/while/body/eval_jaxpr/ppermute | solution.py:87
  105.0 6.6 %collective-permute-start.17 = (f32[1,24,256]{2,1,0:T(8,128)S(1)}, f32[1,24,256]{2,1,0:T(8,128)S(1)}, u32[]{:S(2)}, u32[]{:S(2)}) collective-permute-start(f32[1,24,256]{2,1,0:T(8,128)S(1)} %eval_jaxpr.19.a), channel_id=1, source_target_pairs={{0,64},{1,65},{2,66},{3,67},{4,68},{5,69},{6,70},{7,71},{8,72},{9,... | collective-permute-start | bytes 73736 | tf_op jit(solution)/shard_map/while/body/eval_jaxpr/ppermute | solution.py:87
  106.1 6.8 %collective-permute-start.16 = (f32[1,24,256]{2,1,0:T(8,128)S(1)}, f32[1,24,256]{2,1,0:T(8,128)S(1)}, u32[]{:S(2)}, u32[]{:S(2)}) collective-permute-start(f32[1,24,256]{2,1,0:T(8,128)S(1)} %eval_jaxpr.19.a), channel_id=1, source_target_pairs={{0,160},{1,161},{2,162},{3,163},{4,164},{5,165},{6,166},{7,167},{8... | collective-permute-start | bytes 73736 | tf_op jit(solution)/shard_map/while/body/eval_jaxpr/ppermute | solution.py:87
  119.9 7.2 %collective-permute-start.25 = (f32[4,24,256]{2,1,0:T(8,128)}, f32[4,24,256]{2,1,0:T(8,128)}, u32[]{:S(2)}, u32[]{:S(2)}) collective-permute-start(f32[4,24,256]{2,1,0:T(8,128)} %eval_jaxpr.21), channel_id=1, source_target_pairs={{0,1},{1,0},{2,3},{3,2},{4,5},{5,4},{6,7},{7,6},{8,9},{9,8},{10,11... | collective-permute-start | bytes 294920 | tf_op jit(solution)/shard_map/while/body/eval_jaxpr/ppermute | solution.py:87
  135.3 7.7 %collective-permute-start.1 = (f32[2,384,128]{2,1,0:T(8,128)S(1)}, f32[2,384,128]{2,1,0:T(8,128)S(1)}, u32[]{:S(2)}, u32[]{:S(2)}) collective-permute-start(f32[2,384,128]{2,1,0:T(8,128)S(1)} %get-tuple-element.386.gl.refs_3_), channel_id=1, source_target_pairs={{0,14},{8,0},{2,8},{10,2},{4,10},{12,4},{6,12},{14,6},{16,30},{24,... | collective-permute-start | bytes 1179656 | tf_op jit(solution)/shard_map/while/body/eval_jaxpr/ppermute | solution.py:87
  137.7 8.4 %collective-permute-start = (f32[2,384,128]{2,1,0:T(8,128)S(1)}, f32[2,384,128]{2,1,0:T(8,128)S(1)}, u32[]{:S(2)}, u32[]{:S(2)}) collective-permute-start(f32[2,384,128]{2,1,0:T(8,128)S(1)} %get-tuple-element.387.gr.refs_4_), channel_id=1, source_target_pairs={{0,8},{8,2},{2,10},{10,4},{4,12},{12,6},{6,14},{14,0},{16,24},{24,... | collective-permute-start | bytes 1179656 | tf_op jit(solution)/shard_map/while/body/eval_jaxpr/ppermute | solution.py:87
  146.7 7.3 %collective-permute-start.2 = (f32[2,128,256]{2,1,0:T(8,128)S(1)}, f32[2,128,256]{2,1,0:T(8,128)S(1)}, u32[]{:S(2)}, u32[]{:S(2)}) collective-permute-start(f32[2,128,256]{2,1,0:T(8,128)S(1)} %get-tuple-element.388), channel_id=1, source_target_pairs={{0,16},{8,24},{2,18},{10,26},{4,20},{12,28},{6,22},{14,30},{16,1},... | collective-permute-start | bytes 786440 | tf_op jit(solution)/shard_map/while/body/eval_jaxpr/ppermute | solution.py:87
  147.0 7.0 %collective-permute-start.3 = (f32[2,128,256]{2,1,0:T(8,128)S(1)}, f32[2,128,256]{2,1,0:T(8,128)S(1)}, u32[]{:S(2)}, u32[]{:S(2)}) collective-permute-start(f32[2,128,256]{2,1,0:T(8,128)S(1)} %get-tuple-element.389), channel_id=1, source_target_pairs={{0,241},{8,249},{2,243},{10,251},{4,245},{12,253},{6,247},{14,255}... | collective-permute-start | bytes 786440 | tf_op jit(solution)/shard_map/while/body/eval_jaxpr/ppermute | solution.py:87
  158.6 6.6 %collective-permute-start.5 = (f32[2,384,128]{2,1,0:T(8,128)S(1)}, f32[2,384,128]{2,1,0:T(8,128)S(1)}, u32[]{:S(2)}, u32[]{:S(2)}) collective-permute-start(f32[2,384,128]{2,1,0:T(8,128)S(1)} %get-tuple-element.392.gl), channel_id=1, source_target_pairs={{0,14},{8,0},{2,8},{10,2},{4,10},{12,4},{6,12},{14,6},{16,30},{24,... | collective-permute-start | bytes 1179656 | tf_op jit(solution)/shard_map/while/body/eval_jaxpr/ppermute | solution.py:87
  159.9 8.4 %collective-permute-start.4 = (f32[2,384,128]{2,1,0:T(8,128)S(1)}, f32[2,384,128]{2,1,0:T(8,128)S(1)}, u32[]{:S(2)}, u32[]{:S(2)}) collective-permute-start(f32[2,384,128]{2,1,0:T(8,128)S(1)} %get-tuple-element.393.gr), channel_id=1, source_target_pairs={{0,8},{8,2},{2,10},{10,4},{4,12},{12,6},{6,14},{14,0},{16,24},{24,... | collective-permute-start | bytes 1179656 | tf_op jit(solution)/shard_map/while/body/eval_jaxpr/ppermute | solution.py:87
  159.9 14.5 %collective-permute-start.8 = (f32[16,24,256]{2,1,0:T(8,128)S(1)}, f32[16,24,256]{2,1,0:T(8,128)S(1)}, u32[]{:S(2)}, u32[]{:S(2)}) collective-permute-start(f32[16,24,256]{2,1,0:T(8,128)S(1)} %get-tuple-element.398), channel_id=1, source_target_pairs={{0,8},{1,9},{2,10},{3,11},{4,12},{5,13},{6,14},{7,15},{8,0},{9,1},... | collective-permute-start | bytes 1179656 | tf_op jit(solution)/shard_map/while/body/eval_jaxpr/ppermute | solution.py:87
  169.0 12.7 %collective-permute-start.6 = (f32[2,128,256]{2,1,0:T(8,128)S(1)}, f32[2,128,256]{2,1,0:T(8,128)S(1)}, u32[]{:S(2)}, u32[]{:S(2)}) collective-permute-start(f32[2,128,256]{2,1,0:T(8,128)S(1)} %get-tuple-element.394), channel_id=1, source_target_pairs={{0,16},{8,24},{2,18},{10,26},{4,20},{12,28},{6,22},{14,30},{16,1},... | collective-permute-start | bytes 786440 | tf_op jit(solution)/shard_map/while/body/eval_jaxpr/ppermute | solution.py:87
  172.9 10.3 %collective-permute-start.7 = (f32[2,128,256]{2,1,0:T(8,128)S(1)}, f32[2,128,256]{2,1,0:T(8,128)S(1)}, u32[]{:S(2)}, u32[]{:S(2)}) collective-permute-start(f32[2,128,256]{2,1,0:T(8,128)S(1)} %get-tuple-element.395), channel_id=1, source_target_pairs={{0,241},{8,249},{2,243},{10,251},{4,245},{12,253},{6,247},{14,255}... | collective-permute-start | bytes 786440 | tf_op jit(solution)/shard_map/while/body/eval_jaxpr/ppermute | solution.py:87
  174.5 11.6 %collective-permute-start.9 = (f32[4,24,256]{2,1,0:T(8,128)S(1)}, f32[4,24,256]{2,1,0:T(8,128)S(1)}, u32[]{:S(2)}, u32[]{:S(2)}) collective-permute-start(f32[4,24,256]{2,1,0:T(8,128)S(1)} %get-tuple-element.400), channel_id=1, source_target_pairs={{0,16},{1,17},{2,18},{3,19},{4,20},{5,21},{6,22},{7,23},{8,24},{9,... | collective-permute-start | bytes 294920 | tf_op jit(solution)/shard_map/while/body/eval_jaxpr/ppermute | solution.py:87
  184.2 41.3 %collective-permute-start.23 = (f32[2,256,128]{2,1,0:T(8,128)S(1)}, f32[2,256,128]{2,1,0:T(8,128)}, u32[]{:S(2)}, u32[]{:S(2)}) collective-permute-start(f32[2,256,128]{2,1,0:T(8,128)S(1)} %get-tuple-element.407), channel_id=1, source_target_pairs={{0,0},{8,1},{2,2},{10,3},{4,4},{12,5},{6,6},{14,7},{16,8},{24,9},{... | collective-permute-start | bytes 786440 | tf_op jit(solution)/shard_map/while/body/eval_jaxpr/ppermute | solution.py:87
  186.4 7.4 %collective-permute-start.13 = (f32[1,24,256]{2,1,0:T(8,128)S(1)}, f32[1,24,256]{2,1,0:T(8,128)S(1)}, u32[]{:S(2)}, u32[]{:S(2)}) collective-permute-start(f32[1,24,256]{2,1,0:T(8,128)S(1)} %get-tuple-element.405), channel_id=1, source_target_pairs={{0,4},{1,5},{2,6},{3,7},{4,0},{5,1},{6,2},{7,3},{8,12},{9,13},{10,... | collective-permute-start | bytes 73736 | tf_op jit(solution)/shard_map/while/body/eval_jaxpr/ppermute | solution.py:87
  203.9 6.8 %collective-permute-start.16 = (f32[1,24,256]{2,1,0:T(8,128)S(1)}, f32[1,24,256]{2,1,0:T(8,128)S(1)}, u32[]{:S(2)}, u32[]{:S(2)}) collective-permute-start(f32[1,24,256]{2,1,0:T(8,128)S(1)} %eval_jaxpr.19.a), channel_id=1, source_target_pairs={{0,160},{1,161},{2,162},{3,163},{4,164},{5,165},{6,166},{7,167},{8... | collective-permute-start | bytes 73736 | tf_op jit(solution)/shard_map/while/body/eval_jaxpr/ppermute | solution.py:87
  (40 other events, 174.3 us)

commit v2 on v1

--- a/solution.py
+++ b/solution.py
@@ -149,18 +149,30 @@
                 store(ch, block, side, obj_ref[ch, span, cols] - factor * g)
 
 
-def new_probe(place_ref, probe_ref, sums, total_ref, out_ref):
-    c, x, y = place_ref[2], place_ref[3], place_ref[4]
+def block_row(place_ref, half, k, j):
+    x, y = place_ref[3], place_ref[4]
+    return pl.multiple_of((half * 16 + (x ^ k) * 4 + (y ^ j)) * 8, 8)
+
+
+def assemble(place_ref, pieces, out_ref):
+    c = place_ref[2]
     for k in range(4):
         for j in range(4):
-            block = (x ^ k) * 4 + (y ^ j)
-            for half, ref in ((c, sums[k]), (1 - c, sums[4 + k])):
-                row = pl.multiple_of((half * 16 + block) * 8, 8)
-                for ch in range(3):
-                    total_ref[ch, pl.ds(row, 8), :] = ref[j, ch * 8 : ch * 8 + 8, :]
-    scale = 0.5 / (total_ref[2] + 1.0)
-    for ch in range(2):
-        out_ref[ch] = probe_ref[ch] - total_ref[ch] * scale
+            for half, ref in ((c, pieces[k]), (1 - c, pieces[4 + k])):
+                row = block_row(place_ref, half, k, j)
+                for ch in range(2):
+                    out_ref[ch, pl.ds(row, 8), :] = ref[j, ch * 8 : ch * 8 + 8, :]
+
+
+def first_pieces(place_ref, probe_ref, *outs):
+    c = place_ref[2]
+    for k in range(4):
+        for j in range(4):
+            for half, ref in ((c, outs[k]), (1 - c, outs[4 + k])):
+                row = block_row(place_ref, half, k, j)
+                for ch in range(2):
+                    ref[j, ch * 8 : ch * 8 + 8, :] = probe_ref[ch, pl.ds(row, 8), :]
+    outs[8][...] = jnp.zeros_like(outs[8])
 
 
 def lifted(value, shift):
@@ -226,26 +238,27 @@
 
 
 def split_probe_grad(place_ref, pg_ref, keep_ref, send_ref):
-    c, x, y = place_ref[2], place_ref[3], place_ref[4]
+    c = place_ref[2]
     for k in range(4):
         for j in range(4):
-            block = (x ^ k) * 4 + (y ^ j)
             for half, ref in ((c, keep_ref), (1 - c, send_ref)):
-                row = pl.multiple_of((half * 16 + block) * 8, 8)
+                row = block_row(place_ref, half, k, j)
                 for ch in range(3):
                     ref[k * 4 + j, ch * 8 : ch * 8 + 8, :] = pg_ref[ch, pl.ds(row, 8), :]
 
 
-def pass_kernel(first, last_inner, fresh_probe, *refs):
+def pass_kernel(last_inner, *refs):
     refs = list(refs)
     place_ref, offset_ref, obj_ref = [refs.pop(0) for _ in range(3)]
-    parts = None if first else [refs.pop(0) for _ in range(6)]
-    probe_ref = refs.pop(0)
-    sums = [refs.pop(0) for _ in range(8)] if fresh_probe else None
+    if last_inner:
+        parts = [refs.pop(0) for _ in range(6)]
+        probe_ref = refs.pop(0)
+    else:
+        pieces = [refs.pop(0) for _ in range(8)]
     amp_ref, fwd_ref, inv_ref = [refs.pop(0) for _ in range(3)]
     gl_ref, gr_ref = [refs.pop(0) for _ in range(2)]
-    if not first:
-        out_ref = refs.pop(0)
+    if last_inner:
+        out_ref, keep_ref, send_ref, pg_ref = refs
 
         def store(ch, block, side, value):
             rows = slice(block * LANES, (block + 1) * LANES)
@@ -253,34 +266,27 @@
 
         updated(place_ref, probe_ref, obj_ref, parts, store)
         obj_ref = out_ref
-    if fresh_probe:
-        fresh_ref = refs.pop(0)
-    if last_inner:
-        keep_ref, send_ref = [refs.pop(0) for _ in range(2)]
-    if fresh_probe:
-        new_probe(place_ref, probe_ref, sums, refs[-1], fresh_ref)
-        probe_ref = fresh_ref
-    pg_ref = refs[-1] if last_inner else None
-    patterns(offset_ref, obj_ref, probe_ref, amp_ref, fwd_ref, inv_ref, gl_ref, gr_ref, pg_ref)
+    else:
+        (probe_ref,), pg_ref = refs, None
+        assemble(place_ref, pieces, probe_ref)
+    fields = (obj_ref, probe_ref, amp_ref, fwd_ref, inv_ref, gl_ref, gr_ref, pg_ref)
+    patterns(offset_ref, *fields)
     if last_inner:
         split_probe_grad(place_ref, pg_ref, keep_ref, send_ref)
 
 
-def run_pass(where, offsets, obj, parts, probe, sums, amp, tables, last_inner):
-    first, fresh = parts is None, sums is not None
-    args = [where, offsets, obj] + ([] if first else list(parts)) + [probe]
-    args += (list(sums) if fresh else []) + [amp, *tables]
-    outs = [(2, EXT, LANES)] * 2
-    outs += [] if first else [(2, EXT, PW)]
-    outs += [(2, PW, PW)] if fresh else []
-    outs += [(16, 24, PW)] * 2 if last_inner else []
-    scratch = [pltpu.VMEM((3, PW, PW), F32)] if fresh or last_inner else []
-    kernel = functools.partial(pass_kernel, first, last_inner, fresh)
-    got = list(vmem_call(kernel, outs, scratch, *args, grant=24 << 20))
-    gl, gr = got.pop(0), got.pop(0)
-    obj = obj if first else got.pop(0)
-    probe = got.pop(0) if fresh else probe
-    return gl, gr, obj, probe, got
+def first_pass(where, offsets, obj, pieces, amp, tables):
+    outs = [(2, EXT, LANES)] * 2 + [(2, PW, PW)]
+    args = (where, offsets, obj, *pieces, amp, *tables)
+    kernel = functools.partial(pass_kernel, False)
+    return vmem_call(kernel, outs, [], *args, grant=24 << 20)
+
+
+def second_pass(where, offsets, obj, parts, probe, amp, tables):
+    outs = [(2, EXT, LANES)] * 2 + [(2, EXT, PW)] + [(16, 24, PW)] * 2
+    args = (where, offsets, obj, *parts, probe, amp, *tables)
+    kernel, scratch = functools.partial(pass_kernel, True), [pltpu.VMEM((3, PW, PW), F32)]
+    return vmem_call(kernel, outs, scratch, *args, grant=24 << 20)
 
 
 def object_kernel(place_ref, obj_ref, gl, gr, rl, rr, rt, rb, probe_ref, out_ref, middle_ref):
@@ -292,9 +298,8 @@
     middle_ref[...] = out_ref[:, HALO : HALO + PW, HALO : HALO + TILE_W]
 
 
-def last_kernel(place_ref, probe_ref, object_ref, *refs):
-    new_probe(place_ref, probe_ref, refs[:8], refs[10], refs[8])
-    refs[9][...] = object_ref[...]
+def last_kernel(place_ref, *refs):
+    assemble(place_ref, refs[:8], refs[8])
 
 
 def exchange_columns(gl, gr):
@@ -332,11 +337,16 @@
     return vmem_call(kernel, [(rows, *shape[1:])] * parts, [], *arrays)
 
 
-def add_pairs(*arrays):
-    def kernel(a, b, c, d, out):
-        out[...] = (a[...] + b[...]) + (c[...] + d[...])
-
-    return vmem_call(kernel, [arrays[0].shape], [], *arrays)[0]
+def new_block(where, probe, *arrays):
+    def kernel(place_ref, probe_ref, a, b, c, d, out):
+        total = (a[...] + b[...]) + (c[...] + d[...])
+        scale = 0.5 / (total[0, 16:24] + 1.0)
+        row = block_row(place_ref, place_ref[2], 0, 0)
+        for ch in range(2):
+            span = slice(ch * 8, ch * 8 + 8)
+            out[0, span, :] = probe_ref[ch, pl.ds(row, 8), :] - total[0, span] * scale
+
+    return vmem_call(kernel, [(1, 16, PW)], [], where, probe, *arrays)[0]
 
 
 def join(*arrays):
@@ -366,31 +376,50 @@
     value = add_split((1, 24, PW), 1, value, send(value, next_z()))[0]
     outs = [(2, EXT, PW), (2, PW, TILE_W)]
     obj, middle = vmem_call(object_kernel, outs, [], where, obj, *rows, probe)
-    object_out = send(middle, from_host())
     far = send(value, far_z())
     above, below = send(value, along_z(2)), send(value, along_z(-2))
-    value = add_pairs(value, far, above, below)
+    value = new_block(where, probe, value, far, above, below)
     value = join(value, *[send(value, along_y(k)) for k in (1, 2, 3)])
     near = [value] + [send(value, along_x(k)) for k in (1, 2, 3)]
-    near[3], object_out = lax.optimization_barrier((near[3], object_out))
-    return obj, object_out, near + [send(part, core_swap()) for part in near]
-
-
-def first_windows(current, s, t):
-    def packed(half):
-        return jnp.concatenate([half[:, : PW // 2], half[:, PW // 2 :]], axis=2)
-
-    def unpacked(value):
-        return jnp.concatenate([value[:, :, :HALO], value[:, :, HALO:]], axis=1)
-
-    left = unpacked(send(packed(current[:, :, TILE_W - HALO :]), neighbour(0, 1)))
-    right = unpacked(send(packed(current[:, :, :HALO]), neighbour(0, -1)))
-    left, right = jnp.where(t == 0, 0.0, left), jnp.where(t == TILES - 1, 0.0, right)
-    wide = jnp.concatenate([left, current, right], axis=2)
-    top = send(wide[:, PW - HALO :], neighbour(1, 0))
-    bottom = send(wide[:, :HALO], neighbour(-1, 0))
-    top, bottom = jnp.where(s == 0, 0.0, top), jnp.where(s == STRIPES - 1, 0.0, bottom)
-    return jnp.concatenate([top, wide, bottom], axis=1)
+    return obj, middle, near + [send(part, core_swap()) for part in near]
+
+
+def first_windows(where, current):
+    half, ends = PW // 2, (slice(0, HALO), slice(HALO, TILE_W))
+
+    def pack(cur, to_right, to_left):
+        for ch in range(2):
+            for k, lanes in enumerate(ends):
+                rows = slice(k * half, (k + 1) * half)
+                to_right[ch, :, lanes] = cur[ch, rows, ends[1]]
+                to_left[ch, :, lanes] = cur[ch, rows, ends[0]]
+
+    def widen(place_ref, cur, from_left, from_right, wide, to_above, to_below):
+        t = place_ref[1]
+        for ch in range(2):
+            wide[ch, :, HALO : HALO + TILE_W] = cur[ch]
+            for k, lanes in enumerate(ends):
+                rows = slice(k * half, (k + 1) * half)
+                wide[ch, rows, 0:HALO] = unless(t == 0, from_left[ch, :, lanes])
+                wide[ch, rows, PW - HALO :] = unless(t == TILES - 1, from_right[ch, :, lanes])
+            to_above[ch] = wide[ch, 0:HALO]
+            to_below[ch] = wide[ch, PW - HALO : PW]
+
+    def stack(place_ref, wide, top, bottom, out):
+        s = place_ref[0]
+        for ch in range(2):
+            out[ch, 0:HALO] = unless(s == 0, top[ch])
+            out[ch, HALO : HALO + PW] = wide[ch]
+            out[ch, HALO + PW :] = unless(s == STRIPES - 1, bottom[ch])
+
+    to_right, to_left = vmem_call(pack, [(2, half, TILE_W)] * 2, [], current)
+    left = send(to_right, neighbour(0, 1))
+    right = send(to_left, neighbour(0, -1))
+    outs = [(2, PW, PW), (2, HALO, PW), (2, HALO, PW)]
+    wide, above, below = vmem_call(widen, outs, [], where, current, left, right)
+    top = send(below, neighbour(1, 0))
+    bottom = send(above, neighbour(-1, 0))
+    return vmem_call(stack, [(2, EXT, PW)], [], where, wide, top, bottom)[0]
 
 
 def per_device(positions, row_offsets, amplitudes, object_field, probe_field):
@@ -398,28 +427,25 @@
     stripe, tile = lax.axis_index("stripe"), lax.axis_index("tile")
     core, x, y, z = stripe % 2, (tile % 2) * 2 + (stripe // 2) % 2, tile // 2, stripe // 4
     s, t = z * 4 + x, y * 2 + core
+    where = jnp.stack([s, t, core, x, y]).astype(jnp.int32)
     current = send(object_field, to_host())
     amp = send(amplitudes[0], to_host())
     offsets = send(row_offsets, to_host())
-    obj = first_windows(current, s, t)
-    where = jnp.stack([s, t, core, x, y]).astype(jnp.int32)
+    obj = first_windows(where, current)
 
     def outer(unused, state):
-        obj, unused, probe, sums = state
-        first = run_pass(where, offsets, obj, None, probe, sums, amp, tables, False)
-        gl, gr, obj, probe, _ = first
+        obj, unused, pieces = state
+        gl, gr, probe = first_pass(where, offsets, obj, pieces, amp, tables)
         parts = exchange(where, gl, gr)
-        second = run_pass(where, offsets, obj, parts, probe, None, amp, tables, True)
-        gl, gr, obj, probe, rest = second
-        obj, object_out, sums = exchange_and_total(where, obj, probe, gl, gr, *rest)
-        return obj, object_out, probe, sums
-
-    none = [jnp.zeros((4, 24, PW), F32) for _ in range(8)]
-    state = (obj, jnp.zeros_like(object_field), probe_field, none)
-    obj, object_out, probe, sums = lax.fori_loop(0, OUTER, outer, state)
-    scratch, args = [pltpu.VMEM((3, PW, PW), F32)], (where, probe, object_out, *sums)
-    outs = [(2, PW, PW), (2, PW, TILE_W)]
-    probe_out, object_out = vmem_call(last_kernel, outs, scratch, *args, held=False)
+        passed = second_pass(where, offsets, obj, parts, probe, amp, tables)
+        gl, gr, obj, keep, sent = passed
+        return exchange_and_total(where, obj, probe, gl, gr, keep, sent)
+
+    outs = [(4, 16, PW)] * 8 + [(2, PW, TILE_W)]
+    *pieces, blank = vmem_call(first_pieces, outs, [], where, probe_field)
+    obj, middle, pieces = lax.fori_loop(0, OUTER, outer, (obj, blank, pieces))
+    object_out = send(middle, from_host())
+    probe_out = vmem_call(last_kernel, [(2, PW, PW)], [], where, *pieces, held=False)[0]
     return object_out, probe_out
 
 

time: 233 us -> 259 us (1.11); the launches traced: 229 us -> 258 us
  local copies, waits for them, and re-layouts: 4.58 us -> 18.9 us
  waiting for transfers between devices: 97.1 us -> 105 us
  Pallas kernels: 26.2 us -> 31.2 us
  starting transfers between devices: 99.3 us -> 102 us
    while x2 -> x52, local copies, waits for them, and re-layouts: 0.07 us -> 18.1 us
    ppermute x67 -> x66, waiting for transfers between devices: 97.1 us -> 105 us  [send(): return lax.ppermute(value, AXES, pairs)]
    pallas_call x23 -> x27, Pallas kernels: 26.2 us -> 31.2 us  [vmem_call(): pl.pallas_call(kernel, in_specs=[smem if a.dtype == jnp.int32 else vmem f...]
    ppermute x67 -> x66, starting transfers between devices: 99.3 us -> 102 us  [send(): return lax.ppermute(value, AXES, pairs)]
    another operation x8 -> x0, local copies, waits for them, and re-layouts: 2.6 us -> none
  transfers between devices with their start and end apart: 67 -> 66, of which waited for: 43 -> 39; matrix products, arithmetic and copies ran while one was open for 0% -> 0% of each run, Pallas kernels for 2% -> 5%
where the time goes in v2:
time: 259 us; the launch traced here: 258 us
  waiting for transfers between devices  105 us (41%)
  starting transfers between devices  102 us (39%)
  Pallas kernels  31.2 us (12%)
  local copies, waits for them, and re-layouts  18.9 us (7%)
    ppermute x66, waiting for transfers between devices, send(): return lax.ppermute(value, AXES, pairs)  105 us
    ppermute x66, starting transfers between devices, send(): return lax.ppermute(value, AXES, pairs)  102 us
    pallas_call x27, Pallas kernels, vmem_call(): pl.pallas_call(kernel, in_specs=[smem if a.dtype == jnp.int32 else vmem f...  31.2 us
    while x52, local copies, waits for them, and re-layouts  18.1 us
  transfers between devices with their start and end apart: 66, of which 39 were waited for; matrix products, arithmetic and copies ran while one was open for 0% of the time, Pallas kernels for 5%

profile of v2, /device:TPU:2, one launch (start us, length us, event | category | flops | bytes accessed | tf_op | source)
XLA Modules:
  0.0 258.2 jit_solution(2973095032262338164)
XLA Ops:
  0.6 3.5 %collective-permute-start.35 = (f32[3,256,256]{2,1,0:T(8,128)}, f32[3,256,256]{2,1,0:T(8,128)S(1)}, u32[]{:S(2)}, u32[]{:S(2)}) collective-permute-start(f32[3,256,256]{2,1,0:T(8,128)} %bitcast.6), channel_id=1, source_target_pairs={{0,0},{1,8},{2,2},{3,10},{4,4},{5,12},{6,6},{7,14},{8,16},{9,24},{... | collective-permute-start | bytes 2359304 | tf_op jit(solution)/shard_map/ppermute | solution.py:87
  6.1 11.0 %collective-permute-done.29.cur = f32[2,256,128]{2,1,0:T(8,128)S(1)} collective-permute-done((f32[2,256,128]{2,1,0:T(8,128)}, f32[2,256,128]{2,1,0:T(8,128)S(1)}, u32[]{:S(2)}, u32[]{:S(2)}) %collective-permute-start.29) | collective-permute-done | bytes 262176 | tf_op jit(solution)/shard_map/ppermute | solution.py:87
  25.8 4.0 %collective-permute-start.34 = (s32[1,3]{1,0:T(1,128)S(1)}, s32[1,3]{1,0:T(1,128)S(1)}, u32[]{:S(2)}, u32[]{:S(2)}) collective-permute-start(s32[1,3]{1,0:T(1,128)S(1)} %copy-done.17), channel_id=1, source_target_pairs={{0,0},{1,8},{2,2},{3,10},{4,4},{5,12},{6,6},{7,14},{8,16},{9,24},{... | collective-permute-start | bytes 44 | tf_op jit(solution)/shard_map/ppermute | solution.py:87
  32.4 4.4 %collective-permute-done.34 = s32[1,3]{1,0:T(1,128)S(1)} collective-permute-done((s32[1,3]{1,0:T(1,128)S(1)}, s32[1,3]{1,0:T(1,128)S(1)}, u32[]{:S(2)}, u32[]{:S(2)}) %collective-permute-start.34) | collective-permute-done | bytes 44 | tf_op jit(solution)/shard_map/ppermute | solution.py:87
  36.8 209.4 %while.29 = (s32[]{:T(128)}, f32[2,384,256]{2,1,0:T(8,128)S(1)}, f32[2,256,128]{2,1,0:T(8,128)}, f32[4,16,256]{2,1,0:T(8,128)}, f32[4,16,256]{2,1,0:T(8,128)}, /...) while((s32[]{:T(128)}, f32[2,384,256]{2,1,0:T(8,128)S(1)}, ...), condition=%wide.region_1.2_spmd.clone, body=%wide.region_0.1_spmd.sunk.clone.sunk | while | flops 2 | bytes 36931216 | solution.py:446
  37.0 4.4 %eval_jaxpr.11 = (f32[2,384,128]{2,1,0:T(8,128)S(1)}, f32[2,384,128]{2,1,0:T(8,128)S(1)}, f32[2,256,256]{2,1,0:T(8,128)S(1)}) custom-call(s32[5]{0:T(128)S(1)} %get-tuple-element.439.refs_0_.place_ref, s32[1,3]{1,0:T(1,128)S(1)} %get-tuple-element.440.refs_1_, f32[2,384,256]{2,1,0:T(8,128)S(1)} %get-tuple-element.412.refs_2_, ...), custom_call_target="tpu_custom_call" | custom-call | tf_op jit(solution)/shard_map/while/body/eval_jaxpr/pallas_call | solution.py:106
  42.0 4.8 %collective-permute-done.1.rr.refs_6_ = f32[2,384,128]{2,1,0:T(8,128)S(1)} collective-permute-done((f32[2,384,128]{2,1,0:T(8,128)S(1)}, f32[2,384,128]{2,1,0:T(8,128)S(1)}, u32[]{:S(2)}, u32[]{:S(2)}) %collective-permute-start.1) | collective-permute-done | bytes 393248 | tf_op jit(solution)/shard_map/while/body/eval_jaxpr/ppermute | solution.py:87
  46.8 3.1 %collective-permute-done.rl.refs_5_ = f32[2,384,128]{2,1,0:T(8,128)S(1)} collective-permute-done((f32[2,384,128]{2,1,0:T(8,128)S(1)}, f32[2,384,128]{2,1,0:T(8,128)S(1)}, u32[]{:S(2)}, u32[]{:S(2)}) %collective-permute-start) | collective-permute-done | bytes 393248 | tf_op jit(solution)/shard_map/while/body/eval_jaxpr/ppermute | solution.py:87
  53.4 3.4 %collective-permute-start.3 = (f32[2,128,256]{2,1,0:T(8,128)S(1)}, f32[2,128,256]{2,1,0:T(8,128)S(1)}, u32[]{:S(2)}, u32[]{:S(2)}) collective-permute-start(f32[2,128,256]{2,1,0:T(8,128)S(1)} %get-tuple-element.375), channel_id=1, source_target_pairs={{0,241},{8,249},{2,243},{10,251},{4,245},{12,253},{6,247},{14,255}... | collective-permute-start | bytes 786440 | tf_op jit(solution)/shard_map/while/body/eval_jaxpr/ppermute | solution.py:87
  56.8 4.3 %collective-permute-done.2.refs_7_ = f32[2,128,256]{2,1,0:T(8,128)S(1)} collective-permute-done((f32[2,128,256]{2,1,0:T(8,128)S(1)}, f32[2,128,256]{2,1,0:T(8,128)S(1)}, u32[]{:S(2)}, u32[]{:S(2)}) %collective-permute-start.2) | collective-permute-done | bytes 262176 | tf_op jit(solution)/shard_map/while/body/eval_jaxpr/ppermute | solution.py:87
  61.1 4.6 %eval_jaxpr.13 = (f32[2,384,128]{2,1,0:T(8,128)S(1)}, f32[2,384,128]{2,1,0:T(8,128)S(1)}, f32[2,384,256]{2,1,0:T(8,128)S(1)}, f32[16,24,256]{2,1,0:T(8,128)S(1)}, f32[16,24,256]{2,1,0:T(8,128)S(1)}) custom-call(s32[5]{0:T(128)S(1)} %get-tuple-element.439.refs_0_.place_ref, s32[1,3]{1,0:T(1,128)S(1)} %get-tuple-element.440.refs_1_, ...), custom_call_target="tpu_custom_call" | custom-call | tf_op jit(solution)/shard_map/while/body/eval_jaxpr/pallas_call | solution.py:106
  68.2 5.3 %collective-permute-done.5.rr = f32[2,384,128]{2,1,0:T(8,128)S(1)} collective-permute-done((f32[2,384,128]{2,1,0:T(8,128)S(1)}, f32[2,384,128]{2,1,0:T(8,128)S(1)}, u32[]{:S(2)}, u32[]{:S(2)}) %collective-permute-start.5) | collective-permute-done | bytes 393248 | tf_op jit(solution)/shard_map/while/body/eval_jaxpr/ppermute | solution.py:87
  73.5 3.1 %collective-permute-done.4.rl = f32[2,384,128]{2,1,0:T(8,128)S(1)} collective-permute-done((f32[2,384,128]{2,1,0:T(8,128)S(1)}, f32[2,384,128]{2,1,0:T(8,128)S(1)}, u32[]{:S(2)}, u32[]{:S(2)}) %collective-permute-start.4) | collective-permute-done | bytes 393248 | tf_op jit(solution)/shard_map/while/body/eval_jaxpr/ppermute | solution.py:87
  78.1 5.7 %collective-permute-start.9 = (f32[4,24,256]{2,1,0:T(8,128)S(1)}, f32[4,24,256]{2,1,0:T(8,128)S(1)}, u32[]{:S(2)}, u32[]{:S(2)}) collective-permute-start(f32[4,24,256]{2,1,0:T(8,128)S(1)} %get-tuple-element.387), channel_id=1, source_target_pairs={{0,16},{1,17},{2,18},{3,19},{4,20},{5,21},{6,22},{7,23},{8,24},{9,... | collective-permute-start | bytes 294920 | tf_op jit(solution)/shard_map/while/body/eval_jaxpr/ppermute | solution.py:87
  85.3 3.1 %collective-permute-start.7 = (f32[2,128,256]{2,1,0:T(8,128)}, f32[2,128,256]{2,1,0:T(8,128)S(1)}, u32[]{:S(2)}, u32[]{:S(2)}) collective-permute-start(f32[2,128,256]{2,1,0:T(8,128)} %get-tuple-element.381), channel_id=1, source_target_pairs={{0,241},{8,249},{2,243},{10,251},{4,245},{12,253},{6,247},{14,255}... | collective-permute-start | bytes 786440 | tf_op jit(solution)/shard_map/while/body/eval_jaxpr/ppermute | solution.py:87
  98.2 3.8 %collective-permute-done.15.refs_1_ = f32[1,24,256]{2,1,0:T(8,128)S(1)} collective-permute-done((f32[1,24,256]{2,1,0:T(8,128)S(1)}, f32[1,24,256]{2,1,0:T(8,128)S(1)}, u32[]{:S(2)}, u32[]{:S(2)}) %collective-permute-start.15) | collective-permute-done | bytes 24608 | tf_op jit(solution)/shard_map/while/body/eval_jaxpr/ppermute | solution.py:87
  102.0 5.0 %collective-permute-start.18 = (f32[1,24,256]{2,1,0:T(8,128)S(1)}, f32[1,24,256]{2,1,0:T(8,128)S(1)}, u32[]{:S(2)}, u32[]{:S(2)}) collective-permute-start(f32[1,24,256]{2,1,0:T(8,128)S(1)} %eval_jaxpr.19.a), channel_id=1, source_target_pairs={{0,192},{1,193},{2,194},{3,195},{4,196},{5,197},{6,198},{7,199},{8... | collective-permute-start | bytes 73736 | tf_op jit(solution)/shard_map/while/body/eval_jaxpr/ppermute | solution.py:87
  107.0 3.0 %collective-permute-start.16 = (f32[1,24,256]{2,1,0:T(8,128)S(1)}, f32[1,24,256]{2,1,0:T(8,128)S(1)}, u32[]{:S(2)}, u32[]{:S(2)}) collective-permute-start(f32[1,24,256]{2,1,0:T(8,128)S(1)} %eval_jaxpr.19.a), channel_id=1, source_target_pairs={{0,160},{1,161},{2,162},{3,163},{4,164},{5,165},{6,166},{7,167},{8... | collective-permute-start | bytes 73736 | tf_op jit(solution)/shard_map/while/body/eval_jaxpr/ppermute | solution.py:87
  115.6 3.0 %collective-permute-start.19 = (f32[1,16,256]{2,1,0:T(8,128)S(1)}, f32[1,16,256]{2,1,0:T(8,128)S(1)}, u32[]{:S(2)}, u32[]{:S(2)}) collective-permute-start(f32[1,16,256]{2,1,0:T(8,128)S(1)} %eval_jaxpr.20.refs_0_), channel_id=1, source_target_pairs={{0,2},{1,3},{2,0},{3,1},{4,6},{5,7},{6,4},{7,5},{8,10},{9,11},{10,... | collective-permute-start | bytes 49160 | tf_op jit(solution)/shard_map/while/body/eval_jaxpr/ppermute | solution.py:87
  122.8 5.6 %collective-permute-start.23 = (f32[4,16,256]{2,1,0:T(8,128)}, f32[4,16,256]{2,1,0:T(8,128)}, u32[]{:S(2)}, u32[]{:S(2)}) collective-permute-start(f32[4,16,256]{2,1,0:T(8,128)} %eval_jaxpr.21), channel_id=1, source_target_pairs={{0,1},{1,0},{2,3},{3,2},{4,5},{5,4},{6,7},{7,6},{8,9},{9,8},{10,11... | collective-permute-start | bytes 196616 | tf_op jit(solution)/shard_map/while/body/eval_jaxpr/ppermute | solution.py:87
  142.7 4.4 %eval_jaxpr.11 = (f32[2,384,128]{2,1,0:T(8,128)S(1)}, f32[2,384,128]{2,1,0:T(8,128)S(1)}, f32[2,256,256]{2,1,0:T(8,128)S(1)}) custom-call(s32[5]{0:T(128)S(1)} %get-tuple-element.439.refs_0_.place_ref, s32[1,3]{1,0:T(1,128)S(1)} %get-tuple-element.440.refs_1_, f32[2,384,256]{2,1,0:T(8,128)S(1)} %get-tuple-element.412.refs_2_, ...), custom_call_target="tpu_custom_call" | custom-call | tf_op jit(solution)/shard_map/while/body/eval_jaxpr/pallas_call | solution.py:106
  149.3 5.3 %collective-permute-done.1.rr.refs_6_ = f32[2,384,128]{2,1,0:T(8,128)S(1)} collective-permute-done((f32[2,384,128]{2,1,0:T(8,128)S(1)}, f32[2,384,128]{2,1,0:T(8,128)S(1)}, u32[]{:S(2)}, u32[]{:S(2)}) %collective-permute-start.1) | collective-permute-done | bytes 393248 | tf_op jit(solution)/shard_map/while/body/eval_jaxpr/ppermute | solution.py:87
  154.6 3.1 %collective-permute-done.rl.refs_5_ = f32[2,384,128]{2,1,0:T(8,128)S(1)} collective-permute-done((f32[2,384,128]{2,1,0:T(8,128)S(1)}, f32[2,384,128]{2,1,0:T(8,128)S(1)}, u32[]{:S(2)}, u32[]{:S(2)}) %collective-permute-start) | collective-permute-done | bytes 393248 | tf_op jit(solution)/shard_map/while/body/eval_jaxpr/ppermute | solution.py:87
  160.8 4.3 %collective-permute-done.2.refs_7_ = f32[2,128,256]{2,1,0:T(8,128)S(1)} collective-permute-done((f32[2,128,256]{2,1,0:T(8,128)S(1)}, f32[2,128,256]{2,1,0:T(8,128)S(1)}, u32[]{:S(2)}, u32[]{:S(2)}) %collective-permute-start.2) | collective-permute-done | bytes 262176 | tf_op jit(solution)/shard_map/while/body/eval_jaxpr/ppermute | solution.py:87
  166.5 4.6 %eval_jaxpr.13 = (f32[2,384,128]{2,1,0:T(8,128)S(1)}, f32[2,384,128]{2,1,0:T(8,128)S(1)}, f32[2,384,256]{2,1,0:T(8,128)S(1)}, f32[16,24,256]{2,1,0:T(8,128)S(1)}, f32[16,24,256]{2,1,0:T(8,128)S(1)}) custom-call(s32[5]{0:T(128)S(1)} %get-tuple-element.439.refs_0_.place_ref, s32[1,3]{1,0:T(1,128)S(1)} %get-tuple-element.440.refs_1_, ...), custom_call_target="tpu_custom_call" | custom-call | tf_op jit(solution)/shard_map/while/body/eval_jaxpr/pallas_call | solution.py:106
  173.7 5.3 %collective-permute-done.5.rr = f32[2,384,128]{2,1,0:T(8,128)S(1)} collective-permute-done((f32[2,384,128]{2,1,0:T(8,128)S(1)}, f32[2,384,128]{2,1,0:T(8,128)S(1)}, u32[]{:S(2)}, u32[]{:S(2)}) %collective-permute-start.5) | collective-permute-done | bytes 393248 | tf_op jit(solution)/shard_map/while/body/eval_jaxpr/ppermute | solution.py:87
  178.9 3.1 %collective-permute-done.4.rl = f32[2,384,128]{2,1,0:T(8,128)S(1)} collective-permute-done((f32[2,384,128]{2,1,0:T(8,128)S(1)}, f32[2,384,128]{2,1,0:T(8,128)S(1)}, u32[]{:S(2)}, u32[]{:S(2)}) %collective-permute-start.4) | collective-permute-done | bytes 393248 | tf_op jit(solution)/shard_map/while/body/eval_jaxpr/ppermute | solution.py:87
  206.1 4.6 %collective-permute-start.18 = (f32[1,24,256]{2,1,0:T(8,128)S(1)}, f32[1,24,256]{2,1,0:T(8,128)S(1)}, u32[]{:S(2)}, u32[]{:S(2)}) collective-permute-start(f32[1,24,256]{2,1,0:T(8,128)S(1)} %eval_jaxpr.19.a), channel_id=1, source_target_pairs={{0,192},{1,193},{2,194},{3,195},{4,196},{5,197},{6,198},{7,199},{8... | collective-permute-start | bytes 73736 | tf_op jit(solution)/shard_map/while/body/eval_jaxpr/ppermute | solution.py:87
  210.7 3.2 %collective-permute-start.16 = (f32[1,24,256]{2,1,0:T(8,128)S(1)}, f32[1,24,256]{2,1,0:T(8,128)S(1)}, u32[]{:S(2)}, u32[]{:S(2)}) collective-permute-start(f32[1,24,256]{2,1,0:T(8,128)S(1)} %eval_jaxpr.19.a), channel_id=1, source_target_pairs={{0,160},{1,161},{2,162},{3,163},{4,164},{5,165},{6,166},{7,167},{8... | collective-permute-start | bytes 73736 | tf_op jit(solution)/shard_map/while/body/eval_jaxpr/ppermute | solution.py:87
  226.0 5.9 %collective-permute-start.23 = (f32[4,16,256]{2,1,0:T(8,128)}, f32[4,16,256]{2,1,0:T(8,128)}, u32[]{:S(2)}, u32[]{:S(2)}) collective-permute-start(f32[4,16,256]{2,1,0:T(8,128)} %eval_jaxpr.21), channel_id=1, source_target_pairs={{0,1},{1,0},{2,3},{3,2},{4,5},{5,4},{6,7},{7,6},{8,9},{9,8},{10,11... | collective-permute-start | bytes 196616 | tf_op jit(solution)/shard_map/while/body/eval_jaxpr/ppermute | solution.py:87
  246.2 4.1 %collective-permute-start.36 = (f32[2,256,128]{2,1,0:T(8,128)}, f32[2,256,128]{2,1,0:T(8,128)S(1)}, u32[]{:S(2)}, u32[]{:S(2)}) collective-permute-start(f32[2,256,128]{2,1,0:T(8,128)} %get-tuple-element.141), channel_id=1, source_target_pairs={{0,0},{8,1},{2,2},{10,3},{4,4},{12,5},{6,6},{14,7},{16,8},{24,9},{... | collective-permute-start | bytes 786440 | tf_op jit(solution)/shard_map/ppermute | solution.py:87
  252.2 5.3 %collective-permute-done.36 = f32[2,256,128]{2,1,0:T(8,128)S(1)} collective-permute-done((f32[2,256,128]{2,1,0:T(8,128)}, f32[2,256,128]{2,1,0:T(8,128)S(1)}, u32[]{:S(2)}, u32[]{:S(2)}) %collective-permute-start.36) | collective-permute-done | bytes 262176 | tf_op jit(solution)/shard_map/ppermute | solution.py:87
  (192 shorter events, 118.5 us)
Async XLA Ops:
  0.6 36.2 %collective-permute-start.35 = (f32[3,256,256]{2,1,0:T(8,128)}, f32[3,256,256]{2,1,0:T(8,128)S(1)}, u32[]{:S(2)}, u32[]{:S(2)}) collective-permute-start(f32[3,256,256]{2,1,0:T(8,128)} %bitcast.6), channel_id=1, source_target_pairs={{0,0},{1,8},{2,2},{3,10},{4,4},{5,12},{6,6},{7,14},{8,16},{9,24},{... | collective-permute-start | bytes 2359304 | tf_op jit(solution)/shard_map/ppermute | solution.py:87
  4.2 12.9 %collective-permute-start.29 = (f32[2,256,128]{2,1,0:T(8,128)}, f32[2,256,128]{2,1,0:T(8,128)S(1)}, u32[]{:S(2)}, u32[]{:S(2)}) collective-permute-start(f32[2,256,128]{2,1,0:T(8,128)} %param.11), channel_id=1, source_target_pairs={{0,0},{1,8},{2,2},{3,10},{4,4},{5,12},{6,6},{7,14},{8,16},{9,24},{... | collective-permute-start | bytes 786440 | tf_op jit(solution)/shard_map/ppermute | solution.py:87
  23.6 7.6 %collective-permute-start.32 = (f32[2,64,256]{2,1,0:T(8,128)S(1)}, f32[2,64,256]{2,1,0:T(8,128)S(1)}, u32[]{:S(2)}, u32[]{:S(2)}) collective-permute-start(f32[2,64,256]{2,1,0:T(8,128)S(1)} %get-tuple-element.130), channel_id=1, source_target_pairs={{0,16},{8,24},{2,18},{10,26},{4,20},{12,28},{6,22},{14,30},{16,1},... | collective-permute-start | bytes 393224 | tf_op jit(solution)/shard_map/ppermute | solution.py:87
  25.8 11.1 %collective-permute-start.34 = (s32[1,3]{1,0:T(1,128)S(1)}, s32[1,3]{1,0:T(1,128)S(1)}, u32[]{:S(2)}, u32[]{:S(2)}) collective-permute-start(s32[1,3]{1,0:T(1,128)S(1)} %copy-done.17), channel_id=1, source_target_pairs={{0,0},{1,8},{2,2},{3,10},{4,4},{5,12},{6,6},{7,14},{8,16},{9,24},{... | collective-permute-start | bytes 44 | tf_op jit(solution)/shard_map/ppermute | solution.py:87
  41.5 8.4 %collective-permute-start = (f32[2,384,128]{2,1,0:T(8,128)S(1)}, f32[2,384,128]{2,1,0:T(8,128)S(1)}, u32[]{:S(2)}, u32[]{:S(2)}) collective-permute-start(f32[2,384,128]{2,1,0:T(8,128)S(1)} %get-tuple-element.373.gr.refs_4_), channel_id=1, source_target_pairs={{0,8},{8,2},{2,10},{10,4},{4,12},{12,6},{6,14},{14,0},{16,24},{24,... | collective-permute-start | bytes 1179656 | tf_op jit(solution)/shard_map/while/body/eval_jaxpr/ppermute | solution.py:87
  50.5 10.5 %collective-permute-start.2 = (f32[2,128,256]{2,1,0:T(8,128)S(1)}, f32[2,128,256]{2,1,0:T(8,128)S(1)}, u32[]{:S(2)}, u32[]{:S(2)}) collective-permute-start(f32[2,128,256]{2,1,0:T(8,128)S(1)} %get-tuple-element.374), channel_id=1, source_target_pairs={{0,16},{8,24},{2,18},{10,26},{4,20},{12,28},{6,22},{14,30},{16,1},... | collective-permute-start | bytes 786440 | tf_op jit(solution)/shard_map/while/body/eval_jaxpr/ppermute | solution.py:87
  53.4 7.7 %collective-permute-start.3 = (f32[2,128,256]{2,1,0:T(8,128)S(1)}, f32[2,128,256]{2,1,0:T(8,128)S(1)}, u32[]{:S(2)}, u32[]{:S(2)}) collective-permute-start(f32[2,128,256]{2,1,0:T(8,128)S(1)} %get-tuple-element.375), channel_id=1, source_target_pairs={{0,241},{8,249},{2,243},{10,251},{4,245},{12,253},{6,247},{14,255}... | collective-permute-start | bytes 786440 | tf_op jit(solution)/shard_map/while/body/eval_jaxpr/ppermute | solution.py:87
  68.2 8.4 %collective-permute-start.4 = (f32[2,384,128]{2,1,0:T(8,128)S(1)}, f32[2,384,128]{2,1,0:T(8,128)S(1)}, u32[]{:S(2)}, u32[]{:S(2)}) collective-permute-start(f32[2,384,128]{2,1,0:T(8,128)S(1)} %get-tuple-element.379.gr), channel_id=1, source_target_pairs={{0,8},{8,2},{2,10},{10,4},{4,12},{12,6},{6,14},{14,0},{16,24},{24,... | collective-permute-start | bytes 1179656 | tf_op jit(solution)/shard_map/while/body/eval_jaxpr/ppermute | solution.py:87
  68.2 9.8 %collective-permute-start.8 = (f32[16,24,256]{2,1,0:T(8,128)S(1)}, f32[16,24,256]{2,1,0:T(8,128)S(1)}, u32[]{:S(2)}, u32[]{:S(2)}) collective-permute-start(f32[16,24,256]{2,1,0:T(8,128)S(1)} %get-tuple-element.385), channel_id=1, source_target_pairs={{0,8},{1,9},{2,10},{3,11},{4,12},{5,13},{6,14},{7,15},{8,0},{9,1},... | collective-permute-start | bytes 1179656 | tf_op jit(solution)/shard_map/while/body/eval_jaxpr/ppermute | solution.py:87
  77.9 55.1 %collective-permute-start.6 = (f32[2,128,256]{2,1,0:T(8,128)S(1)}, f32[2,128,256]{2,1,0:T(8,128)S(1)}, u32[]{:S(2)}, u32[]{:S(2)}) collective-permute-start(f32[2,128,256]{2,1,0:T(8,128)S(1)} %get-tuple-element.380), channel_id=1, source_target_pairs={{0,16},{8,24},{2,18},{10,26},{4,20},{12,28},{6,22},{14,30},{16,1},... | collective-permute-start | bytes 786440 | tf_op jit(solution)/shard_map/while/body/eval_jaxpr/ppermute | solution.py:87
  78.1 10.9 %collective-permute-start.9 = (f32[4,24,256]{2,1,0:T(8,128)S(1)}, f32[4,24,256]{2,1,0:T(8,128)S(1)}, u32[]{:S(2)}, u32[]{:S(2)}) collective-permute-start(f32[4,24,256]{2,1,0:T(8,128)S(1)} %get-tuple-element.387), channel_id=1, source_target_pairs={{0,16},{1,17},{2,18},{3,19},{4,20},{5,21},{6,22},{7,23},{8,24},{9,... | collective-permute-start | bytes 294920 | tf_op jit(solution)/shard_map/while/body/eval_jaxpr/ppermute | solution.py:87
  85.3 48.9 %collective-permute-start.7 = (f32[2,128,256]{2,1,0:T(8,128)}, f32[2,128,256]{2,1,0:T(8,128)S(1)}, u32[]{:S(2)}, u32[]{:S(2)}) collective-permute-start(f32[2,128,256]{2,1,0:T(8,128)} %get-tuple-element.381), channel_id=1, source_target_pairs={{0,241},{8,249},{2,243},{10,251},{4,245},{12,253},{6,247},{14,255}... | collective-permute-start | bytes 786440 | tf_op jit(solution)/shard_map/while/body/eval_jaxpr/ppermute | solution.py:87
  102.0 8.0 %collective-permute-start.18 = (f32[1,24,256]{2,1,0:T(8,128)S(1)}, f32[1,24,256]{2,1,0:T(8,128)S(1)}, u32[]{:S(2)}, u32[]{:S(2)}) collective-permute-start(f32[1,24,256]{2,1,0:T(8,128)S(1)} %eval_jaxpr.19.a), channel_id=1, source_target_pairs={{0,192},{1,193},{2,194},{3,195},{4,196},{5,197},{6,198},{7,199},{8... | collective-permute-start | bytes 73736 | tf_op jit(solution)/shard_map/while/body/eval_jaxpr/ppermute | solution.py:87
  122.8 8.2 %collective-permute-start.23 = (f32[4,16,256]{2,1,0:T(8,128)}, f32[4,16,256]{2,1,0:T(8,128)}, u32[]{:S(2)}, u32[]{:S(2)}) collective-permute-start(f32[4,16,256]{2,1,0:T(8,128)} %eval_jaxpr.21), channel_id=1, source_target_pairs={{0,1},{1,0},{2,3},{3,2},{4,5},{5,4},{6,7},{7,6},{8,9},{9,8},{10,11... | collective-permute-start | bytes 196616 | tf_op jit(solution)/shard_map/while/body/eval_jaxpr/ppermute | solution.py:87
  128.7 14.0 %collective-permute-start.25 = (f32[4,16,256]{2,1,0:T(8,128)}, f32[4,16,256]{2,1,0:T(8,128)}, u32[]{:S(2)}, u32[]{:S(2)}) collective-permute-start(f32[4,16,256]{2,1,0:T(8,128)} %eval_jaxpr.21), channel_id=1, source_target_pairs={{0,8},{1,9},{2,10},{3,11},{4,12},{5,13},{6,14},{7,15},{8,0},{9,1},... | collective-permute-start | bytes 196616 | tf_op jit(solution)/shard_map/while/body/eval_jaxpr/ppermute | solution.py:87
  131.0 11.7 %collective-permute-start.28 = (f32[4,16,256]{2,1,0:T(8,128)}, f32[4,16,256]{2,1,0:T(8,128)}, u32[]{:S(2)}, u32[]{:S(2)}) collective-permute-start(f32[4,16,256]{2,1,0:T(8,128)} %collective-permute-done.24), channel_id=1, source_target_pairs={{0,8},{1,9},{2,10},{3,11},{4,12},{5,13},{6,14},{7,15},{8,0},{9,1},... | collective-permute-start | bytes 196616 | tf_op jit(solution)/shard_map/while/body/eval_jaxpr/ppermute | solution.py:87
  133.0 9.7 %collective-permute-start.27 = (f32[4,16,256]{2,1,0:T(8,128)}, f32[4,16,256]{2,1,0:T(8,128)}, u32[]{:S(2)}, u32[]{:S(2)}) collective-permute-start(f32[4,16,256]{2,1,0:T(8,128)} %collective-permute-done.23), channel_id=1, source_target_pairs={{0,8},{1,9},{2,10},{3,11},{4,12},{5,13},{6,14},{7,15},{8,0},{9,1},... | collective-permute-start | bytes 196616 | tf_op jit(solution)/shard_map/while/body/eval_jaxpr/ppermute | solution.py:87
  133.7 9.0 %collective-permute-start.26 = (f32[4,16,256]{2,1,0:T(8,128)}, f32[4,16,256]{2,1,0:T(8,128)}, u32[]{:S(2)}, u32[]{:S(2)}) collective-permute-start(f32[4,16,256]{2,1,0:T(8,128)} %collective-permute-done.22), channel_id=1, source_target_pairs={{0,8},{1,9},{2,10},{3,11},{4,12},{5,13},{6,14},{7,15},{8,0},{9,1},... | collective-permute-start | bytes 196616 | tf_op jit(solution)/shard_map/while/body/eval_jaxpr/ppermute | solution.py:87
  147.2 7.4 %collective-permute-start.1 = (f32[2,384,128]{2,1,0:T(8,128)S(1)}, f32[2,384,128]{2,1,0:T(8,128)S(1)}, u32[]{:S(2)}, u32[]{:S(2)}) collective-permute-start(f32[2,384,128]{2,1,0:T(8,128)S(1)} %get-tuple-element.372.gl.refs_3_), channel_id=1, source_target_pairs={{0,14},{8,0},{2,8},{10,2},{4,10},{12,4},{6,12},{14,6},{16,30},{24,... | collective-permute-start | bytes 1179656 | tf_op jit(solution)/shard_map/while/body/eval_jaxpr/ppermute | solution.py:87
  149.3 8.4 %collective-permute-start = (f32[2,384,128]{2,1,0:T(8,128)S(1)}, f32[2,384,128]{2,1,0:T(8,128)S(1)}, u32[]{:S(2)}, u32[]{:S(2)}) collective-permute-start(f32[2,384,128]{2,1,0:T(8,128)S(1)} %get-tuple-element.373.gr.refs_4_), channel_id=1, source_target_pairs={{0,8},{8,2},{2,10},{10,4},{4,12},{12,6},{6,14},{14,0},{16,24},{24,... | collective-permute-start | bytes 1179656 | tf_op jit(solution)/shard_map/while/body/eval_jaxpr/ppermute | solution.py:87
  173.7 8.4 %collective-permute-start.4 = (f32[2,384,128]{2,1,0:T(8,128)S(1)}, f32[2,384,128]{2,1,0:T(8,128)S(1)}, u32[]{:S(2)}, u32[]{:S(2)}) collective-permute-start(f32[2,384,128]{2,1,0:T(8,128)S(1)} %get-tuple-element.379.gr), channel_id=1, source_target_pairs={{0,8},{8,2},{2,10},{10,4},{4,12},{12,6},{6,14},{14,0},{16,24},{24,... | collective-permute-start | bytes 1179656 | tf_op jit(solution)/shard_map/while/body/eval_jaxpr/ppermute | solution.py:87
  173.7 10.5 %collective-permute-start.8 = (f32[16,24,256]{2,1,0:T(8,128)S(1)}, f32[16,24,256]{2,1,0:T(8,128)S(1)}, u32[]{:S(2)}, u32[]{:S(2)}) collective-permute-start(f32[16,24,256]{2,1,0:T(8,128)S(1)} %get-tuple-element.385), channel_id=1, source_target_pairs={{0,8},{1,9},{2,10},{3,11},{4,12},{5,13},{6,14},{7,15},{8,0},{9,1},... | collective-permute-start | bytes 1179656 | tf_op jit(solution)/shard_map/while/body/eval_jaxpr/ppermute | solution.py:87
  183.4 53.1 %collective-permute-start.6 = (f32[2,128,256]{2,1,0:T(8,128)S(1)}, f32[2,128,256]{2,1,0:T(8,128)S(1)}, u32[]{:S(2)}, u32[]{:S(2)}) collective-permute-start(f32[2,128,256]{2,1,0:T(8,128)S(1)} %get-tuple-element.380), channel_id=1, source_target_pairs={{0,16},{8,24},{2,18},{10,26},{4,20},{12,28},{6,22},{14,30},{16,1},... | collective-permute-start | bytes 786440 | tf_op jit(solution)/shard_map/while/body/eval_jaxpr/ppermute | solution.py:87
  184.2 8.9 %collective-permute-start.9 = (f32[4,24,256]{2,1,0:T(8,128)S(1)}, f32[4,24,256]{2,1,0:T(8,128)S(1)}, u32[]{:S(2)}, u32[]{:S(2)}) collective-permute-start(f32[4,24,256]{2,1,0:T(8,128)S(1)} %get-tuple-element.387), channel_id=1, source_target_pairs={{0,16},{1,17},{2,18},{3,19},{4,20},{5,21},{6,22},{7,23},{8,24},{9,... | collective-permute-start | bytes 294920 | tf_op jit(solution)/shard_map/while/body/eval_jaxpr/ppermute | solution.py:87
  188.9 48.8 %collective-permute-start.7 = (f32[2,128,256]{2,1,0:T(8,128)}, f32[2,128,256]{2,1,0:T(8,128)S(1)}, u32[]{:S(2)}, u32[]{:S(2)}) collective-permute-start(f32[2,128,256]{2,1,0:T(8,128)} %get-tuple-element.381), channel_id=1, source_target_pairs={{0,241},{8,249},{2,243},{10,251},{4,245},{12,253},{6,247},{14,255}... | collective-permute-start | bytes 786440 | tf_op jit(solution)/shard_map/while/body/eval_jaxpr/ppermute | solution.py:87
  206.1 7.8 %collective-permute-start.18 = (f32[1,24,256]{2,1,0:T(8,128)S(1)}, f32[1,24,256]{2,1,0:T(8,128)S(1)}, u32[]{:S(2)}, u32[]{:S(2)}) collective-permute-start(f32[1,24,256]{2,1,0:T(8,128)S(1)} %eval_jaxpr.19.a), channel_id=1, source_target_pairs={{0,192},{1,193},{2,194},{3,195},{4,196},{5,197},{6,198},{7,199},{8... | collective-permute-start | bytes 73736 | tf_op jit(solution)/shard_map/while/body/eval_jaxpr/ppermute | solution.py:87
  226.0 8.5 %collective-permute-start.23 = (f32[4,16,256]{2,1,0:T(8,128)}, f32[4,16,256]{2,1,0:T(8,128)}, u32[]{:S(2)}, u32[]{:S(2)}) collective-permute-start(f32[4,16,256]{2,1,0:T(8,128)} %eval_jaxpr.21), channel_id=1, source_target_pairs={{0,1},{1,0},{2,3},{3,2},{4,5},{5,4},{6,7},{7,6},{8,9},{9,8},{10,11... | collective-permute-start | bytes 196616 | tf_op jit(solution)/shard_map/while/body/eval_jaxpr/ppermute | solution.py:87
  232.5 13.7 %collective-permute-start.25 = (f32[4,16,256]{2,1,0:T(8,128)}, f32[4,16,256]{2,1,0:T(8,128)}, u32[]{:S(2)}, u32[]{:S(2)}) collective-permute-start(f32[4,16,256]{2,1,0:T(8,128)} %eval_jaxpr.21), channel_id=1, source_target_pairs={{0,8},{1,9},{2,10},{3,11},{4,12},{5,13},{6,14},{7,15},{8,0},{9,1},... | collective-permute-start | bytes 196616 | tf_op jit(solution)/shard_map/while/body/eval_jaxpr/ppermute | solution.py:87
  234.5 11.7 %collective-permute-start.28 = (f32[4,16,256]{2,1,0:T(8,128)}, f32[4,16,256]{2,1,0:T(8,128)}, u32[]{:S(2)}, u32[]{:S(2)}) collective-permute-start(f32[4,16,256]{2,1,0:T(8,128)} %collective-permute-done.24), channel_id=1, source_target_pairs={{0,8},{1,9},{2,10},{3,11},{4,12},{5,13},{6,14},{7,15},{8,0},{9,1},... | collective-permute-start | bytes 196616 | tf_op jit(solution)/shard_map/while/body/eval_jaxpr/ppermute | solution.py:87
  236.5 9.7 %collective-permute-start.27 = (f32[4,16,256]{2,1,0:T(8,128)}, f32[4,16,256]{2,1,0:T(8,128)}, u32[]{:S(2)}, u32[]{:S(2)}) collective-permute-start(f32[4,16,256]{2,1,0:T(8,128)} %collective-permute-done.23), channel_id=1, source_target_pairs={{0,8},{1,9},{2,10},{3,11},{4,12},{5,13},{6,14},{7,15},{8,0},{9,1},... | collective-permute-start | bytes 196616 | tf_op jit(solution)/shard_map/while/body/eval_jaxpr/ppermute | solution.py:87
  237.2 9.0 %collective-permute-start.26 = (f32[4,16,256]{2,1,0:T(8,128)}, f32[4,16,256]{2,1,0:T(8,128)}, u32[]{:S(2)}, u32[]{:S(2)}) collective-permute-start(f32[4,16,256]{2,1,0:T(8,128)} %collective-permute-done.22), channel_id=1, source_target_pairs={{0,8},{1,9},{2,10},{3,11},{4,12},{5,13},{6,14},{7,15},{8,0},{9,1},... | collective-permute-start | bytes 196616 | tf_op jit(solution)/shard_map/while/body/eval_jaxpr/ppermute | solution.py:87
  246.2 11.3 %collective-permute-start.36 = (f32[2,256,128]{2,1,0:T(8,128)}, f32[2,256,128]{2,1,0:T(8,128)S(1)}, u32[]{:S(2)}, u32[]{:S(2)}) collective-permute-start(f32[2,256,128]{2,1,0:T(8,128)} %get-tuple-element.141), channel_id=1, source_target_pairs={{0,0},{8,1},{2,2},{10,3},{4,4},{12,5},{6,6},{14,7},{16,8},{24,9},{... | collective-permute-start | bytes 786440 | tf_op jit(solution)/shard_map/ppermute | solution.py:87
  (65 other events, 287.4 us)

commit v3 on v2

--- a/solution.py
+++ b/solution.py
@@ -158,21 +158,21 @@
     c = place_ref[2]
     for k in range(4):
         for j in range(4):
-            for half, ref in ((c, pieces[k]), (1 - c, pieces[4 + k])):
+            for half, ref in ((c, pieces[0]), (1 - c, pieces[1])):
                 row = block_row(place_ref, half, k, j)
                 for ch in range(2):
-                    out_ref[ch, pl.ds(row, 8), :] = ref[j, ch * 8 : ch * 8 + 8, :]
+                    out_ref[ch, pl.ds(row, 8), :] = ref[k * 4 + j, ch * 8 : ch * 8 + 8, :]
 
 
 def first_pieces(place_ref, probe_ref, *outs):
     c = place_ref[2]
     for k in range(4):
         for j in range(4):
-            for half, ref in ((c, outs[k]), (1 - c, outs[4 + k])):
+            for half, ref in ((c, outs[0]), (1 - c, outs[1])):
                 row = block_row(place_ref, half, k, j)
                 for ch in range(2):
-                    ref[j, ch * 8 : ch * 8 + 8, :] = probe_ref[ch, pl.ds(row, 8), :]
-    outs[8][...] = jnp.zeros_like(outs[8])
+                    ref[k * 4 + j, ch * 8 : ch * 8 + 8, :] = probe_ref[ch, pl.ds(row, 8), :]
+    outs[2][...] = jnp.zeros_like(outs[2])
 
 
 def lifted(value, shift):
@@ -254,7 +254,7 @@
         parts = [refs.pop(0) for _ in range(6)]
         probe_ref = refs.pop(0)
     else:
-        pieces = [refs.pop(0) for _ in range(8)]
+        pieces = [refs.pop(0) for _ in range(2)]
     amp_ref, fwd_ref, inv_ref = [refs.pop(0) for _ in range(3)]
     gl_ref, gr_ref = [refs.pop(0) for _ in range(2)]
     if last_inner:
@@ -298,8 +298,9 @@
     middle_ref[...] = out_ref[:, HALO : HALO + PW, HALO : HALO + TILE_W]
 
 
-def last_kernel(place_ref, *refs):
-    assemble(place_ref, refs[:8], refs[8])
+def last_kernel(place_ref, near_ref, far_ref, object_ref, probe_out_ref, object_out_ref):
+    assemble(place_ref, (near_ref, far_ref), probe_out_ref)
+    object_out_ref[...] = object_ref[...]
 
 
 def exchange_columns(gl, gr):
@@ -376,12 +377,14 @@
     value = add_split((1, 24, PW), 1, value, send(value, next_z()))[0]
     outs = [(2, EXT, PW), (2, PW, TILE_W)]
     obj, middle = vmem_call(object_kernel, outs, [], where, obj, *rows, probe)
+    object_out = send(middle, from_host())
     far = send(value, far_z())
     above, below = send(value, along_z(2)), send(value, along_z(-2))
     value = new_block(where, probe, value, far, above, below)
     value = join(value, *[send(value, along_y(k)) for k in (1, 2, 3)])
-    near = [value] + [send(value, along_x(k)) for k in (1, 2, 3)]
-    return obj, middle, near + [send(part, core_swap()) for part in near]
+    near = join(value, *[send(value, along_x(k)) for k in (1, 2, 3)])
+    near, object_out = lax.optimization_barrier((near, object_out))
+    return obj, object_out, near, send(near, core_swap())
 
 
 def first_windows(where, current):
@@ -434,18 +437,18 @@
     obj = first_windows(where, current)
 
     def outer(unused, state):
-        obj, unused, pieces = state
+        obj, unused, *pieces = state
         gl, gr, probe = first_pass(where, offsets, obj, pieces, amp, tables)
         parts = exchange(where, gl, gr)
         passed = second_pass(where, offsets, obj, parts, probe, amp, tables)
         gl, gr, obj, keep, sent = passed
         return exchange_and_total(where, obj, probe, gl, gr, keep, sent)
 
-    outs = [(4, 16, PW)] * 8 + [(2, PW, TILE_W)]
-    *pieces, blank = vmem_call(first_pieces, outs, [], where, probe_field)
-    obj, middle, pieces = lax.fori_loop(0, OUTER, outer, (obj, blank, pieces))
-    object_out = send(middle, from_host())
-    probe_out = vmem_call(last_kernel, [(2, PW, PW)], [], where, *pieces, held=False)[0]
+    outs = [(16, 16, PW)] * 2 + [(2, PW, TILE_W)]
+    near, far, blank = vmem_call(first_pieces, outs, [], where, probe_field)
+    obj, middle, near, far = lax.fori_loop(0, OUTER, outer, (obj, blank, near, far))
+    outs, args = [(2, PW, PW), (2, PW, TILE_W)], (where, near, far, middle)
+    probe_out, object_out = vmem_call(last_kernel, outs, [], *args, held=False)
     return object_out, probe_out
 
 

time: 259 us -> 250 us (0.965)
  waiting for transfers between devices: 105 us -> 125 us
  local copies, waits for them, and re-layouts: 18.9 us -> 0.1 us
  starting transfers between devices: 102 us -> 95.1 us
  Pallas kernels: 31.2 us -> 26.3 us
    ppermute x66 -> x61, waiting for transfers between devices: 105 us -> 125 us  [send(): return lax.ppermute(value, AXES, pairs)]
    while x52 -> x0, local copies, waits for them, and re-layouts: 18.1 us -> none
    ppermute x66 -> x61, starting transfers between devices: 102 us -> 95.1 us  [send(): return lax.ppermute(value, AXES, pairs)]
    pallas_call x27 -> x29, Pallas kernels: 31.2 us -> 26.3 us  [vmem_call(): pl.pallas_call(kernel, in_specs=[smem if a.dtype == jnp.int32 else vmem f...]
  transfers between devices with their start and end apart: 66 -> 61, of which waited for: 39 -> 46; matrix products, arithmetic and copies ran while one was open for 0% -> 0% of each run, Pallas kernels for 5% -> 3%
where the time goes in v3:
time: 250 us; the launch traced here: 247 us
  waiting for transfers between devices  125 us (50%)
  starting transfers between devices  95.1 us (38%)
  Pallas kernels  26.3 us (11%)
    ppermute x61, waiting for transfers between devices, send(): return lax.ppermute(value, AXES, pairs)  125 us
    ppermute x61, starting transfers between devices, send(): return lax.ppermute(value, AXES, pairs)  95.1 us
    pallas_call x29, Pallas kernels, vmem_call(): pl.pallas_call(kernel, in_specs=[smem if a.dtype == jnp.int32 else vmem f...  26.3 us
  transfers between devices with their start and end apart: 61, of which 46 were waited for; matrix products, arithmetic and copies ran while one was open for 0% of the time, Pallas kernels for 3%

profile of v3, /device:TPU:2, one launch (start us, length us, event | category | flops | bytes accessed | tf_op | source)
XLA Modules:
  0.0 247.4 jit_solution(17018193292438339815)
XLA Ops:
  0.6 3.5 %collective-permute-start.33 = (f32[3,256,256]{2,1,0:T(8,128)}, f32[3,256,256]{2,1,0:T(8,128)S(1)}, u32[]{:S(2)}, u32[]{:S(2)}) collective-permute-start(f32[3,256,256]{2,1,0:T(8,128)} %bitcast.6), channel_id=1, source_target_pairs={{0,0},{1,8},{2,2},{3,10},{4,4},{5,12},{6,6},{7,14},{8,16},{9,24},{... | collective-permute-start | bytes 2359304 | tf_op jit(solution)/shard_map/ppermute | solution.py:87
  6.1 11.0 %collective-permute-done.27.cur = f32[2,256,128]{2,1,0:T(8,128)S(1)} collective-permute-done((f32[2,256,128]{2,1,0:T(8,128)}, f32[2,256,128]{2,1,0:T(8,128)S(1)}, u32[]{:S(2)}, u32[]{:S(2)}) %collective-permute-start.27) | collective-permute-done | bytes 262176 | tf_op jit(solution)/shard_map/ppermute | solution.py:87
  25.8 4.0 %collective-permute-start.32 = (s32[1,3]{1,0:T(1,128)S(1)}, s32[1,3]{1,0:T(1,128)S(1)}, u32[]{:S(2)}, u32[]{:S(2)}) collective-permute-start(s32[1,3]{1,0:T(1,128)S(1)} %copy-done.3), channel_id=1, source_target_pairs={{0,0},{1,8},{2,2},{3,10},{4,4},{5,12},{6,6},{7,14},{8,16},{9,24},{... | collective-permute-start | bytes 44 | tf_op jit(solution)/shard_map/ppermute | solution.py:87
  32.4 4.5 %collective-permute-done.32 = s32[1,3]{1,0:T(1,128)S(1)} collective-permute-done((s32[1,3]{1,0:T(1,128)S(1)}, s32[1,3]{1,0:T(1,128)S(1)}, u32[]{:S(2)}, u32[]{:S(2)}) %collective-permute-start.32) | collective-permute-done | bytes 44 | tf_op jit(solution)/shard_map/ppermute | solution.py:87
  36.8 209.1 %while.17 = (s32[]{:T(128)}, f32[2,384,256]{2,1,0:T(8,128)S(1)}, f32[2,256,128]{2,1,0:T(8,128)S(1)}, f32[16,16,256]{2,1,0:T(8,128)S(1)}, f32[16,16,256]{2,1,0:T(...) while((s32[]{:T(128)}, f32[2,384,256]{2,1,0:T(8,128)S(1)}, ...), condition=%wide.region_1.2_spmd.clone, body=%wide.region_0.1_spmd.sunk.clone.sunk | while | flops 2 | bytes 17007780 | solution.py:449
  37.0 3.9 %eval_jaxpr.12 = (f32[2,384,128]{2,1,0:T(8,128)S(1)}, f32[2,384,128]{2,1,0:T(8,128)S(1)}, f32[2,256,256]{2,1,0:T(8,128)S(1)}) custom-call(s32[5]{0:T(128)S(1)} %get-tuple-element.315.refs_0_.place_ref, s32[1,3]{1,0:T(1,128)S(1)} %get-tuple-element.316.refs_1_, f32[2,384,256]{2,1,0:T(8,128)S(1)} %get-tuple-element.300.refs_2_, ...), custom_call_target="tpu_custom_call" | custom-call | tf_op jit(solution)/shard_map/while/body/eval_jaxpr/pallas_call | solution.py:106
  41.5 4.8 %collective-permute-done.1.rr.refs_6_ = f32[2,384,128]{2,1,0:T(8,128)S(1)} collective-permute-done((f32[2,384,128]{2,1,0:T(8,128)S(1)}, f32[2,384,128]{2,1,0:T(8,128)S(1)}, u32[]{:S(2)}, u32[]{:S(2)}) %collective-permute-start.1) | collective-permute-done | bytes 393248 | tf_op jit(solution)/shard_map/while/body/eval_jaxpr/ppermute | solution.py:87
  46.3 3.1 %collective-permute-done.rl.refs_5_ = f32[2,384,128]{2,1,0:T(8,128)S(1)} collective-permute-done((f32[2,384,128]{2,1,0:T(8,128)S(1)}, f32[2,384,128]{2,1,0:T(8,128)S(1)}, u32[]{:S(2)}, u32[]{:S(2)}) %collective-permute-start) | collective-permute-done | bytes 393248 | tf_op jit(solution)/shard_map/while/body/eval_jaxpr/ppermute | solution.py:87
  52.0 4.3 %collective-permute-start.3 = (f32[2,128,256]{2,1,0:T(8,128)S(1)}, f32[2,128,256]{2,1,0:T(8,128)S(1)}, u32[]{:S(2)}, u32[]{:S(2)}) collective-permute-start(f32[2,128,256]{2,1,0:T(8,128)S(1)} %get-tuple-element.267), channel_id=1, source_target_pairs={{0,241},{8,249},{2,243},{10,251},{4,245},{12,253},{6,247},{14,255}... | collective-permute-start | bytes 786440 | tf_op jit(solution)/shard_map/while/body/eval_jaxpr/ppermute | solution.py:87
  56.3 4.3 %collective-permute-done.2.refs_7_ = f32[2,128,256]{2,1,0:T(8,128)S(1)} collective-permute-done((f32[2,128,256]{2,1,0:T(8,128)S(1)}, f32[2,128,256]{2,1,0:T(8,128)S(1)}, u32[]{:S(2)}, u32[]{:S(2)}) %collective-permute-start.2) | collective-permute-done | bytes 262176 | tf_op jit(solution)/shard_map/while/body/eval_jaxpr/ppermute | solution.py:87
  60.5 4.6 %eval_jaxpr.14 = (f32[2,384,128]{2,1,0:T(8,128)S(1)}, f32[2,384,128]{2,1,0:T(8,128)S(1)}, f32[2,384,256]{2,1,0:T(8,128)S(1)}, f32[16,24,256]{2,1,0:T(8,128)S(1)}, f32[16,24,256]{2,1,0:T(8,128)S(1)}) custom-call(s32[5]{0:T(128)S(1)} %get-tuple-element.315.refs_0_.place_ref, s32[1,3]{1,0:T(1,128)S(1)} %get-tuple-element.316.refs_1_, ...), custom_call_target="tpu_custom_call" | custom-call | tf_op jit(solution)/shard_map/while/body/eval_jaxpr/pallas_call | solution.py:106
  66.8 5.3 %collective-permute-done.5.rr = f32[2,384,128]{2,1,0:T(8,128)S(1)} collective-permute-done((f32[2,384,128]{2,1,0:T(8,128)S(1)}, f32[2,384,128]{2,1,0:T(8,128)S(1)}, u32[]{:S(2)}, u32[]{:S(2)}) %collective-permute-start.5) | collective-permute-done | bytes 393248 | tf_op jit(solution)/shard_map/while/body/eval_jaxpr/ppermute | solution.py:87
  72.1 3.1 %collective-permute-done.4.rl = f32[2,384,128]{2,1,0:T(8,128)S(1)} collective-permute-done((f32[2,384,128]{2,1,0:T(8,128)S(1)}, f32[2,384,128]{2,1,0:T(8,128)S(1)}, u32[]{:S(2)}, u32[]{:S(2)}) %collective-permute-start.4) | collective-permute-done | bytes 393248 | tf_op jit(solution)/shard_map/while/body/eval_jaxpr/ppermute | solution.py:87
  75.9 5.7 %collective-permute-start.7 = (f32[2,128,256]{2,1,0:T(8,128)S(1)}, f32[2,128,256]{2,1,0:T(8,128)S(1)}, u32[]{:S(2)}, u32[]{:S(2)}) collective-permute-start(f32[2,128,256]{2,1,0:T(8,128)S(1)} %get-tuple-element.273), channel_id=1, source_target_pairs={{0,241},{8,249},{2,243},{10,251},{4,245},{12,253},{6,247},{14,255}... | collective-permute-start | bytes 786440 | tf_op jit(solution)/shard_map/while/body/eval_jaxpr/ppermute | solution.py:87
  81.5 4.3 %collective-permute-done.6.rt = f32[2,128,256]{2,1,0:T(8,128)S(1)} collective-permute-done((f32[2,128,256]{2,1,0:T(8,128)S(1)}, f32[2,128,256]{2,1,0:T(8,128)S(1)}, u32[]{:S(2)}, u32[]{:S(2)}) %collective-permute-start.6) | collective-permute-done | bytes 262176 | tf_op jit(solution)/shard_map/while/body/eval_jaxpr/ppermute | solution.py:87
  88.8 4.2 %collective-permute-start.9 = (f32[4,24,256]{2,1,0:T(8,128)S(1)}, f32[4,24,256]{2,1,0:T(8,128)S(1)}, u32[]{:S(2)}, u32[]{:S(2)}) collective-permute-start(f32[4,24,256]{2,1,0:T(8,128)S(1)} %get-tuple-element.278), channel_id=1, source_target_pairs={{0,16},{1,17},{2,18},{3,19},{4,20},{5,21},{6,22},{7,23},{8,24},{9,... | collective-permute-start | bytes 294920 | tf_op jit(solution)/shard_map/while/body/eval_jaxpr/ppermute | solution.py:87
  101.2 3.8 %collective-permute-start.13 = (f32[1,24,256]{2,1,0:T(8,128)S(1)}, f32[1,24,256]{2,1,0:T(8,128)S(1)}, u32[]{:S(2)}, u32[]{:S(2)}) collective-permute-start(f32[1,24,256]{2,1,0:T(8,128)S(1)} %get-tuple-element.283), channel_id=1, source_target_pairs={{0,4},{1,5},{2,6},{3,7},{4,0},{5,1},{6,2},{7,3},{8,12},{9,13},{10,... | collective-permute-start | bytes 73736 | tf_op jit(solution)/shard_map/while/body/eval_jaxpr/ppermute | solution.py:87
  110.1 3.8 %collective-permute-done.15.refs_1_ = f32[1,24,256]{2,1,0:T(8,128)S(1)} collective-permute-done((f32[1,24,256]{2,1,0:T(8,128)S(1)}, f32[1,24,256]{2,1,0:T(8,128)S(1)}, u32[]{:S(2)}, u32[]{:S(2)}) %collective-permute-start.15) | collective-permute-done | bytes 24608 | tf_op jit(solution)/shard_map/while/body/eval_jaxpr/ppermute | solution.py:87
  113.9 5.5 %collective-permute-start.18 = (f32[1,24,256]{2,1,0:T(8,128)S(1)}, f32[1,24,256]{2,1,0:T(8,128)S(1)}, u32[]{:S(2)}, u32[]{:S(2)}) collective-permute-start(f32[1,24,256]{2,1,0:T(8,128)S(1)} %eval_jaxpr.20.a), channel_id=1, source_target_pairs={{0,192},{1,193},{2,194},{3,195},{4,196},{5,197},{6,198},{7,199},{8... | collective-permute-start | bytes 73736 | tf_op jit(solution)/shard_map/while/body/eval_jaxpr/ppermute | solution.py:87
  142.5 3.9 %eval_jaxpr.12 = (f32[2,384,128]{2,1,0:T(8,128)S(1)}, f32[2,384,128]{2,1,0:T(8,128)S(1)}, f32[2,256,256]{2,1,0:T(8,128)S(1)}) custom-call(s32[5]{0:T(128)S(1)} %get-tuple-element.315.refs_0_.place_ref, s32[1,3]{1,0:T(1,128)S(1)} %get-tuple-element.316.refs_1_, f32[2,384,256]{2,1,0:T(8,128)S(1)} %get-tuple-element.300.refs_2_, ...), custom_call_target="tpu_custom_call" | custom-call | tf_op jit(solution)/shard_map/while/body/eval_jaxpr/pallas_call | solution.py:106
  148.1 5.3 %collective-permute-done.1.rr.refs_6_ = f32[2,384,128]{2,1,0:T(8,128)S(1)} collective-permute-done((f32[2,384,128]{2,1,0:T(8,128)S(1)}, f32[2,384,128]{2,1,0:T(8,128)S(1)}, u32[]{:S(2)}, u32[]{:S(2)}) %collective-permute-start.1) | collective-permute-done | bytes 393248 | tf_op jit(solution)/shard_map/while/body/eval_jaxpr/ppermute | solution.py:87
  153.4 3.1 %collective-permute-done.rl.refs_5_ = f32[2,384,128]{2,1,0:T(8,128)S(1)} collective-permute-done((f32[2,384,128]{2,1,0:T(8,128)S(1)}, f32[2,384,128]{2,1,0:T(8,128)S(1)}, u32[]{:S(2)}, u32[]{:S(2)}) %collective-permute-start) | collective-permute-done | bytes 393248 | tf_op jit(solution)/shard_map/while/body/eval_jaxpr/ppermute | solution.py:87
  159.3 4.3 %collective-permute-done.2.refs_7_ = f32[2,128,256]{2,1,0:T(8,128)S(1)} collective-permute-done((f32[2,128,256]{2,1,0:T(8,128)S(1)}, f32[2,128,256]{2,1,0:T(8,128)S(1)}, u32[]{:S(2)}, u32[]{:S(2)}) %collective-permute-start.2) | collective-permute-done | bytes 262176 | tf_op jit(solution)/shard_map/while/body/eval_jaxpr/ppermute | solution.py:87
  164.3 4.6 %eval_jaxpr.14 = (f32[2,384,128]{2,1,0:T(8,128)S(1)}, f32[2,384,128]{2,1,0:T(8,128)S(1)}, f32[2,384,256]{2,1,0:T(8,128)S(1)}, f32[16,24,256]{2,1,0:T(8,128)S(1)}, f32[16,24,256]{2,1,0:T(8,128)S(1)}) custom-call(s32[5]{0:T(128)S(1)} %get-tuple-element.315.refs_0_.place_ref, s32[1,3]{1,0:T(1,128)S(1)} %get-tuple-element.316.refs_1_, ...), custom_call_target="tpu_custom_call" | custom-call | tf_op jit(solution)/shard_map/while/body/eval_jaxpr/pallas_call | solution.py:106
  170.5 5.3 %collective-permute-done.5.rr = f32[2,384,128]{2,1,0:T(8,128)S(1)} collective-permute-done((f32[2,384,128]{2,1,0:T(8,128)S(1)}, f32[2,384,128]{2,1,0:T(8,128)S(1)}, u32[]{:S(2)}, u32[]{:S(2)}) %collective-permute-start.5) | collective-permute-done | bytes 393248 | tf_op jit(solution)/shard_map/while/body/eval_jaxpr/ppermute | solution.py:87
  175.8 3.1 %collective-permute-done.4.rl = f32[2,384,128]{2,1,0:T(8,128)S(1)} collective-permute-done((f32[2,384,128]{2,1,0:T(8,128)S(1)}, f32[2,384,128]{2,1,0:T(8,128)S(1)}, u32[]{:S(2)}, u32[]{:S(2)}) %collective-permute-start.4) | collective-permute-done | bytes 393248 | tf_op jit(solution)/shard_map/while/body/eval_jaxpr/ppermute | solution.py:87
  183.8 4.3 %collective-permute-done.6.rt = f32[2,128,256]{2,1,0:T(8,128)S(1)} collective-permute-done((f32[2,128,256]{2,1,0:T(8,128)S(1)}, f32[2,128,256]{2,1,0:T(8,128)S(1)}, u32[]{:S(2)}, u32[]{:S(2)}) %collective-permute-start.6) | collective-permute-done | bytes 262176 | tf_op jit(solution)/shard_map/while/body/eval_jaxpr/ppermute | solution.py:87
  198.6 7.5 %collective-permute-done.10.refs_2_ = f32[4,24,256]{2,1,0:T(8,128)S(1)} collective-permute-done((f32[4,24,256]{2,1,0:T(8,128)S(1)}, f32[4,24,256]{2,1,0:T(8,128)S(1)}, u32[]{:S(2)}, u32[]{:S(2)}) %collective-permute-start.10) | collective-permute-done | bytes 98336 | tf_op jit(solution)/shard_map/while/body/eval_jaxpr/ppermute | solution.py:87
  206.6 3.7 %collective-permute-start.13 = (f32[1,24,256]{2,1,0:T(8,128)S(1)}, f32[1,24,256]{2,1,0:T(8,128)S(1)}, u32[]{:S(2)}, u32[]{:S(2)}) collective-permute-start(f32[1,24,256]{2,1,0:T(8,128)S(1)} %get-tuple-element.283), channel_id=1, source_target_pairs={{0,4},{1,5},{2,6},{3,7},{4,0},{5,1},{6,2},{7,3},{8,12},{9,13},{10,... | collective-permute-start | bytes 73736 | tf_op jit(solution)/shard_map/while/body/eval_jaxpr/ppermute | solution.py:87
  216.1 3.1 %collective-permute-done.15.refs_1_ = f32[1,24,256]{2,1,0:T(8,128)S(1)} collective-permute-done((f32[1,24,256]{2,1,0:T(8,128)S(1)}, f32[1,24,256]{2,1,0:T(8,128)S(1)}, u32[]{:S(2)}, u32[]{:S(2)}) %collective-permute-start.15) | collective-permute-done | bytes 24608 | tf_op jit(solution)/shard_map/while/body/eval_jaxpr/ppermute | solution.py:87
  219.3 4.2 %collective-permute-start.18 = (f32[1,24,256]{2,1,0:T(8,128)S(1)}, f32[1,24,256]{2,1,0:T(8,128)S(1)}, u32[]{:S(2)}, u32[]{:S(2)}) collective-permute-start(f32[1,24,256]{2,1,0:T(8,128)S(1)} %eval_jaxpr.20.a), channel_id=1, source_target_pairs={{0,192},{1,193},{2,194},{3,195},{4,196},{5,197},{6,198},{7,199},{8... | collective-permute-start | bytes 73736 | tf_op jit(solution)/shard_map/while/body/eval_jaxpr/ppermute | solution.py:87
  225.8 3.6 %collective-permute-done.17.c = f32[1,24,256]{2,1,0:T(8,128)S(1)} collective-permute-done((f32[1,24,256]{2,1,0:T(8,128)S(1)}, f32[1,24,256]{2,1,0:T(8,128)S(1)}, u32[]{:S(2)}, u32[]{:S(2)}) %collective-permute-start.17) | collective-permute-done | bytes 24608 | tf_op jit(solution)/shard_map/while/body/eval_jaxpr/ppermute | solution.py:87
  (129 shorter events, 106.8 us)
Async XLA Ops:
  0.6 36.2 %collective-permute-start.33 = (f32[3,256,256]{2,1,0:T(8,128)}, f32[3,256,256]{2,1,0:T(8,128)S(1)}, u32[]{:S(2)}, u32[]{:S(2)}) collective-permute-start(f32[3,256,256]{2,1,0:T(8,128)} %bitcast.6), channel_id=1, source_target_pairs={{0,0},{1,8},{2,2},{3,10},{4,4},{5,12},{6,6},{7,14},{8,16},{9,24},{... | collective-permute-start | bytes 2359304 | tf_op jit(solution)/shard_map/ppermute | solution.py:87
  4.2 12.9 %collective-permute-start.27 = (f32[2,256,128]{2,1,0:T(8,128)}, f32[2,256,128]{2,1,0:T(8,128)S(1)}, u32[]{:S(2)}, u32[]{:S(2)}) collective-permute-start(f32[2,256,128]{2,1,0:T(8,128)} %param.11), channel_id=1, source_target_pairs={{0,0},{1,8},{2,2},{3,10},{4,4},{5,12},{6,6},{7,14},{8,16},{9,24},{... | collective-permute-start | bytes 786440 | tf_op jit(solution)/shard_map/ppermute | solution.py:87
  23.6 6.8 %collective-permute-start.30 = (f32[2,64,256]{2,1,0:T(8,128)S(1)}, f32[2,64,256]{2,1,0:T(8,128)S(1)}, u32[]{:S(2)}, u32[]{:S(2)}) collective-permute-start(f32[2,64,256]{2,1,0:T(8,128)S(1)} %get-tuple-element.92), channel_id=1, source_target_pairs={{0,16},{8,24},{2,18},{10,26},{4,20},{12,28},{6,22},{14,30},{16,1},... | collective-permute-start | bytes 393224 | tf_op jit(solution)/shard_map/ppermute | solution.py:87
  25.8 11.1 %collective-permute-start.32 = (s32[1,3]{1,0:T(1,128)S(1)}, s32[1,3]{1,0:T(1,128)S(1)}, u32[]{:S(2)}, u32[]{:S(2)}) collective-permute-start(s32[1,3]{1,0:T(1,128)S(1)} %copy-done.3), channel_id=1, source_target_pairs={{0,0},{1,8},{2,2},{3,10},{4,4},{5,12},{6,6},{7,14},{8,16},{9,24},{... | collective-permute-start | bytes 44 | tf_op jit(solution)/shard_map/ppermute | solution.py:87
  41.0 8.4 %collective-permute-start = (f32[2,384,128]{2,1,0:T(8,128)S(1)}, f32[2,384,128]{2,1,0:T(8,128)S(1)}, u32[]{:S(2)}, u32[]{:S(2)}) collective-permute-start(f32[2,384,128]{2,1,0:T(8,128)S(1)} %get-tuple-element.265.gr.refs_4_), channel_id=1, source_target_pairs={{0,8},{8,2},{2,10},{10,4},{4,12},{12,6},{6,14},{14,0},{16,24},{24,... | collective-permute-start | bytes 1179656 | tf_op jit(solution)/shard_map/while/body/eval_jaxpr/ppermute | solution.py:87
  50.0 10.5 %collective-permute-start.2 = (f32[2,128,256]{2,1,0:T(8,128)S(1)}, f32[2,128,256]{2,1,0:T(8,128)S(1)}, u32[]{:S(2)}, u32[]{:S(2)}) collective-permute-start(f32[2,128,256]{2,1,0:T(8,128)S(1)} %get-tuple-element.266), channel_id=1, source_target_pairs={{0,16},{8,24},{2,18},{10,26},{4,20},{12,28},{6,22},{14,30},{16,1},... | collective-permute-start | bytes 786440 | tf_op jit(solution)/shard_map/while/body/eval_jaxpr/ppermute | solution.py:87
  52.0 8.6 %collective-permute-start.3 = (f32[2,128,256]{2,1,0:T(8,128)S(1)}, f32[2,128,256]{2,1,0:T(8,128)S(1)}, u32[]{:S(2)}, u32[]{:S(2)}) collective-permute-start(f32[2,128,256]{2,1,0:T(8,128)S(1)} %get-tuple-element.267), channel_id=1, source_target_pairs={{0,241},{8,249},{2,243},{10,251},{4,245},{12,253},{6,247},{14,255}... | collective-permute-start | bytes 786440 | tf_op jit(solution)/shard_map/while/body/eval_jaxpr/ppermute | solution.py:87
  65.1 6.9 %collective-permute-start.5 = (f32[2,384,128]{2,1,0:T(8,128)S(1)}, f32[2,384,128]{2,1,0:T(8,128)S(1)}, u32[]{:S(2)}, u32[]{:S(2)}) collective-permute-start(f32[2,384,128]{2,1,0:T(8,128)S(1)} %get-tuple-element.270.gl), channel_id=1, source_target_pairs={{0,14},{8,0},{2,8},{10,2},{4,10},{12,4},{6,12},{14,6},{16,30},{24,... | collective-permute-start | bytes 1179656 | tf_op jit(solution)/shard_map/while/body/eval_jaxpr/ppermute | solution.py:87
  66.8 8.4 %collective-permute-start.4 = (f32[2,384,128]{2,1,0:T(8,128)S(1)}, f32[2,384,128]{2,1,0:T(8,128)S(1)}, u32[]{:S(2)}, u32[]{:S(2)}) collective-permute-start(f32[2,384,128]{2,1,0:T(8,128)S(1)} %get-tuple-element.271.gr), channel_id=1, source_target_pairs={{0,8},{8,2},{2,10},{10,4},{4,12},{12,6},{6,14},{14,0},{16,24},{24,... | collective-permute-start | bytes 1179656 | tf_op jit(solution)/shard_map/while/body/eval_jaxpr/ppermute | solution.py:87
  66.8 22.0 %collective-permute-start.8 = (f32[16,24,256]{2,1,0:T(8,128)S(1)}, f32[16,24,256]{2,1,0:T(8,128)S(1)}, u32[]{:S(2)}, u32[]{:S(2)}) collective-permute-start(f32[16,24,256]{2,1,0:T(8,128)S(1)} %get-tuple-element.276), channel_id=1, source_target_pairs={{0,8},{1,9},{2,10},{3,11},{4,12},{5,13},{6,14},{7,15},{8,0},{9,1},... | collective-permute-start | bytes 1179656 | tf_op jit(solution)/shard_map/while/body/eval_jaxpr/ppermute | solution.py:87
  75.8 10.0 %collective-permute-start.6 = (f32[2,128,256]{2,1,0:T(8,128)S(1)}, f32[2,128,256]{2,1,0:T(8,128)S(1)}, u32[]{:S(2)}, u32[]{:S(2)}) collective-permute-start(f32[2,128,256]{2,1,0:T(8,128)S(1)} %get-tuple-element.272), channel_id=1, source_target_pairs={{0,16},{8,24},{2,18},{10,26},{4,20},{12,28},{6,22},{14,30},{16,1},... | collective-permute-start | bytes 786440 | tf_op jit(solution)/shard_map/while/body/eval_jaxpr/ppermute | solution.py:87
  75.9 9.9 %collective-permute-start.7 = (f32[2,128,256]{2,1,0:T(8,128)S(1)}, f32[2,128,256]{2,1,0:T(8,128)S(1)}, u32[]{:S(2)}, u32[]{:S(2)}) collective-permute-start(f32[2,128,256]{2,1,0:T(8,128)S(1)} %get-tuple-element.273), channel_id=1, source_target_pairs={{0,241},{8,249},{2,243},{10,251},{4,245},{12,253},{6,247},{14,255}... | collective-permute-start | bytes 786440 | tf_op jit(solution)/shard_map/while/body/eval_jaxpr/ppermute | solution.py:87
  86.8 54.1 %collective-permute-start.25 = (f32[2,256,128]{2,1,0:T(8,128)S(1)}, f32[2,256,128]{2,1,0:T(8,128)S(1)}, u32[]{:S(2)}, u32[]{:S(2)}) collective-permute-start(f32[2,256,128]{2,1,0:T(8,128)S(1)} %get-tuple-element.285), channel_id=1, source_target_pairs={{0,0},{8,1},{2,2},{10,3},{4,4},{12,5},{6,6},{14,7},{16,8},{24,9},{... | collective-permute-start | bytes 786440 | tf_op jit(solution)/shard_map/while/body/eval_jaxpr/ppermute | solution.py:87
  88.8 7.7 %collective-permute-start.9 = (f32[4,24,256]{2,1,0:T(8,128)S(1)}, f32[4,24,256]{2,1,0:T(8,128)S(1)}, u32[]{:S(2)}, u32[]{:S(2)}) collective-permute-start(f32[4,24,256]{2,1,0:T(8,128)S(1)} %get-tuple-element.278), channel_id=1, source_target_pairs={{0,16},{1,17},{2,18},{3,19},{4,20},{5,21},{6,22},{7,23},{8,24},{9,... | collective-permute-start | bytes 294920 | tf_op jit(solution)/shard_map/while/body/eval_jaxpr/ppermute | solution.py:87
  93.0 6.2 %collective-permute-start.10 = (f32[4,24,256]{2,1,0:T(8,128)S(1)}, f32[4,24,256]{2,1,0:T(8,128)S(1)}, u32[]{:S(2)}, u32[]{:S(2)}) collective-permute-start(f32[4,24,256]{2,1,0:T(8,128)S(1)} %get-tuple-element.279), channel_id=1, source_target_pairs={{0,1},{1,0},{2,3},{3,2},{4,5},{5,4},{6,7},{7,6},{8,9},{9,8},{10,11... | collective-permute-start | bytes 294920 | tf_op jit(solution)/shard_map/while/body/eval_jaxpr/ppermute | solution.py:87
  93.0 7.6 %collective-permute-start.11 = (f32[4,24,256]{2,1,0:T(8,128)S(1)}, f32[4,24,256]{2,1,0:T(8,128)S(1)}, u32[]{:S(2)}, u32[]{:S(2)}) collective-permute-start(f32[4,24,256]{2,1,0:T(8,128)S(1)} %get-tuple-element.280), channel_id=1, source_target_pairs={{0,17},{1,16},{2,19},{3,18},{4,21},{5,20},{6,23},{7,22},{8,25},{9,... | collective-permute-start | bytes 294920 | tf_op jit(solution)/shard_map/while/body/eval_jaxpr/ppermute | solution.py:87
  113.9 8.5 %collective-permute-start.18 = (f32[1,24,256]{2,1,0:T(8,128)S(1)}, f32[1,24,256]{2,1,0:T(8,128)S(1)}, u32[]{:S(2)}, u32[]{:S(2)}) collective-permute-start(f32[1,24,256]{2,1,0:T(8,128)S(1)} %eval_jaxpr.20.a), channel_id=1, source_target_pairs={{0,192},{1,193},{2,194},{3,195},{4,196},{5,197},{6,198},{7,199},{8... | collective-permute-start | bytes 73736 | tf_op jit(solution)/shard_map/while/body/eval_jaxpr/ppermute | solution.py:87
  119.4 6.9 %collective-permute-start.16 = (f32[1,24,256]{2,1,0:T(8,128)S(1)}, f32[1,24,256]{2,1,0:T(8,128)S(1)}, u32[]{:S(2)}, u32[]{:S(2)}) collective-permute-start(f32[1,24,256]{2,1,0:T(8,128)S(1)} %eval_jaxpr.20.a), channel_id=1, source_target_pairs={{0,160},{1,161},{2,162},{3,163},{4,164},{5,165},{6,166},{7,167},{8... | collective-permute-start | bytes 73736 | tf_op jit(solution)/shard_map/while/body/eval_jaxpr/ppermute | solution.py:87
  146.4 7.0 %collective-permute-start.1 = (f32[2,384,128]{2,1,0:T(8,128)S(1)}, f32[2,384,128]{2,1,0:T(8,128)S(1)}, u32[]{:S(2)}, u32[]{:S(2)}) collective-permute-start(f32[2,384,128]{2,1,0:T(8,128)S(1)} %get-tuple-element.264.gl.refs_3_), channel_id=1, source_target_pairs={{0,14},{8,0},{2,8},{10,2},{4,10},{12,4},{6,12},{14,6},{16,30},{24,... | collective-permute-start | bytes 1179656 | tf_op jit(solution)/shard_map/while/body/eval_jaxpr/ppermute | solution.py:87
  148.1 8.4 %collective-permute-start = (f32[2,384,128]{2,1,0:T(8,128)S(1)}, f32[2,384,128]{2,1,0:T(8,128)S(1)}, u32[]{:S(2)}, u32[]{:S(2)}) collective-permute-start(f32[2,384,128]{2,1,0:T(8,128)S(1)} %get-tuple-element.265.gr.refs_4_), channel_id=1, source_target_pairs={{0,8},{8,2},{2,10},{10,4},{4,12},{12,6},{6,14},{14,0},{16,24},{24,... | collective-permute-start | bytes 1179656 | tf_op jit(solution)/shard_map/while/body/eval_jaxpr/ppermute | solution.py:87
  157.1 6.4 %collective-permute-start.2 = (f32[2,128,256]{2,1,0:T(8,128)S(1)}, f32[2,128,256]{2,1,0:T(8,128)S(1)}, u32[]{:S(2)}, u32[]{:S(2)}) collective-permute-start(f32[2,128,256]{2,1,0:T(8,128)S(1)} %get-tuple-element.266), channel_id=1, source_target_pairs={{0,16},{8,24},{2,18},{10,26},{4,20},{12,28},{6,22},{14,30},{16,1},... | collective-permute-start | bytes 786440 | tf_op jit(solution)/shard_map/while/body/eval_jaxpr/ppermute | solution.py:87
  157.9 6.4 %collective-permute-start.3 = (f32[2,128,256]{2,1,0:T(8,128)S(1)}, f32[2,128,256]{2,1,0:T(8,128)S(1)}, u32[]{:S(2)}, u32[]{:S(2)}) collective-permute-start(f32[2,128,256]{2,1,0:T(8,128)S(1)} %get-tuple-element.267), channel_id=1, source_target_pairs={{0,241},{8,249},{2,243},{10,251},{4,245},{12,253},{6,247},{14,255}... | collective-permute-start | bytes 786440 | tf_op jit(solution)/shard_map/while/body/eval_jaxpr/ppermute | solution.py:87
  168.9 6.9 %collective-permute-start.5 = (f32[2,384,128]{2,1,0:T(8,128)S(1)}, f32[2,384,128]{2,1,0:T(8,128)S(1)}, u32[]{:S(2)}, u32[]{:S(2)}) collective-permute-start(f32[2,384,128]{2,1,0:T(8,128)S(1)} %get-tuple-element.270.gl), channel_id=1, source_target_pairs={{0,14},{8,0},{2,8},{10,2},{4,10},{12,4},{6,12},{14,6},{16,30},{24,... | collective-permute-start | bytes 1179656 | tf_op jit(solution)/shard_map/while/body/eval_jaxpr/ppermute | solution.py:87
  170.5 8.4 %collective-permute-start.4 = (f32[2,384,128]{2,1,0:T(8,128)S(1)}, f32[2,384,128]{2,1,0:T(8,128)S(1)}, u32[]{:S(2)}, u32[]{:S(2)}) collective-permute-start(f32[2,384,128]{2,1,0:T(8,128)S(1)} %get-tuple-element.271.gr), channel_id=1, source_target_pairs={{0,8},{8,2},{2,10},{10,4},{4,12},{12,6},{6,14},{14,0},{16,24},{24,... | collective-permute-start | bytes 1179656 | tf_op jit(solution)/shard_map/while/body/eval_jaxpr/ppermute | solution.py:87
  170.5 22.7 %collective-permute-start.8 = (f32[16,24,256]{2,1,0:T(8,128)S(1)}, f32[16,24,256]{2,1,0:T(8,128)S(1)}, u32[]{:S(2)}, u32[]{:S(2)}) collective-permute-start(f32[16,24,256]{2,1,0:T(8,128)S(1)} %get-tuple-element.276), channel_id=1, source_target_pairs={{0,8},{1,9},{2,10},{3,11},{4,12},{5,13},{6,14},{7,15},{8,0},{9,1},... | collective-permute-start | bytes 1179656 | tf_op jit(solution)/shard_map/while/body/eval_jaxpr/ppermute | solution.py:87
  179.6 8.5 %collective-permute-start.6 = (f32[2,128,256]{2,1,0:T(8,128)S(1)}, f32[2,128,256]{2,1,0:T(8,128)S(1)}, u32[]{:S(2)}, u32[]{:S(2)}) collective-permute-start(f32[2,128,256]{2,1,0:T(8,128)S(1)} %get-tuple-element.272), channel_id=1, source_target_pairs={{0,16},{8,24},{2,18},{10,26},{4,20},{12,28},{6,22},{14,30},{16,1},... | collective-permute-start | bytes 786440 | tf_op jit(solution)/shard_map/while/body/eval_jaxpr/ppermute | solution.py:87
  182.4 7.9 %collective-permute-start.7 = (f32[2,128,256]{2,1,0:T(8,128)S(1)}, f32[2,128,256]{2,1,0:T(8,128)S(1)}, u32[]{:S(2)}, u32[]{:S(2)}) collective-permute-start(f32[2,128,256]{2,1,0:T(8,128)S(1)} %get-tuple-element.273), channel_id=1, source_target_pairs={{0,241},{8,249},{2,243},{10,251},{4,245},{12,253},{6,247},{14,255}... | collective-permute-start | bytes 786440 | tf_op jit(solution)/shard_map/while/body/eval_jaxpr/ppermute | solution.py:87
  191.3 53.1 %collective-permute-start.25 = (f32[2,256,128]{2,1,0:T(8,128)S(1)}, f32[2,256,128]{2,1,0:T(8,128)S(1)}, u32[]{:S(2)}, u32[]{:S(2)}) collective-permute-start(f32[2,256,128]{2,1,0:T(8,128)S(1)} %get-tuple-element.285), channel_id=1, source_target_pairs={{0,0},{8,1},{2,2},{10,3},{4,4},{12,5},{6,6},{14,7},{16,8},{24,9},{... | collective-permute-start | bytes 786440 | tf_op jit(solution)/shard_map/while/body/eval_jaxpr/ppermute | solution.py:87
  195.5 10.5 %collective-permute-start.10 = (f32[4,24,256]{2,1,0:T(8,128)S(1)}, f32[4,24,256]{2,1,0:T(8,128)S(1)}, u32[]{:S(2)}, u32[]{:S(2)}) collective-permute-start(f32[4,24,256]{2,1,0:T(8,128)S(1)} %get-tuple-element.279), channel_id=1, source_target_pairs={{0,1},{1,0},{2,3},{3,2},{4,5},{5,4},{6,7},{7,6},{8,9},{9,8},{10,11... | collective-permute-start | bytes 294920 | tf_op jit(solution)/shard_map/while/body/eval_jaxpr/ppermute | solution.py:87
  197.6 8.8 %collective-permute-start.11 = (f32[4,24,256]{2,1,0:T(8,128)S(1)}, f32[4,24,256]{2,1,0:T(8,128)S(1)}, u32[]{:S(2)}, u32[]{:S(2)}) collective-permute-start(f32[4,24,256]{2,1,0:T(8,128)S(1)} %get-tuple-element.280), channel_id=1, source_target_pairs={{0,17},{1,16},{2,19},{3,18},{4,21},{5,20},{6,23},{7,22},{8,25},{9,... | collective-permute-start | bytes 294920 | tf_op jit(solution)/shard_map/while/body/eval_jaxpr/ppermute | solution.py:87
  219.3 6.5 %collective-permute-start.18 = (f32[1,24,256]{2,1,0:T(8,128)S(1)}, f32[1,24,256]{2,1,0:T(8,128)S(1)}, u32[]{:S(2)}, u32[]{:S(2)}) collective-permute-start(f32[1,24,256]{2,1,0:T(8,128)S(1)} %eval_jaxpr.20.a), channel_id=1, source_target_pairs={{0,192},{1,193},{2,194},{3,195},{4,196},{5,197},{6,198},{7,199},{8... | collective-permute-start | bytes 73736 | tf_op jit(solution)/shard_map/while/body/eval_jaxpr/ppermute | solution.py:87
  223.4 6.8 %collective-permute-start.16 = (f32[1,24,256]{2,1,0:T(8,128)S(1)}, f32[1,24,256]{2,1,0:T(8,128)S(1)}, u32[]{:S(2)}, u32[]{:S(2)}) collective-permute-start(f32[1,24,256]{2,1,0:T(8,128)S(1)} %eval_jaxpr.20.a), channel_id=1, source_target_pairs={{0,160},{1,161},{2,162},{3,163},{4,164},{5,165},{6,166},{7,167},{8... | collective-permute-start | bytes 73736 | tf_op jit(solution)/shard_map/while/body/eval_jaxpr/ppermute | solution.py:87
  (33 other events, 183.5 us)
